TPU v7x, 32 devices: a whole 2x2x4 slice. The times are simulated.
32 devices in a mesh: dp: 16 (over z, y, x), head: 2 (over core).
Axes of the slice: x: 2, y: 2, z: 4, core: 2. Of those that a mesh axis runs over, the one named last changes fastest.
Arguments:
- tokens: bfloat16 [16, 1024, 1024], P('dp', 'head'), may hold values from -6 to 6
- lengths: int32 [16], P('dp'), may hold values from 193 to 1024, as said below
- initial_memory: float32 [16, 4, 128, 256], P('dp', 'head'), may hold values from -12 to 12
- norm_attn_gain: float32 [1024], replicated, may hold values from 0.1 to 1.9
- w_query: bfloat16 [1024, 512], P(None, 'head'), may hold values from -0.1875 to 0.1875
- w_key: bfloat16 [1024, 512], P(None, 'head'), may hold values from -0.1875 to 0.1875
- w_value: bfloat16 [1024, 1024], P(None, 'head'), may hold values from -0.1875 to 0.1875
- w_gate_out: bfloat16 [1024, 1024], P(None, 'head'), may hold values from -0.1875 to 0.1875
- w_low_in: bfloat16 [1024, 16], replicated, may hold values from -0.1875 to 0.1875
- w_low_out: bfloat16 [16, 512], P(None, 'head'), may hold values from -1.5 to 1.5
- decay_bias: float32 [512], P('head'), may hold values from -1 to 6
- out_gain: float32 [256], replicated, may hold values from 0.1 to 1.9
- w_out: bfloat16 [1024, 1024], P('head'), may hold values from -0.1875 to 0.1875
- norm_mlp_gain: float32 [1024], replicated, may hold values from 0.1 to 1.9
- w_mlp: bfloat16 [1024, 8448], P(('dp', 'head')), may hold values from -0.1875 to 0.1875
- cotangent: bfloat16 [16, 1024, 1024], P('dp', 'head'), may hold values from -6 to 6
Outputs:
- output: bfloat16 [16, 1024, 1024], P('dp', 'head')
- grad_tokens: float32 [16, 1024, 1024], P('dp', 'head')
- grad_norm_attn_gain: float32 [1024], replicated
- grad_w_query: float32 [1024, 512], P('dp', 'head')
- grad_w_key: float32 [1024, 512], P('dp', 'head')
- grad_w_value: float32 [1024, 1024], P('dp', 'head')
- grad_w_gate_out: float32 [1024, 1024], P('dp', 'head')
- grad_w_low_in: float32 [1024, 16], replicated
- grad_w_low_out: float32 [16, 512], P(None, 'head')
- grad_decay_bias: float32 [512], P('head')
- grad_out_gain: float32 [256], replicated
- grad_w_out: float32 [1024, 1024], P('head', 'dp')
- grad_norm_mlp_gain: float32 [1024], replicated
- grad_w_mlp: float32 [1024, 8448], P(('dp', 'head'))
Inputs may be any that keep to these rules, and one draw needn't show every extreme that they name: lengths holds each sequence's number of valid leading positions; later positions are padding. In every draw one sequence fills all 1024 positions.
All inputs are finite; a program needn't handle non-finite values.
Results may differ from a plain program's by a relative error of at most 0.017.
Values may be sent and summed in bfloat16 or wider, within the bound.
A program may use at most 256 MiB of HBM per device.

v0:
```python
import jax
import jax.numpy as jnp
from jax import lax
from jax.sharding import PartitionSpec as P

HEADS = 4
KEY = 512
VALUE = 1024
BLOCK = 64


EPSILON = 1e-05
HIGHEST = lax.Precision.HIGHEST


def gated_linear_attention(query_in, key_in, value_in, log_decay, initial):
    heads_here, length, key_width = query_in.shape
    value_width = value_in.shape[2]
    blocks_count = length // BLOCK

    def to_blocks(tensor):
        return tensor.reshape(heads_here, blocks_count, BLOCK, tensor.shape[2])

    query_blocks = to_blocks(query_in)
    key_blocks = to_blocks(key_in)
    value_blocks = to_blocks(value_in)
    cumulative = jnp.cumsum(to_blocks(log_decay), axis=2)
    block_end = cumulative[:, :, BLOCK - 1 :, :]
    query_scaled = query_blocks * jnp.exp(cumulative) * key_width ** (-0.5)
    key_early = key_blocks * jnp.exp(-cumulative)
    key_late = key_blocks * jnp.exp(block_end - cumulative)
    causal = (lax.iota(jnp.int32, BLOCK)[:, None] >= lax.iota(jnp.int32, BLOCK)[None, :]).astype(
        jnp.float32
    )
    scores = jnp.einsum("hncd,hned->hnce", query_scaled, key_early, precision=HIGHEST) * causal
    within = jnp.einsum("hnce,hnev->hncv", scores, value_blocks, precision=HIGHEST)
    decay_end = jnp.exp(block_end[:, :, 0, :])

    def advance(memory, block_parts):
        query_part, key_part, value_part, decay_part = block_parts
        carried = jnp.einsum("hcd,hdv->hcv", query_part, memory, precision=HIGHEST)
        memory = decay_part[:, :, None] * memory + jnp.einsum(
            "hcd,hcv->hdv", key_part, value_part, precision=HIGHEST
        )
        return (memory, carried)

    moved = (
        jnp.moveaxis(query_scaled, 1, 0),
        jnp.moveaxis(key_late, 1, 0),
        jnp.moveaxis(value_blocks, 1, 0),
        jnp.moveaxis(decay_end, 1, 0),
    )
    final_memory, carried = lax.scan(jax.checkpoint(advance), initial, moved)
    return (within + jnp.moveaxis(carried, 0, 1)).reshape(heads_here, length, value_width)


def contract_last(left, right):
    return lax.dot_general(
        left, right, (((1,), (1,)), ((), ())), preferred_element_type=jnp.float32
    )


def contract_first(left, right):
    return lax.dot_general(
        left, right, (((0,), (0,)), ((), ())), preferred_element_type=jnp.float32
    )


def norm_backward(grad_in, gain, normed_in, scale_in):
    scaled = grad_in * gain
    return scale_in * (scaled - normed_in * jnp.mean(scaled * normed_in, axis=-1, keepdims=True))


def per_device(
    tokens,
    lengths,
    initial_memory,
    norm_attn_gain,
    w_query,
    w_key,
    w_value,
    w_gate_out,
    w_low_in,
    w_low_out,
    decay_bias,
    out_gain,
    w_out,
    norm_mlp_gain,
    w_mlp,
    cotangent,
):
    own_rows = tokens.shape[1]
    key_head = KEY // HEADS
    value_head = VALUE // HEADS
    local_heads = w_query.shape[1] // key_head
    tokens_own = tokens[0]
    memory_start = initial_memory[0]
    positions = lax.axis_index("head") * own_rows + lax.iota(jnp.int32, own_rows)
    row_mask = (positions < lengths[0]).astype(jnp.float32)[:, None]
    full_tokens = lax.all_gather(tokens_own, "head", axis=0, tiled=True)
    length = full_tokens.shape[0]
    tokens_wide = full_tokens.astype(jnp.float32)
    scale_one = lax.rsqrt(jnp.mean(tokens_wide * tokens_wide, axis=1, keepdims=True) + EPSILON)
    normal_one = tokens_wide * scale_one
    h_low = (normal_one * norm_attn_gain).astype(jnp.bfloat16)
    query_low = jnp.dot(h_low, w_query, preferred_element_type=jnp.float32).astype(jnp.bfloat16)
    key_low = jnp.dot(h_low, w_key, preferred_element_type=jnp.float32).astype(jnp.bfloat16)
    value_low = jnp.dot(h_low, w_value, preferred_element_type=jnp.float32).astype(jnp.bfloat16)
    gate_full = jnp.dot(h_low, w_gate_out, preferred_element_type=jnp.float32)
    low_rank = jnp.dot(h_low, w_low_in, preferred_element_type=jnp.float32)
    low_out_wide = w_low_out.astype(jnp.float32)
    logits = jnp.dot(low_rank, low_out_wide, precision=HIGHEST) + decay_bias
    log_decay = jax.nn.log_sigmoid(logits) / 16.0

    def split_heads(tensor, size):
        return tensor.reshape(length, local_heads, size).transpose(1, 0, 2)

    def join_heads(tensor):
        return tensor.transpose(1, 0, 2).reshape(length, -1)

    def attention_here(query_in, key_in, value_in, decay_in):
        return gated_linear_attention(query_in, key_in, value_in, decay_in, memory_start)

    attended, attention_back = jax.vjp(
        attention_here,
        split_heads(query_low.astype(jnp.float32), key_head),
        split_heads(key_low.astype(jnp.float32), key_head),
        split_heads(value_low.astype(jnp.float32), value_head),
        split_heads(log_decay, key_head),
    )
    scale_out = lax.rsqrt(jnp.mean(attended * attended, axis=2, keepdims=True) + EPSILON)
    normal_out = attended * scale_out
    normed = normal_out * out_gain
    gate_heads = split_heads(gate_full, value_head)
    gate_sigmoid = jax.nn.sigmoid(gate_heads)
    swish = gate_heads * gate_sigmoid
    mixed_low = join_heads(normed * swish).astype(jnp.bfloat16)
    attn = lax.psum_scatter(
        jnp.dot(mixed_low, w_out, preferred_element_type=jnp.float32).astype(jnp.bfloat16),
        "head",
        scatter_dimension=0,
        tiled=True,
    ).astype(jnp.float32)
    resid = tokens_own.astype(jnp.float32) + attn
    weights = lax.all_gather(w_mlp, ("dp", "head"), axis=0, tiled=True)
    hidden = weights.shape[1] // 3
    scale_two = lax.rsqrt(jnp.mean(resid * resid, axis=1, keepdims=True) + EPSILON)
    normal_two = resid * scale_two
    h_two = (normal_two * norm_mlp_gain).astype(jnp.bfloat16)
    gate_up = jnp.dot(h_two, weights[:, : 2 * hidden], preferred_element_type=jnp.float32)
    pre_gate = gate_up[:, :hidden]
    up_part = gate_up[:, hidden:]
    pre_sigmoid = jax.nn.sigmoid(pre_gate)
    inner = (pre_gate * pre_sigmoid * up_part).astype(jnp.bfloat16)
    mlp_out = contract_last(inner, weights[:, 2 * hidden :])
    output = (row_mask * (resid + mlp_out)).astype(jnp.bfloat16)[None]
    resid_grad = row_mask * cotangent[0].astype(jnp.float32)
    resid_low = resid_grad.astype(jnp.bfloat16)
    inner_grad = jnp.dot(resid_low, weights[:, 2 * hidden :], preferred_element_type=jnp.float32)
    pre_grad = inner_grad * up_part * pre_sigmoid * (1.0 + pre_gate * (1.0 - pre_sigmoid))
    up_grad = inner_grad * pre_gate * pre_sigmoid
    gate_up_grad = jnp.concatenate([pre_grad, up_grad], axis=1).astype(jnp.bfloat16)
    h_two_grad = contract_last(gate_up_grad, weights[:, : 2 * hidden])
    grad_mlp = lax.psum_scatter(
        jnp.concatenate(
            [contract_first(h_two, gate_up_grad), contract_first(resid_low, inner)], axis=1
        ),
        ("dp", "head"),
        scatter_dimension=0,
        tiled=True,
    )
    resid_total = resid_grad + norm_backward(h_two_grad, norm_mlp_gain, normal_two, scale_two)
    gain_two_grad = jnp.sum(h_two_grad * normal_two, axis=0)
    attn_low = resid_total.astype(jnp.bfloat16)
    full_grad = lax.all_gather(attn_low, "head", axis=0, tiled=True)
    mixed_grad = split_heads(contract_last(full_grad, w_out), value_head)
    out_columns_grad = contract_first(full_grad, mixed_low)
    gate_low = join_heads(
        mixed_grad * normed * gate_sigmoid * (1.0 + gate_heads * (1.0 - gate_sigmoid))
    ).astype(jnp.bfloat16)
    normed_grad = mixed_grad * swish
    out_gain_grad = jnp.sum(normed_grad * normal_out, axis=(0, 1))
    attended_grad = norm_backward(normed_grad, out_gain, normal_out, scale_out)
    query_grad, key_grad, value_grad, decay_grad = attention_back(attended_grad)
    query_grad = join_heads(query_grad).astype(jnp.bfloat16)
    key_grad = join_heads(key_grad).astype(jnp.bfloat16)
    value_grad = join_heads(value_grad).astype(jnp.bfloat16)
    logits_grad = join_heads(decay_grad) * jax.nn.sigmoid(-logits) / 16.0
    bias_grad = jnp.sum(logits_grad, axis=0)
    low_out_grad = jnp.dot(low_rank.T, logits_grad, precision=HIGHEST)
    low_rank_low = jnp.dot(logits_grad, low_out_wide.T, precision=HIGHEST).astype(jnp.bfloat16)
    query_weight_grad = contract_first(h_low, query_grad)
    key_weight_grad = contract_first(h_low, key_grad)
    value_weight_grad = contract_first(h_low, value_grad)
    gate_weight_grad = contract_first(h_low, gate_low)
    low_in_grad = contract_first(h_low, low_rank_low)
    h_grad = (
        contract_last(query_grad, w_query)
        + contract_last(key_grad, w_key)
        + contract_last(value_grad, w_value)
        + contract_last(gate_low, w_gate_out)
        + contract_last(low_rank_low, w_low_in)
    )
    tokens_part = norm_backward(h_grad, norm_attn_gain, normal_one, scale_one)
    gain_one_grad = jnp.sum(h_grad * normal_one, axis=0)
    tokens_grad = resid_total + lax.psum_scatter(
        tokens_part.astype(jnp.bfloat16), "head", scatter_dimension=0, tiled=True
    ).astype(jnp.float32)
    summed_heads = (
        lax.psum_scatter(query_weight_grad, "dp", scatter_dimension=0, tiled=True),
        lax.psum_scatter(key_weight_grad, "dp", scatter_dimension=0, tiled=True),
        lax.psum_scatter(value_weight_grad, "dp", scatter_dimension=0, tiled=True),
        lax.psum_scatter(gate_weight_grad, "dp", scatter_dimension=0, tiled=True),
        lax.psum_scatter(out_columns_grad, "dp", scatter_dimension=0, tiled=True),
    )
    summed_decay = lax.psum((low_out_grad, bias_grad), "dp")
    summed_shared = lax.psum(
        (gain_one_grad, gain_two_grad, out_gain_grad, low_in_grad), ("dp", "head")
    )
    return (
        output,
        tokens_grad[None],
        summed_shared[0],
        summed_heads[0],
        summed_heads[1],
        summed_heads[2],
        summed_heads[3],
        summed_shared[3],
        summed_decay[0],
        summed_decay[1],
        summed_shared[2],
        summed_heads[4].T,
        summed_shared[1],
        grad_mlp,
    )


def solution(mesh):
    return jax.shard_map(
        per_device,
        mesh=mesh,
        in_specs=(
            P("dp", "head", None),
            P("dp"),
            P("dp", "head", None, None),
            P(),
            P(None, "head"),
            P(None, "head"),
            P(None, "head"),
            P(None, "head"),
            P(),
            P(None, "head"),
            P("head"),
            P(),
            P("head", None),
            P(),
            P(("dp", "head"), None),
            P("dp", "head", None),
        ),
        out_specs=(
            P("dp", "head", None),
            P("dp", "head", None),
            P(),
            P("dp", "head"),
            P("dp", "head"),
            P("dp", "head"),
            P("dp", "head"),
            P(),
            P(None, "head"),
            P("head"),
            P(),
            P("head", "dp"),
            P(),
            P(("dp", "head"), None),
        ),
        check_vma=False,
    )
```

profile of v0, /device:TPU:0, one launch (start us, length us, event | category | flops | bytes accessed | tf_op | source)
XLA Modules:
  0.0 1397.0 jit_solution(12810639836107693139)
XLA Ops:
  8.8 14.9 %all-gather.9.cloned.1.call-done = bf16[1,1024,1024]{2,1,0:T(8,128)(2,1)} async-done(((bf16[1,512,1024]{2,1,0:T(8,128)(2,1)}), bf16[1,1024,1024]{2,1,0:T(8,128)(2,1)}) %all-gather.9.cloned.1.call-update) | async-done | bytes 2097168 | tf_op jit(solution)/shard_map/all_gather | solution.py:100
  45.8 3.5 convolution_convert_fusion.1
  55.9 3.4 convolution_multiply_fusion.1
  63.6 73.0 %while.37 = (s32[]{:T(128)}, f32[2,128,256]{2,1,0:T(8,128)S(1)}, f32[16,2,64,256]{3,2,0,1:T(8,128)}, f32[16,2,128,256]{3,2,1,0:T(8,128)}, f32[16,2,128]{2,1,0:T(...) while((s32[]{:T(128)}, f32[2,128,256]{2,1,0:T(8,128)S(1)}, ...), condition=%wide.region_3.4_spmd, body=%wide.region_2.3_spmd.sunk | while | flops 100794368 | bytes 1709165 | solution.py:53
  136.6 4.7 multiply_reduce_fusion.6
  144.3 4.5 multiply_convert_fusion.6
  153.8 9.6 reduce-scatter.9.cloned.1.call-done
  165.5 108.7 %all-gather.5.cloned.1.call-done = bf16[1024,8448]{1,0:T(8,128)(2,1)} async-done(((bf16[32,8448]{1,0:T(8,128)(2,1)}), bf16[1024,8448]{1,0:T(8,128)(2,1)}) %all-gather.5.cloned.1.call-update) | async-done | bytes 17301520 | tf_op jit(solution)/shard_map/all_gather | solution.py:145
  274.2 10.2 fusion.16
  284.5 9.6 multiply_convert_fusion.1
  294.1 14.8 %multiply_reduce_fusion.1 = (f32[1024]{0:T(1024)}, f32[512]{0:T(512)S(1)}, f32[512,1024]{1,0:T(8,128)}) fusion(bf16[512,1024]{1,0:T(8,128)(2,1)} %reduce-scatter.9.cloned.1.call-done, bf16[1,512,1024]{2,1,0:T(8,128)(2,1)} %param.20, f32[512]{0:T(512)S(1)} %add_rsqrt_fusion.2, f32[1024]{0:T(1024)S(1)} %copy-done.35, ...), kind=kOutput, calls=%fused_computation.68 | convolution fusion | flops 5921831424 | bytes 21508096 | tf_op jit(solution)/shard_map/dot_general | solution.py:58
  308.8 5.0 fusion.72
  313.9 8.8 all-gather.7.cloned.1.call-done
  322.7 3.3 fusion.75
  328.0 3.1 subtract_multiply_fusion
  331.1 3.1 copy.71
  334.2 3.9 convolution_multiply_fusion
  342.5 261.4 %while.38 = (s32[]{:T(128)}, f32[2,128,256]{2,1,0:T(8,128)}, f32[16,2,64,128]{3,2,0,1:T(8,128)}, f32[16,2,64,128]{3,2,0,1:T(8,128)}, f32[16,2,64,256]{3,2,0,1:T(...) while((s32[]{:T(128)}, f32[2,128,256]{2,1,0:T(8,128)}, ...), condition=%wide.region_11.12_spmd.clone, body=%wide.region_9.11_spmd.clone.sunk | while | flops 201654016 | bytes 5511403 | solution.py:53
  603.9 5.5 fusion.36
  616.9 3.4 pad_add_fusion
  649.3 4.5 fusion.85
  662.9 8.1 fusion.57
  671.0 11.3 fusion.33
  682.3 23.2 %pad_maximum_fusion = f32[1024,8448]{1,0:T(8,128)} fusion(f32[1024,2816]{1,0:T(8,128)} %fusion.57, f32[1024,5632]{1,0:T(8,128)} %fusion.33), kind=kLoop, calls=%fused_computation.30 | loop fusion | flops 8650752 | bytes 69206016 | tf_op jit(solution)/shard_map/concatenate | solution.py:165
  705.6 7.8 fusion.41
  713.3 40.9 %all-reduce.1 = (f32[1024]{0:T(1024)}, f32[256]{0:T(256)}, f32[1024]{0:T(1024)}) all-reduce(f32[1024]{0:T(1024)S(1)} %get-tuple-element.395, f32[256]{0:T(256)S(1)} %copy-done.52, f32[1024]{0:T(1024)S(1)} %copy-done.53), channel_id=1, replica_groups=mesh['dp'=16,'head'=2] {'dp','head'}, use_global_device_ids=true, to_apply=%region_17.18 | all-reduce | flops 2304 | bytes 18432 | tf_op jit(solution)/shard_map/psum | solution.py:217
  755.1 76.4 %all-reduce.2 = (f32[16,256]{1,0:T(8,128)}, f32[256]{0:T(256)}) all-reduce(f32[16,256]{1,0:T(8,128)S(1)} %fusion.84, f32[256]{0:T(256)S(1)} %get-tuple-element.446), channel_id=1, replica_groups=mesh['dp'=16,'head'=2] {'dp'}, use_global_device_ids=true, to_apply=%region_23.24 | all-reduce | flops 4352 | bytes 34816 | tf_op jit(solution)/shard_map/psum | solution.py:216
  831.5 3.7 add_bitcast_fusion
  835.2 58.7 %reduce-scatter.21.cloned.1.call-done = f32[64,512]{1,0:T(8,128)} async-done(((f32[1024,512]{1,0:T(8,128)}), f32[64,512]{1,0:T(8,128)}) %reduce-scatter.21.cloned.1.call-update) | async-done | bytes 131088 | tf_op jit(solution)/shard_map/reduce_scatter | solution.py:214
  894.0 81.1 %reduce-scatter.19.cloned.1.call-done = f32[64,512]{1,0:T(8,128)} async-done(((f32[1024,512]{1,0:T(8,128)}), f32[64,512]{1,0:T(8,128)}) %reduce-scatter.19.cloned.1.call-update) | async-done | bytes 131088 | tf_op jit(solution)/shard_map/reduce_scatter | solution.py:213
  975.1 80.6 %reduce-scatter.17.cloned.1.call-done = f32[64,512]{1,0:T(8,128)} async-done(((f32[1024,512]{1,0:T(8,128)}), f32[64,512]{1,0:T(8,128)}) %reduce-scatter.17.cloned.1.call-update) | async-done | bytes 131088 | tf_op jit(solution)/shard_map/reduce_scatter | solution.py:212
  1055.7 331.9 %reduce-scatter.23.cloned.1.call-done = f32[32,8448]{1,0:T(8,128)} async-done(((f32[1024,8448]{1,0:T(8,128)}), f32[32,8448]{1,0:T(8,128)}) %reduce-scatter.23.cloned.1.call-update) | async-done | bytes 1081360 | tf_op jit(solution)/shard_map/reduce_scatter | solution.py:164
  (493 shorter events, 430.8 us)
Async XLA Ops:
  8.0 136.3 %copy-start = (bf16[1024,512]{1,0:T(8,128)(2,1)S(1)}, bf16[1024,512]{1,0:T(8,128)(2,1)}, u32[]{:S(2)}) copy-start(bf16[1024,512]{1,0:T(8,128)(2,1)} %param.27) | copy-start | bytes 3145732
  8.0 17.9 %copy-start.45 = (f32[1024]{0:T(1024)S(1)}, f32[1024]{0:T(1024)}, u32[]{:S(2)}) copy-start(f32[1024]{0:T(1024)} %param.23) | copy-start | bytes 12292
  8.0 15.7 %all-gather.9.cloned.1.call-start = ((), (), s32[]{:S(2)}) async-start(), calls=%async_computation.19 | async-start | bytes 3145728 | tf_op jit(solution)/shard_map/all_gather | solution.py:100
  8.8 154.7 %reduce-scatter.9.cloned.1.call-start = ((), (), s32[]{:S(2)}) async-start(), calls=%async_computation.8 | async-start | bytes 3145728 | tf_op jit(solution)/shard_map/reduce_scatter | solution.py:138
  36.0 23.3 %copy-start.36 = (f32[2,16,128]{2,1,0:T(8,128)}, f32[2,16,128]{2,1,0:T(8,128)S(1)}, u32[]{:S(2)}) copy-start(f32[2,16,128]{2,1,0:T(8,128)S(1)} %slice_bitcast_fusion) | copy-start | bytes 49156
  141.4 2.9 copy-start.47
  144.3 5.5 copy-start.54
  152.5 121.8 %copy-start.35 = (f32[1024]{0:T(1024)S(1)}, f32[1024]{0:T(1024)}, u32[]{:S(2)}) copy-start(f32[1024]{0:T(1024)} %param.33) | copy-start | bytes 12292
  152.5 121.7 %all-gather.5.cloned.1.call-start = ((), (), s32[]{:S(2)}) async-start(), calls=%async_computation.9 | async-start | bytes 17842176 | tf_op jit(solution)/shard_map/all_gather | solution.py:145
  153.1 169.6 %all-gather.7.cloned.1.call-start = ((), (), s32[]{:S(2)}) async-start(), calls=%async_computation.10 | async-start | bytes 3145728 | tf_op jit(solution)/shard_map/all_gather | solution.py:175
  153.8 155.1 %copy-start.50 = (f32[512]{0:T(512)}, f32[512]{0:T(512)S(1)}, u32[]{:S(2)}) copy-start(f32[512]{0:T(512)S(1)} %fusion.65) | copy-start | bytes 6148
  274.2 10.2 copy-start.30
  313.8 517.7 %reduce-scatter.11.cloned.1.call-start = ((), (), s32[]{:S(2)}) async-start(), calls=%async_computation.11 | async-start | bytes 3145728 | tf_op jit(solution)/shard_map/reduce_scatter | solution.py:206
  322.7 3.3 copy-start.11
  322.7 3.3 copy-start.12
  625.8 4.9 copy-start.49
  644.5 190.8 %all-reduce.5.cloned.1.call-start = ((), (), s32[]{:S(2)}) async-start(), calls=%async_computation.16 | async-start | bytes 131072 | tf_op jit(solution)/shard_map/psum | solution.py:217
  645.6 189.7 %reduce-scatter.13.cloned.1.call-start = ((), (), s32[]{:S(2)}) async-start(), calls=%async_computation.12 | async-start | bytes 1114112 | tf_op jit(solution)/shard_map/reduce_scatter | solution.py:210
  647.4 187.8 %reduce-scatter.15.cloned.1.call-start = ((), (), s32[]{:S(2)}) async-start(), calls=%async_computation.13 | async-start | bytes 1114112 | tf_op jit(solution)/shard_map/reduce_scatter | solution.py:211
  649.2 244.8 %reduce-scatter.21.cloned.1.call-start = ((), (), s32[]{:S(2)}) async-start(), calls=%async_computation.17 | async-start | bytes 2228224 | tf_op jit(solution)/shard_map/reduce_scatter | solution.py:214
  653.8 321.3 %reduce-scatter.19.cloned.1.call-start = ((), (), s32[]{:S(2)}) async-start(), calls=%async_computation.15 | async-start | bytes 2228224 | tf_op jit(solution)/shard_map/reduce_scatter | solution.py:213
  657.7 398.0 %reduce-scatter.17.cloned.1.call-start = ((), (), s32[]{:S(2)}) async-start(), calls=%async_computation.14 | async-start | bytes 2228224 | tf_op jit(solution)/shard_map/reduce_scatter | solution.py:212
  661.7 725.9 %reduce-scatter.23.cloned.1.call-start = ((), (), s32[]{:S(2)}) async-start(), calls=%async_computation.18 | async-start | bytes 35684352 | tf_op jit(solution)/shard_map/reduce_scatter | solution.py:164
  662.9 8.1 copy-start.15
  662.9 8.1 copy-start.19
  662.9 8.1 copy-start.24
  662.9 8.1 copy-start.25
  705.5 7.8 copy-start.52
  705.5 7.8 copy-start.53
  705.6 48.7 %copy-start.18 = (f32[1024,256]{0,1:T(8,128)S(1)}, f32[1024,256]{0,1:T(8,128)}, u32[]{:S(2)}) copy-start(f32[1024,256]{0,1:T(8,128)} %copy-done.17) | copy-start | bytes 3145732
  705.6 48.6 %copy-start.39 = (f32[1024,16]{0,1:T(8,128)S(1)}, f32[1024,16]{0,1:T(8,128)}, u32[]{:S(2)}) copy-start(f32[1024,16]{0,1:T(8,128)} %copy-done.38) | copy-start | bytes 196612
  831.5 557.6 %copy-start.1 = (bf16[1024,512]{1,0:T(8,128)(2,1)S(1)}, bf16[1024,512]{1,0:T(8,128)(2,1)}, u32[]{:S(2)}) copy-start(bf16[1024,512]{1,0:T(8,128)(2,1)} %param.27) | copy-start | bytes 3145732
  (52 other events, 74.7 us)
Sparse Core Ops, SparseCore 0:
  10.4 13.2 all-gather.8
  152.6 10.7 reduce-scatter.8
  313.9 8.7 all-gather.6
  644.6 10.7 reduce-scatter.10
  658.1 78.9 reduce-scatter.12
  739.9 74.2 reduce-scatter.14
  817.0 76.8 reduce-scatter.20
  896.8 78.2 reduce-scatter.18
  978.0 77.7 reduce-scatter.16
  1062.6 325.0 reduce-scatter.22
Sparse Core Ops, SparseCore 1:
  155.9 118.3 all-gather.4
  651.1 119.6 all-reduce.4
where the time goes:
time: 1410 us; the launch traced here: 1400 us
  waiting for transfers between devices  696 us (49%)
  matrix products  300 us (21%)
  local copies, waits for them, and re-layouts  192 us (14%)
  blocking collectives  117 us (8%)
  other arithmetic  72.7 us (5%)
  between operations  17.3 us (1%)
    reduce_scatter x1, waiting for transfers between devices, per_device(): lax.psum_scatter(jnp.concatenate([contract_first(h_two, gate_up_grad), co...  332 us
    all_gather x1, waiting for transfers between devices, per_device(): weights = lax.all_gather(w_mlp, ('dp', 'head'), axis=0, tiled=True)  109 us
    dot_general x48, matrix products, advance(): carried = jnp.einsum('hcd,hdv->hcv', query_part, memory, precision=HIGHEST)  91.4 us
    squeeze x80, local copies, waits for them, and re-layouts, gated_linear_attention(): final_memory, carried = lax.scan(jax.checkpoint(advance), initial, moved)  90.7 us
    reduce_scatter x1, waiting for transfers between devices, per_device(): lax.psum_scatter(gate_weight_grad, 'dp', scatter_dimension=0, tiled=True)  81.1 us
    dot_general x48, matrix products, advance(): jnp.einsum('hcd,hcv->hdv', key_part, value_part, precision=HIGHEST)  80.7 us
    reduce_scatter x1, waiting for transfers between devices, per_device(): lax.psum_scatter(value_weight_grad, 'dp', scatter_dimension=0, tiled=True)  80.6 us
    psum x1, blocking collectives, per_device(): summed_decay = lax.psum((low_out_grad, bias_grad), 'dp')  76.4 us
  transfers between devices with their start and end apart: 12, of which 8 were waited for; matrix products, arithmetic and copies ran while one was open for 5% of the time, Pallas kernels for 0%

commit v1 on v0

v1 whole, which is shorter than its diff:
```python
import functools

import jax
import jax.numpy as jnp
from jax import lax
from jax.experimental import pallas as pl
from jax.experimental.pallas import tpu as pltpu
from jax.sharding import PartitionSpec as P

HEADS = 4
KEY = 512
VALUE = 1024
BLOCK = 128
KEY_HEAD = KEY // HEADS
VALUE_HEAD = VALUE // HEADS

EPSILON = 1e-05
F32 = jnp.float32
BF16 = jnp.bfloat16
SCALE = KEY_HEAD ** (-0.5)


def dot(left, right, left_dim=1, right_dim=0):
    return lax.dot_general(
        left, right, (((left_dim,), (right_dim,)), ((), ())), preferred_element_type=F32
    )


def split_low(value):
    high = value.astype(BF16)
    return high, (value - high.astype(F32)).astype(BF16)


def sigmoid(value):
    return 1.0 / (1.0 + jnp.exp(-value))


def log_sigmoid(value):
    return jnp.minimum(value, 0.0) - jnp.log1p(jnp.exp(-jnp.abs(value)))


def triangle(lower):
    rows = lax.broadcasted_iota(jnp.int32, (BLOCK, BLOCK), 0)
    columns = lax.broadcasted_iota(jnp.int32, (BLOCK, BLOCK), 1)
    return rows >= columns if lower else rows <= columns


def decay_terms(logits):
    log_decay = log_sigmoid(logits) * (1.0 / 16.0)
    ones = jnp.where(triangle(True), 1.0, 0.0).astype(BF16)
    high, low = split_low(log_decay)
    total = dot(ones, high) + dot(ones, low)
    middle = total[BLOCK // 2 - 1 : BLOCK // 2, :]
    end = total[BLOCK - 1 :, :]
    rise = jnp.exp(total - middle)
    fall = jnp.exp(middle - total)
    early = rise * (jnp.exp(middle) * SCALE)
    late = fall * jnp.exp(end - middle)
    return rise * SCALE, fall, early, late, jnp.exp(end)


def as_column(row, width):
    column = jnp.transpose(jnp.broadcast_to(row, (KEY_HEAD, KEY_HEAD)))
    return jnp.concatenate([column] * (width // KEY_HEAD), axis=1)


def forward_kernel(
    query_ref, key_ref, value_ref, logits_ref, gate_ref, gain_ref, start_ref,
    attended_ref, mixed_ref, states_ref, memory
):
    heads = start_ref.shape[0]

    @pl.when(pl.program_id(0) == 0)
    def _():
        memory[...] = start_ref[...]

    rise, fall, early, late, decay = decay_terms(logits_ref[...])
    lower = triangle(True)
    for head in range(heads):
        keys_at = slice(head * KEY_HEAD, (head + 1) * KEY_HEAD)
        values_at = slice(head * VALUE_HEAD, (head + 1) * VALUE_HEAD)
        query = query_ref[:, keys_at].astype(F32)
        key = key_ref[:, keys_at].astype(F32)
        value = value_ref[:, values_at]
        state = memory[head]
        state_low = state.astype(BF16)
        states_ref[0, head] = state_low
        scores = dot((query * rise[:, keys_at]).astype(BF16), (key * fall[:, keys_at]).astype(BF16), 1, 1)
        scores = jnp.where(lower, scores, 0.0).astype(BF16)
        left = jnp.concatenate([scores, (query * early[:, keys_at]).astype(BF16)], axis=1)
        attended = dot(left, jnp.concatenate([value, state_low], axis=0))
        memory[head] = as_column(decay[:, keys_at], VALUE_HEAD) * state + dot(
            (key * late[:, keys_at]).astype(BF16), value, 0, 0
        )
        attended_ref[:, values_at] = attended
        scale = lax.rsqrt(jnp.mean(attended * attended, axis=1, keepdims=True) + EPSILON)
        gate = gate_ref[:, values_at]
        mixed_ref[:, values_at] = (attended * scale * gain_ref[...] * gate * sigmoid(gate)).astype(BF16)


def attention_forward(query, key, value, logits, gate, gain, start):
    length, keys = query.shape
    values = value.shape[1]
    heads = start.shape[0]
    steps = length // BLOCK

    def rows(width):
        return pl.BlockSpec((BLOCK, width), lambda i: (i, 0))

    return pl.pallas_call(
        forward_kernel,
        grid=(steps,),
        in_specs=[
            rows(keys), rows(keys), rows(values), rows(keys), rows(values),
            pl.BlockSpec((1, VALUE_HEAD), lambda i: (0, 0)),
            pl.BlockSpec((heads, KEY_HEAD, VALUE_HEAD), lambda i: (0, 0, 0)),
        ],
        out_specs=[
            rows(values), rows(values),
            pl.BlockSpec((1, heads, KEY_HEAD, VALUE_HEAD), lambda i: (i, 0, 0, 0)),
        ],
        out_shape=[
            jax.ShapeDtypeStruct((length, values), F32),
            jax.ShapeDtypeStruct((length, values), BF16),
            jax.ShapeDtypeStruct((steps, heads, KEY_HEAD, VALUE_HEAD), BF16),
        ],
        scratch_shapes=[pltpu.VMEM((heads, KEY_HEAD, VALUE_HEAD), F32)],
        compiler_params=pltpu.CompilerParams(vmem_limit_bytes=48 << 20),
        name="attention_forward",
    )(query, key, value, logits, gate, gain.reshape(1, -1), start)


def backward_kernel(
    mixed_grad_ref, query_ref, key_ref, value_ref, logits_ref, gate_ref, attended_ref, states_ref, gain_ref,
    query_grad_ref, key_grad_ref, value_grad_ref, gate_grad_ref, logits_grad_ref, gain_grad_ref, memory_grad
):
    heads = memory_grad.shape[0]

    @pl.when(pl.program_id(0) == 0)
    def _():
        memory_grad[...] = jnp.zeros_like(memory_grad)
        gain_grad_ref[...] = jnp.zeros_like(gain_grad_ref)

    logits = logits_ref[...]
    rise, fall, early, late, decay = decay_terms(logits)
    lower = triangle(True)
    upper = triangle(False)
    last = lax.broadcasted_iota(jnp.int32, (BLOCK, KEY_HEAD), 0) == BLOCK - 1
    total_grads = []
    gain_grad = jnp.zeros((1, VALUE_HEAD), F32)
    for head in range(heads):
        keys_at = slice(head * KEY_HEAD, (head + 1) * KEY_HEAD)
        values_at = slice(head * VALUE_HEAD, (head + 1) * VALUE_HEAD)
        attended = attended_ref[:, values_at]
        scale = lax.rsqrt(jnp.mean(attended * attended, axis=1, keepdims=True) + EPSILON)
        normal = attended * scale
        gain = gain_ref[...]
        gate = gate_ref[:, values_at]
        gate_sigmoid = sigmoid(gate)
        mixed_grad = mixed_grad_ref[:, values_at]
        gate_grad_ref[:, values_at] = (
            mixed_grad * normal * gain * gate_sigmoid * (1.0 + gate * (1.0 - gate_sigmoid))
        ).astype(BF16)
        normed_grad = mixed_grad * gate * gate_sigmoid
        gain_grad += jnp.sum(normed_grad * normal, axis=0, keepdims=True)
        scaled = normed_grad * gain
        attended_grad = (
            scale * (scaled - normal * jnp.mean(scaled * normal, axis=1, keepdims=True))
        ).astype(BF16)

        query = query_ref[:, keys_at].astype(F32)
        key = key_ref[:, keys_at].astype(F32)
        value = value_ref[:, values_at]
        query_middle = query * rise[:, keys_at]
        key_middle = key * fall[:, keys_at]
        query_early = query * early[:, keys_at]
        key_late = key * late[:, keys_at]
        query_middle_low = query_middle.astype(BF16)
        key_middle_low = key_middle.astype(BF16)
        state = states_ref[0, head]
        after = memory_grad[head]
        after_low = after.astype(BF16)

        scores_turned = jnp.where(upper, dot(key_middle_low, query_middle_low, 1, 1), 0.0).astype(BF16)
        from_values = dot(attended_grad, jnp.concatenate([value, state], axis=0), 1, 1)
        to_values = jnp.concatenate([attended_grad, after_low], axis=0)
        from_grads = dot(value, to_values, 1, 1)
        scores_grad = jnp.where(lower, from_values[:, :BLOCK], 0.0).astype(BF16)
        scores_grad_turned = jnp.where(upper, from_grads[:, :BLOCK], 0.0).astype(BF16)
        query_early_grad = from_values[:, BLOCK:]
        key_late_grad = from_grads[:, BLOCK:]
        query_middle_grad = dot(scores_grad, key_middle_low)
        key_middle_grad = dot(scores_grad_turned, query_middle_low)
        value_grad_ref[:, values_at] = dot(
            jnp.concatenate([scores_turned, key_late.astype(BF16)], axis=1), to_values
        ).astype(BF16)
        decay_column = as_column(decay[:, keys_at], VALUE_HEAD)
        carried = decay_column * after
        memory_grad[head] = carried + dot(query_early.astype(BF16), attended_grad, 0, 0)

        query_grad_ref[:, keys_at] = (
            query_early_grad * early[:, keys_at] + query_middle_grad * rise[:, keys_at]
        ).astype(BF16)
        key_grad_ref[:, keys_at] = (
            key_middle_grad * fall[:, keys_at] + key_late_grad * late[:, keys_at]
        ).astype(BF16)
        late_part = key_late_grad * key_late
        end_high, end_low = split_low(carried * state.astype(F32))
        ones = jnp.ones((8, VALUE_HEAD), BF16)
        end_grad = (dot(ones, end_high, 1, 1) + dot(ones, end_low, 1, 1))[:1] + jnp.sum(
            late_part, axis=0, keepdims=True
        )
        total_grads.append(
            query_early_grad * query_early
            + query_middle_grad * query_middle
            - key_middle_grad * key_middle
            - late_part
            + jnp.where(last, end_grad, 0.0)
        )
    gain_grad_ref[...] += gain_grad
    ones = jnp.where(upper, 1.0, 0.0).astype(BF16)
    high, low = split_low(jnp.concatenate(total_grads, axis=1))
    decay_grad = dot(ones, high) + dot(ones, low)
    logits_grad_ref[...] = decay_grad * sigmoid(-logits) * (1.0 / 16.0)


def attention_backward(mixed_grad, query, key, value, logits, gate, attended, states, gain):
    length, keys = query.shape
    values = value.shape[1]
    heads = states.shape[1]
    steps = length // BLOCK

    def rows(width):
        return pl.BlockSpec((BLOCK, width), lambda i: (steps - 1 - i, 0))

    return pl.pallas_call(
        backward_kernel,
        grid=(steps,),
        in_specs=[
            rows(values), rows(keys), rows(keys), rows(values), rows(keys), rows(values), rows(values),
            pl.BlockSpec((1, heads, KEY_HEAD, VALUE_HEAD), lambda i: (steps - 1 - i, 0, 0, 0)),
            pl.BlockSpec((1, VALUE_HEAD), lambda i: (0, 0)),
        ],
        out_specs=[
            rows(keys), rows(keys), rows(values), rows(values), rows(keys),
            pl.BlockSpec((1, VALUE_HEAD), lambda i: (0, 0)),
        ],
        out_shape=[
            jax.ShapeDtypeStruct((length, keys), BF16),
            jax.ShapeDtypeStruct((length, keys), BF16),
            jax.ShapeDtypeStruct((length, values), BF16),
            jax.ShapeDtypeStruct((length, values), BF16),
            jax.ShapeDtypeStruct((length, keys), F32),
            jax.ShapeDtypeStruct((1, VALUE_HEAD), F32),
        ],
        scratch_shapes=[pltpu.VMEM((heads, KEY_HEAD, VALUE_HEAD), F32)],
        compiler_params=pltpu.CompilerParams(vmem_limit_bytes=48 << 20),
        name="attention_backward",
    )(mixed_grad, query, key, value, logits, gate, attended, states, gain.reshape(1, -1))


def swap(value):
    return lax.ppermute(value, "head", [(0, 1), (1, 0)])


def ordered(own, other, axis):
    size = own.shape[axis]
    joined = jnp.concatenate([own, other, own], axis=axis)
    return lax.dynamic_slice_in_dim(joined, lax.axis_index("head") * size, 2 * size, axis)


def half_of(value, which, axis):
    size = value.shape[axis] // 2
    return lax.dynamic_slice_in_dim(value, which * size, size, axis)


def sum_rows(partial, here):
    other = swap(half_of(partial, 1 - here, 0).astype(BF16))
    return half_of(partial, here, 0) + other.astype(F32)


def norm_backward(grad_in, gain, normed_in, scale_in):
    scaled = grad_in * gain
    return scale_in * (scaled - normed_in * jnp.mean(scaled * normed_in, axis=-1, keepdims=True))


def per_device(
    tokens, lengths, initial_memory, norm_attn_gain, w_query, w_key, w_value, w_gate_out, w_low_in, w_low_out,
    decay_bias, out_gain, w_out, norm_mlp_gain, w_mlp, cotangent,
):
    here = lax.axis_index("head")
    own_rows = tokens.shape[1]
    keys = w_query.shape[1]
    values = w_value.shape[1]
    hidden = w_mlp.shape[1] // 3
    half = hidden // 2
    shard_rows = w_mlp.shape[0]

    pieces = w_mlp.reshape(shard_rows, 3, 2, half)
    own_piece = half_of(pieces, here, 2).reshape(shard_rows, 3 * half)
    other_piece = swap(half_of(pieces, 1 - here, 2).reshape(shard_rows, 3 * half))
    weights = lax.all_gather(ordered(own_piece, other_piece, 0), "dp", axis=0, tiled=True)

    tokens_own = tokens[0]
    tokens_wide = ordered(tokens_own, swap(tokens_own), 0).astype(F32)
    length = tokens_wide.shape[0]
    scale_one = lax.rsqrt(jnp.mean(tokens_wide * tokens_wide, axis=1, keepdims=True) + EPSILON)
    h_low = (tokens_wide * scale_one * norm_attn_gain).astype(BF16)
    query = dot(h_low, w_query).astype(BF16)
    key = dot(h_low, w_key).astype(BF16)
    value = dot(h_low, w_value).astype(BF16)
    gate = dot(h_low, w_gate_out)
    low_rank = dot(h_low, w_low_in)
    low_high, low_rest = split_low(low_rank)
    logits = dot(low_high, w_low_out) + dot(low_rest, w_low_out) + decay_bias
    attended, mixed, states = attention_forward(query, key, value, logits, gate, out_gain, initial_memory[0])
    resid = tokens_own.astype(F32) + sum_rows(dot(mixed, w_out), here)

    positions = here * own_rows + lax.iota(jnp.int32, own_rows)
    row_mask = (positions < lengths[0]).astype(F32)[:, None]
    scale_two = lax.rsqrt(jnp.mean(resid * resid, axis=1, keepdims=True) + EPSILON)
    normal_two = resid * scale_two
    h_two_own = (normal_two * norm_mlp_gain).astype(BF16)
    h_two = ordered(h_two_own, swap(h_two_own), 0)
    resid_grad = row_mask * cotangent[0].astype(F32)
    low_own = resid_grad.astype(BF16)
    resid_low = ordered(low_own, swap(low_own), 0)
    pre_gate = dot(h_two, weights[:, :half])
    up_part = dot(h_two, weights[:, half : 2 * half])
    pre_sigmoid = sigmoid(pre_gate)
    inner = (pre_gate * pre_sigmoid * up_part).astype(BF16)
    inner_grad = dot(resid_low, weights[:, 2 * half :])
    pre_grad = (
        inner_grad * up_part * pre_sigmoid * (1.0 + pre_gate * (1.0 - pre_sigmoid))
    ).astype(BF16)
    up_grad = (inner_grad * pre_gate * pre_sigmoid).astype(BF16)
    mlp_out = sum_rows(dot(inner, weights[:, 2 * half :], 1, 1), here)
    output = (row_mask * (resid + mlp_out)).astype(BF16)[None]
    h_two_grad = sum_rows(
        dot(pre_grad, weights[:, :half], 1, 1) + dot(up_grad, weights[:, half : 2 * half], 1, 1), here
    )
    grad_mlp = jnp.concatenate(
        [
            dot(h_two, pre_grad, 0, 0).astype(BF16),
            dot(h_two, up_grad, 0, 0).astype(BF16),
            dot(resid_low, inner, 0, 0).astype(BF16),
        ],
        axis=1,
    )
    grad_mlp = lax.psum_scatter(grad_mlp, "dp", scatter_dimension=0, tiled=True)
    resid_total = resid_grad + norm_backward(h_two_grad, norm_mlp_gain, normal_two, scale_two)
    gain_two_grad = jnp.sum(h_two_grad * normal_two, axis=0)

    attn_own = resid_total.astype(BF16)
    attn_low = ordered(attn_own, swap(attn_own), 0)
    mixed_grad = dot(attn_low, w_out, 1, 1)
    out_grad = dot(attn_low, mixed, 0, 0)
    query_grad, key_grad, value_grad, gate_grad, logits_grad, out_gain_grad = attention_backward(
        mixed_grad, query, key, value, logits, gate, attended, states, out_gain
    )
    bias_grad = jnp.sum(logits_grad, axis=0)
    grad_high, grad_rest = split_low(logits_grad)
    low_out_grad = (
        dot(low_high, grad_high, 0, 0) + dot(low_rest, grad_high, 0, 0) + dot(low_high, grad_rest, 0, 0)
    )
    low_rank_low = (dot(grad_high, w_low_out, 1, 1) + dot(grad_rest, w_low_out, 1, 1)).astype(BF16)
    low_in_grad = dot(h_low, low_rank_low, 0, 0)
    attn_grads = jnp.concatenate(
        [
            dot(h_low, query_grad, 0, 0).astype(BF16),
            dot(h_low, key_grad, 0, 0).astype(BF16),
            dot(h_low, value_grad, 0, 0).astype(BF16),
            dot(h_low, gate_grad, 0, 0).astype(BF16),
            out_grad.astype(BF16),
        ],
        axis=1,
    )
    attn_grads = lax.psum_scatter(attn_grads, "dp", scatter_dimension=0, tiled=True).astype(F32)
    h_grad = sum_rows(
        dot(query_grad, w_query, 1, 1)
        + dot(key_grad, w_key, 1, 1)
        + dot(value_grad, w_value, 1, 1)
        + dot(gate_grad, w_gate_out, 1, 1)
        + dot(low_rank_low, w_low_in, 1, 1),
        here,
    )
    own_wide = tokens_own.astype(F32)
    own_scale = lax.rsqrt(jnp.mean(own_wide * own_wide, axis=1, keepdims=True) + EPSILON)
    normal_own = own_wide * own_scale
    tokens_grad = resid_total + norm_backward(h_grad, norm_attn_gain, normal_own, own_scale)
    gain_one_grad = jnp.sum(h_grad * normal_own, axis=0)

    low_rank_width = w_low_out.shape[0]
    decay_part = jnp.concatenate([low_out_grad, bias_grad[None]], axis=0)
    slots = jnp.zeros((2,) + decay_part.shape, F32)
    slots = lax.dynamic_update_slice(slots, decay_part[None], (here, 0, 0))
    packed = jnp.concatenate(
        [
            gain_one_grad, gain_two_grad, out_gain_grad.reshape(-1), low_in_grad.reshape(-1), slots.reshape(-1),
        ]
    )
    packed = lax.psum(packed, ("dp", "head"))
    width = gain_one_grad.shape[0]
    edges = [width, 2 * width, 2 * width + VALUE_HEAD]
    edges.append(edges[-1] + width * low_rank_width)
    low_in_grad = packed[edges[2] : edges[3]].reshape(width, low_rank_width)
    decay_part = lax.dynamic_index_in_dim(packed[edges[3] :].reshape(slots.shape), here, 0, keepdims=False)

    own_half = half_of(grad_mlp, here, 0)
    other_half = swap(half_of(grad_mlp, 1 - here, 0))
    grad_mlp = ordered(
        own_half.reshape(shard_rows, 3, 1, half), other_half.reshape(shard_rows, 3, 1, half), 2
    ).reshape(shard_rows, 3 * hidden).astype(F32)
    return (
        output,
        tokens_grad[None],
        packed[: edges[0]],
        attn_grads[:, :keys],
        attn_grads[:, keys : 2 * keys],
        attn_grads[:, 2 * keys : 2 * keys + values],
        attn_grads[:, 2 * keys + values : 2 * keys + 2 * values],
        low_in_grad,
        decay_part[:low_rank_width],
        decay_part[low_rank_width],
        packed[edges[1] : edges[2]],
        attn_grads[:, 2 * keys + 2 * values :].T,
        packed[edges[0] : edges[1]],
        grad_mlp,
    )


def solution(mesh):
    return jax.shard_map(
        per_device,
        mesh=mesh,
        in_specs=(
            P("dp", "head", None),
            P("dp"),
            P("dp", "head", None, None),
            P(),
            P(None, "head"),
            P(None, "head"),
            P(None, "head"),
            P(None, "head"),
            P(),
            P(None, "head"),
            P("head"),
            P(),
            P("head", None),
            P(),
            P(("dp", "head"), None),
            P("dp", "head", None),
        ),
        out_specs=(
            P("dp", "head", None),
            P("dp", "head", None),
            P(),
            P("dp", "head"),
            P("dp", "head"),
            P("dp", "head"),
            P("dp", "head"),
            P(),
            P(None, "head"),
            P("head"),
            P(),
            P("head", "dp"),
            P(),
            P(("dp", "head"), None),
        ),
        check_vma=False,
    )
```

time: 1410 us -> 638 us (0.45)
  waiting for transfers between devices: 696 us -> 431 us
  matrix products: 300 us -> 86.3 us
  local copies, waits for them, and re-layouts: 192 us -> 37.7 us
  blocking collectives: 117 us -> 0 us
  other arithmetic: 72.7 us -> 34.3 us
  Pallas kernels: 0 us -> 20.6 us
    reduce_scatter x8 -> x1, waiting for transfers between devices: 562 us -> 169 us  [per_device(): grad_mlp = lax.psum_scatter(grad_mlp, 'dp', scatter_dimension=0, tiled=True)]
    dot_general x129 -> x34, matrix products: 300 us -> 86.3 us  [dot(): lax.dot_general(left, right, (((left_dim,), (right_dim,)), ((), ())), pre...]
    psum x2 -> x0, blocking collectives: 117 us -> none  [the longest x1 76.4 us: per_device(): summed_decay = lax.psum((low_out_grad, bias_grad), 'dp')]
    squeeze x80 -> x0, local copies, waits for them, and re-layouts: 90.7 us -> none  [gated_linear_attention(): final_memory, carried = lax.scan(jax.checkpoint(advance), initial, moved)]
    unnamed x12 -> x5, waiting for transfers between devices: 1.37 us -> 92 us
    psum x1, waiting for transfers between devices: 0.01 us -> 84.1 us  [per_device(): packed = lax.psum(packed, ('dp', 'head'))]
    all_gather x3 -> x1, waiting for transfers between devices: 132 us -> 78 us  [per_device(): lax.all_gather(ordered(own_piece, other_piece, 0), 'dp', axis=0, tiled=True)]
    dynamic_update_slice x32 -> x0, local copies, waits for them, and re-layouts: 32.6 us -> none  [gated_linear_attention(): final_memory, carried = lax.scan(jax.checkpoint(advance), initial, moved)]
  transfers between devices with their start and end apart: 12 -> 14, of which waited for: 8 -> 9; matrix products, arithmetic and copies ran while one was open for 5% -> 13% of each run, Pallas kernels for 0% -> 1%
where the time goes in v1:
time: 638 us; the launch traced here: 629 us
  waiting for transfers between devices  431 us (68%)
  matrix products  86.3 us (14%)
  local copies, waits for them, and re-layouts  37.7 us (6%)
  other arithmetic  34.3 us (5%)
  Pallas kernels  20.6 us (3%)
  between operations  15.7 us (2%)
    reduce_scatter x1, waiting for transfers between devices, per_device(): grad_mlp = lax.psum_scatter(grad_mlp, 'dp', scatter_dimension=0, tiled=True)  169 us
    unnamed x5, waiting for transfers between devices  92 us
    dot_general x34, matrix products, dot(): lax.dot_general(left, right, (((left_dim,), (right_dim,)), ((), ())), pre...  86.3 us
    psum x1, waiting for transfers between devices, per_device(): packed = lax.psum(packed, ('dp', 'head'))  84.1 us
    all_gather x1, waiting for transfers between devices, per_device(): lax.all_gather(ordered(own_piece, other_piece, 0), 'dp', axis=0, tiled=True)  78 us
    unnamed x112, local copies, waits for them, and re-layouts  21.5 us
    concatenate x4, other arithmetic, ordered(): joined = jnp.concatenate([own, other, own], axis=axis)  14.1 us
  transfers between devices with their start and end apart: 14, of which 9 were waited for; matrix products, arithmetic and copies ran while one was open for 13% of the time, Pallas kernels for 1%

profile of v1, /device:TPU:0, one launch (start us, length us, event | category | flops | bytes accessed | tf_op | source)
XLA Modules:
  0.0 629.1 jit_solution(16756206432461211538)
XLA Ops:
  8.6 3.5 dynamic-slice_reduce_fusion
  15.4 2.3 collective-permute-done
  25.8 2.6 fusion.73.gate_ref
  28.4 9.0 %attention_forward.1 = (f32[1024,512]{1,0:T(8,128)}, bf16[1024,512]{1,0:T(8,128)(2,1)S(1)}, bf16[8,2,128,256]{3,2,1,0:T(8,128)(2,1)S(1)}) custom-call(bf16[1024,256]{1,0:T(8,128)(2,1)S(1)} %convolution_convert_fusion.10.query_ref, bf16[1024,256]{1,0:T(8,128)(2,1)S(1)} %convolution_convert_fusion.9.key_ref, ...), custom_call_target="tpu_custom_call" | custom-call | tf_op jit(solution)/shard_map/attention_forward/pallas_call | solution.py:110
  41.8 2.8 multiply_reduce_fusion.2
  45.3 4.9 fusion.28
  50.2 4.7 fusion.30
  54.9 78.0 %all-gather.2.cloned.1.call-done = bf16[1024,4224]{1,0:T(8,128)(2,1)} async-done(((bf16[64,4224]{1,0:T(8,128)(2,1)}), bf16[1024,4224]{1,0:T(8,128)(2,1)}) %all-gather.2.cloned.1.call-update) | async-done | bytes 8650768 | tf_op jit(solution)/shard_map/all_gather | solution.py:302
  132.9 6.0 fusion.6
  138.9 5.2 fusion.12
  144.1 18.2 %multiply_convert_fusion.1 = (bf16[1024,1408]{1,0:T(8,128)(2,1)}, bf16[1024,1408]{1,0:T(8,128)(2,1)}, bf16[1024,1408]{1,0:T(8,128)(2,1)}) fusion(f32[1024,1408]{1,0:T(8,128)S(1)} %fusion.6, f32[1024,1408]{1,0:T(8,128)} %fusion.12, bf16[1024,1024]{1,0:T(8,128)(2,1)S(1)} %copy-done.27, bf16[1024,4224]{1,0:T(8,128)(2,1)S(1)} %copy-done.40), kind=kOutput, calls=%fused_computation.2 | convolution fusion | flops 2975858688 | bytes 25165824 | tf_op jit(solution)/shard_map/dot_general | solution.py:24
  162.4 5.4 fusion.10
  167.8 3.5 fusion.35
  171.5 3.4 fusion.8
  178.0 2.7 fusion.66
  181.1 2.3 collective-permute-done.7
  183.4 3.4 fusion.26
  186.8 2.8 fusion.75.mixed_grad_ref
  189.7 11.5 %attention_backward.1 = (bf16[1024,256]{1,0:T(8,128)(2,1)S(1)}, bf16[1024,256]{1,0:T(8,128)(2,1)S(1)}, bf16[1024,512]{1,0:T(8,128)(2,1)S(1)}, bf16[1024,512]{1,0...) custom-call(f32[1024,512]{1,0:T(8,128)} %fusion.75.mixed_grad_ref, bf16[1024,256]{1,0:T(8,128)(2,1)S(1)} %copy-done.5, ...), custom_call_target="tpu_custom_call" | custom-call | tf_op jit(solution)/shard_map/attention_backward/pallas_call | solution.py:236
  214.8 3.3 fusion.43
  218.0 2.3 fusion.40
  220.4 2.3 fusion.39
  226.1 3.9 fusion.38
  230.0 6.5 %copy.79 = bf16[1024,2048]{1,0:T(8,128)(2,1)} copy(bf16[1024,2048]{0,1:T(8,128)(2,1)} %fusion.38) | data formatting | bytes 8388608
  238.1 5.9 convolution_convert_fusion
  244.1 3.7 convolution_convert_fusion.1
  247.8 3.7 convolution_convert_fusion.2
  251.6 3.8 pad_maximum_fusion
  257.0 3.9 fusion.22
  260.8 84.1 %all-reduce.2.cloned.1.call-done = f32[27392]{0:T(1024)} async-done(((f32[27392]{0:T(1024)}), f32[27392]{0:T(1024)}) %all-reduce.2.cloned.1.call-update) | async-done | bytes 109584 | tf_op jit(solution)/shard_map/psum | solution.py:402
  351.3 91.9 %reduce-scatter.7.cloned.1.call-done = bf16[64,2048]{1,0:T(8,128)(2,1)} async-done(((bf16[1024,2048]{1,0:T(8,128)(2,1)}), bf16[64,2048]{1,0:T(8,128)(2,1)}) %reduce-scatter.7.cloned.1.call-update) | async-done | bytes 262160
  444.5 169.3 %reduce-scatter.5.cloned.1.call-done = bf16[64,4224]{1,0:T(8,128)(2,1)} async-done(((bf16[1024,4224]{1,0:T(8,128)(2,1)}), bf16[64,4224]{1,0:T(8,128)(2,1)}) %reduce-scatter.5.cloned.1.call-update) | async-done | bytes 540688 | tf_op jit(solution)/shard_map/reduce_scatter | solution.py:350
  (200 shorter events, 56.4 us)
Async XLA Ops:
  7.2 30.3 %copy-start = (bf16[512,1024]{1,0:T(8,128)(2,1)S(1)}, bf16[512,1024]{1,0:T(8,128)(2,1)}, u32[]{:S(2)}) copy-start(bf16[512,1024]{1,0:T(8,128)(2,1)} %param.28) | copy-start | bytes 3145732
  7.2 125.7 %all-gather.2.cloned.1.call-start = ((), (), s32[]{:S(2)}) async-start(), calls=%async_computation.2 | async-start | bytes 9191424 | tf_op jit(solution)/shard_map/all_gather | solution.py:302
  7.2 7.7 %copy-start.20 = (bf16[1,512,1024]{2,1,0:T(8,128)(2,1)S(1)}, bf16[1,512,1024]{2,1,0:T(8,128)(2,1)}, u32[]{:S(2)}) copy-start(bf16[1,512,1024]{2,1,0:T(8,128)(2,1)} %param.16) | copy-start | bytes 3145732
  12.1 1.7 collective-permute-start.3
  13.8 5.6 copy-start.38
  14.9 330.0 %all-reduce.2.cloned.1.call-start = ((), (), s32[]{:S(2)}) async-start(), calls=%async_computation.3 | async-start | bytes 221184 | tf_op jit(solution)/shard_map/psum | solution.py:402
  15.0 2.7 collective-permute-start
  20.1 5.5 copy-start.17
  21.5 6.9 %copy-start.2 = (f32[1024,256]{1,0:T(8,128)}, f32[1024,256]{1,0:T(8,128)S(1)}, u32[]{:S(2)}) copy-start(f32[1024,256]{1,0:T(8,128)S(1)} %fusion.41.logits_ref) | copy-start | bytes 3145732
  22.9 5.5 copy-start.4
  24.3 4.1 copy-start.6
  38.9 2.9 collective-permute-start.1
  41.3 4.0 collective-permute-start.5
  44.8 5.4 collective-permute-start.2
  132.9 6.0 copy-start.27
  132.9 6.0 copy-start.40
  162.4 5.4 copy-start.45
  167.8 3.7 copy-start.48
  171.4 4.3 collective-permute-start.6
  175.2 2.8 collective-permute-start.4
  180.7 2.7 collective-permute-start.7
  189.7 12.0 %copy-start.31 = (bf16[1024,256]{1,0:T(8,128)(2,1)S(1)}, bf16[1024,256]{1,0:T(8,128)(2,1)}, u32[]{:S(2)}) copy-start(bf16[1024,256]{1,0:T(8,128)(2,1)} %param.20) | copy-start | bytes 1572868
  201.2 4.9 copy-start.13
  213.6 9.0 %collective-permute-start.8 = (bf16[512,1024]{1,0:T(8,128)(2,1)}, bf16[512,1024]{1,0:T(8,128)(2,1)}, u32[]{:S(2)}, u32[]{:S(2)}) collective-permute-start(bf16[512,1024]{1,0:T(8,128)(2,1)} %dynamic-slice_convert_fusion), channel_id=1, source_target_pairs={{0,1},{1,0},{2,3},{3,2},{4,5},{5,4},{6,7},{7,6},{8,9},{9,8},{10,11... | collective-permute-start | bytes 3145736 | tf_op jit(solution)/shard_map/ppermute | solution.py:263
  214.7 3.3 copy-start.14
  222.7 3.4 copy-start.12
  226.0 217.2 %reduce-scatter.7.cloned.1.call-start = ((), (), s32[]{:S(2)}) async-start(), calls=%async_computation.5 | async-start | bytes 4456448
  236.5 377.3 %reduce-scatter.5.cloned.1.call-start = ((), (), s32[]{:S(2)}) async-start(), calls=%async_computation.4 | async-start | bytes 9191424 | tf_op jit(solution)/shard_map/reduce_scatter | solution.py:350
  238.1 5.9 copy-start.28
  238.1 5.9 copy-start.47
  244.1 3.7 copy-start.46
  614.9 4.1 collective-permute-start.9
  (31 other events, 62.7 us)
Sparse Core Ops, SparseCore 0:
  15.0 117.8 all-gather.1
  226.1 118.7 all-reduce.1
  347.2 95.9 reduce-scatter.6
  448.8 165.0 reduce-scatter.4

commit v2 on v1

--- a/solution.py
+++ b/solution.py
@@ -259,6 +259,348 @@
     )(mixed_grad, query, key, value, logits, gate, attended, states, gain.reshape(1, -1))
 
 
+MESH = pl.DeviceIdType.MESH
+ANY = pl.BlockSpec(memory_space=pl.ANY)
+
+
+class Place:
+    def __init__(self):
+        self.dp = lax.axis_index("dp")
+        self.head = lax.axis_index("head")
+        self.z = self.dp // 4
+        self.flat = self.dp % 4
+        self.flat_x = self.flat + 1 - 2 * (self.flat % 2)
+        self.flat_y = self.flat + 2 - 4 * (self.flat // 2)
+        self.flat_xy = 3 - self.flat
+        self.sibling = (self.dp, 1 - self.head)
+        self.beside_x = (self.z * 4 + self.flat_x, self.head)
+        self.beside_y = (self.z * 4 + self.flat_y, self.head)
+        self.along_z = [(((self.z + i) % 4) * 4 + self.flat, self.head) for i in range(1, 4)]
+
+    def meet(self):
+        barrier = pltpu.get_barrier_semaphore()
+        others = [self.sibling, self.beside_x, self.beside_y] + self.along_z
+        for other in others:
+            pl.semaphore_signal(barrier, 1, device_id=other, device_id_type=MESH)
+        pl.semaphore_wait(barrier, len(others))
+
+
+def send(source, target, out_sem, in_sem, device):
+    copy = pltpu.make_async_remote_copy(
+        src_ref=source, dst_ref=target, send_sem=out_sem, recv_sem=in_sem, device_id=device, device_id_type=MESH
+    )
+    copy.start()
+    return copy
+
+
+def arrived(target, out_sem, in_sem, device):
+    pltpu.make_async_remote_copy(
+        src_ref=target, dst_ref=target, send_sem=out_sem, recv_sem=in_sem, device_id=device, device_id_type=MESH
+    ).wait_recv()
+
+
+def chunk_columns(width, sizes):
+    starts = [sum(sizes[:i]) * 128 for i in range(len(sizes))]
+    assert sum(sizes) * 128 == width
+    return [slice(start, start + size * 128) for start, size in zip(starts, sizes)]
+
+
+class Gather:
+    def __init__(self, place, own, other, out, chunks, local_sem, out_sems, in_sems):
+        self.place, self.own, self.other, self.out, self.chunks = place, own, other, out, chunks
+        self.local_sem, self.out_sems, self.in_sems = local_sem, out_sems, in_sems
+        self.sent = []
+
+    def put(self, source, target, index, device):
+        chunk, slot = index
+        self.sent.append(send(source, target, self.out_sems.at[chunk, slot], self.in_sems.at[chunk, slot], device))
+
+    def wait(self, target, index):
+        chunk, slot = index
+        arrived(target, self.out_sems.at[chunk, slot], self.in_sems.at[chunk, slot], self.place.sibling)
+
+    def start(self):
+        at, rows = self.place, self.own.shape[0]
+        count = len(self.chunks)
+        mine = pl.ds(at.head * rows, rows)
+        theirs = pl.ds((1 - at.head) * rows, rows)
+        copy = pltpu.make_async_copy(self.own, self.out.at[at.z, at.flat, mine], self.local_sem)
+        copy.start()
+        self.put(self.other, self.out.at[at.z, at.flat, mine], (count, 0), at.sibling)
+        copy.wait()
+        self.wait(self.out.at[at.z, at.flat, theirs], (count, 0))
+
+    def stage(self, number, chunk):
+        at, out, columns = self.place, self.out, self.chunks[chunk]
+        everything = slice(None)
+        if number == 0:
+            block = out.at[at.z, at.flat, everything, columns]
+            for i in range(3):
+                self.put(block, block, (chunk, i), at.along_z[i])
+        if number == 1:
+            for i in range(3):
+                self.wait(out.at[(at.z + 3 - i) % 4, at.flat, everything, columns], (chunk, i))
+            block = out.at[everything, at.flat, everything, columns]
+            self.put(block, block, (chunk, 3), at.beside_x)
+            self.put(block, block, (chunk, 4), at.beside_y)
+        if number == 2:
+            self.wait(out.at[everything, at.flat_x, everything, columns], (chunk, 3))
+            block = out.at[pl.ds(0, 2), at.flat_x, everything, columns]
+            self.put(block, block, (chunk, 5), at.beside_y)
+            self.wait(out.at[everything, at.flat_y, everything, columns], (chunk, 4))
+            block = out.at[pl.ds(2, 2), at.flat_y, everything, columns]
+            self.put(block, block, (chunk, 6), at.beside_x)
+        if number == 3:
+            self.wait(out.at[pl.ds(0, 2), at.flat_xy, everything, columns], (chunk, 5))
+            self.wait(out.at[pl.ds(2, 2), at.flat_xy, everything, columns], (chunk, 6))
+
+    def finish(self):
+        for copy in self.sent:
+            copy.wait_send()
+
+
+def gather_kernel(chunks, own_ref, other_ref, out_ref, local_sem, out_sems, in_sems):
+    place = Place()
+    place.meet()
+    gather = Gather(place, own_ref, other_ref, out_ref, chunks, local_sem, out_sems, in_sems)
+    gather.start()
+    count = len(chunks)
+    for tick in range(count + 3):
+        for number in range(3, -1, -1):
+            if 0 <= tick - number < count:
+                gather.stage(number, tick - number)
+    gather.finish()
+
+
+def gather_weights(own, other):
+    rows, width = own.shape
+    tiles = width // 128
+    count = 6
+    first = max(tiles // 12, 1)
+    rest = tiles - first
+    sizes = [first] + [rest // (count - 1) + (1 if i < rest % (count - 1) else 0) for i in range(count - 1)]
+    chunks = chunk_columns(width, sizes)
+    return pl.pallas_call(
+        functools.partial(gather_kernel, chunks),
+        in_specs=[ANY, ANY],
+        out_specs=ANY,
+        out_shape=jax.ShapeDtypeStruct((4, 4, 2 * rows, width), own.dtype),
+        scratch_shapes=[
+            pltpu.SemaphoreType.DMA,
+            pltpu.SemaphoreType.DMA((count + 1, 7)),
+            pltpu.SemaphoreType.DMA((count + 1, 7)),
+        ],
+        compiler_params=pltpu.CompilerParams(collective_id=0, has_side_effects=True),
+        name="gather_weights",
+    )(own, other).reshape(32 * rows, width)
+
+
+class Reduce:
+    def __init__(self, place, partial, via_x, via_y, from_x, from_y, from_z, chunks, out_sems, in_sems):
+        self.place, self.partial, self.chunks = place, partial, chunks
+        self.via_x, self.via_y, self.from_x, self.from_y, self.from_z = via_x, via_y, from_x, from_y, from_z
+        self.out_sems, self.in_sems = out_sems, in_sems
+        self.sent = []
+
+    def put(self, source, target, index, device):
+        self.sent.append(send(source, target, self.out_sems.at[index], self.in_sems.at[index], device))
+
+    def wait(self, target, index):
+        arrived(target, self.out_sems.at[index], self.in_sems.at[index], self.place.sibling)
+
+    def stage(self, number, chunk):
+        at, partial, columns = self.place, self.partial, self.chunks[chunk]
+        everything = slice(None)
+        low, high = pl.ds(0, 2), pl.ds(2, 2)
+        view = (everything, everything, columns)
+        if number == 0:
+            self.put(partial.at[low, at.flat_xy, everything, columns], self.via_x.at[view], (chunk, 0), at.beside_x)
+            self.put(partial.at[high, at.flat_xy, everything, columns], self.via_y.at[view], (chunk, 1), at.beside_y)
+        if number == 1:
+            self.wait(self.via_x.at[view], (chunk, 0))
+            block = (low, at.flat_y, everything, columns)
+            partial[block] = (partial[block].astype(F32) + self.via_x[view].astype(F32)).astype(BF16)
+            self.put(partial.at[everything, at.flat_y, everything, columns], self.from_y.at[view], (chunk, 2), at.beside_y)
+            self.wait(self.via_y.at[view], (chunk, 1))
+            block = (high, at.flat_x, everything, columns)
+            partial[block] = (partial[block].astype(F32) + self.via_y[view].astype(F32)).astype(BF16)
+            self.put(partial.at[everything, at.flat_x, everything, columns], self.from_x.at[view], (chunk, 3), at.beside_x)
+        if number == 2:
+            self.wait(self.from_y.at[view], (chunk, 2))
+            self.wait(self.from_x.at[view], (chunk, 3))
+            block = (everything, at.flat, everything, columns)
+            partial[block] = (
+                partial[block].astype(F32) + self.from_x[view].astype(F32) + self.from_y[view].astype(F32)
+            ).astype(BF16)
+            for i in range(3):
+                self.put(
+                    partial.at[(at.z + 1 + i) % 4, at.flat, everything, columns],
+                    self.from_z.at[i, everything, columns],
+                    (chunk, 4 + i),
+                    at.along_z[i],
+                )
+
+    def result(self, chunk):
+        at, columns = self.place, self.chunks[chunk]
+        total = self.partial[at.z, at.flat, :, columns].astype(F32)
+        for i in range(3):
+            self.wait(self.from_z.at[i, :, columns], (chunk, 4 + i))
+            total += self.from_z[i, :, columns].astype(F32)
+        return total
+
+    def finish(self):
+        for copy in self.sent:
+            copy.wait_send()
+
+
+def reduce_kernel(
+    half, mlp_chunks, attn_chunks, mlp_ref, attn_ref, small_ref, mlp_out, attn_out, small_out,
+    mlp, attn, mlp_via_x, mlp_via_y, mlp_from_x, mlp_from_y, mlp_from_z,
+    attn_via_x, attn_via_y, attn_from_x, attn_from_y, attn_from_z, summed, swapped, small_in, small_z,
+    load_sems, mlp_sems_out, mlp_sems_in, attn_sems_out, attn_sems_in, other_sems_out, other_sems_in,
+):
+    at = Place()
+    loads = []
+    for i, columns in enumerate(mlp_chunks):
+        loads.append(pltpu.make_async_copy(mlp_ref.at[:, :, :, columns], mlp.at[:, :, :, columns], load_sems.at[i]))
+    for i, columns in enumerate(attn_chunks):
+        loads.append(
+            pltpu.make_async_copy(
+                attn_ref.at[:, :, :, columns], attn.at[:, :, :, columns], load_sems.at[len(mlp_chunks) + i]
+            )
+        )
+    for load in loads:
+        load.start()
+    at.meet()
+    sides = [
+        Reduce(at, mlp, mlp_via_x, mlp_via_y, mlp_from_x, mlp_from_y, mlp_from_z, mlp_chunks, mlp_sems_out, mlp_sems_in),
+        Reduce(
+            at, attn, attn_via_x, attn_via_y, attn_from_x, attn_from_y, attn_from_z, attn_chunks,
+            attn_sems_out, attn_sems_in,
+        ),
+    ]
+    order = [(0, i) for i in range(len(mlp_chunks))] + [(1, i) for i in range(len(attn_chunks))]
+    count = len(order)
+    rows = mlp.shape[2] // 2
+    sent = []
+
+    def put(source, target, slot, device):
+        sent.append(send(source, target, other_sems_out.at[slot], other_sems_in.at[slot], device))
+
+    def wait(target, slot):
+        arrived(target, other_sems_out.at[slot], other_sems_in.at[slot], at.sibling)
+
+    def small(step):
+        if step == 0:
+            put(small_ref, small_in.at[0], 0, at.sibling)
+        elif step in (1, 2):
+            source = small_ref if step == 1 else small_z.at[step - 2]
+            wait(small_in.at[step - 1], step - 1)
+            small_z[step - 1] = source[...] + small_in[step - 1]
+            put(small_z.at[step - 1], small_in.at[step], step, at.beside_x if step == 1 else at.beside_y)
+        elif step == 3:
+            wait(small_in.at[2], 2)
+            small_z[2 + at.z] = small_z[1] + small_in[2]
+            for i in range(3):
+                put(small_z.at[2 + at.z], small_z.at[2 + at.z], 3 + i, at.along_z[i])
+        elif step == 4:
+            for i in range(3):
+                wait(small_z.at[2 + (at.z + 3 - i) % 4], 3 + i)
+            small_out[...] = small_z[2] + small_z[3] + small_z[4] + small_z[5]
+
+    def result(side, chunk):
+        total = sides[side].result(chunk)
+        if side == 0:
+            columns = mlp_chunks[chunk]
+            summed[:, columns] = total
+            put(
+                summed.at[pl.ds((1 - at.head) * rows, rows), columns], swapped.at[:, columns], 6 + chunk, at.sibling
+            )
+        else:
+            attn_out[:, attn_chunks[chunk]] = total
+
+    for tick in range(count + 3):
+        if 0 <= tick - 3 < count:
+            result(*order[tick - 3])
+        for number in range(2, -1, -1):
+            if 0 <= tick - number < count:
+                if number == 0:
+                    loads[tick].wait()
+                side, chunk = order[tick - number]
+                sides[side].stage(number, chunk)
+        if tick < 5:
+            small(tick)
+    for part in range(3):
+        columns = slice(part * half, (part + 1) * half)
+        mine = pl.ds(pl.multiple_of(part * 2 * half + at.head * half, 128), half)
+        mlp_out[:, mine] = summed[pl.ds(pl.multiple_of(at.head * rows, 8), rows), columns]
+    for chunk, columns in enumerate(mlp_chunks):
+        wait(swapped.at[:, columns], 6 + chunk)
+    for part in range(3):
+        columns = slice(part * half, (part + 1) * half)
+        other = pl.ds(pl.multiple_of(part * 2 * half + (1 - at.head) * half, 128), half)
+        mlp_out[:, other] = swapped[:, columns]
+    for copy in sent:
+        copy.wait_send()
+    for side in sides:
+        side.finish()
+
+
+def reduce_gradients(mlp, attn, small):
+    rows = mlp.shape[0] // 16
+    half = mlp.shape[1] // 3
+    tiles = mlp.shape[1] // 128
+    mlp_count = 6
+    mlp_chunks = chunk_columns(
+        mlp.shape[1], [tiles // mlp_count + (1 if i < tiles % mlp_count else 0) for i in range(mlp_count)]
+    )
+    attn_tiles = attn.shape[1] // 128
+    attn_count = 4
+    attn_chunks = chunk_columns(
+        attn.shape[1], [attn_tiles // attn_count + (1 if i < attn_tiles % attn_count else 0) for i in range(attn_count)]
+    )
+    vmem = pl.BlockSpec(memory_space=pltpu.VMEM)
+    buffers = []
+    for width in (mlp.shape[1], attn.shape[1]):
+        buffers += [
+            pltpu.VMEM((2, rows, width), BF16),
+            pltpu.VMEM((2, rows, width), BF16),
+            pltpu.VMEM((4, rows, width), BF16),
+            pltpu.VMEM((4, rows, width), BF16),
+            pltpu.VMEM((3, rows, width), BF16),
+        ]
+    return pl.pallas_call(
+        functools.partial(reduce_kernel, half, mlp_chunks, attn_chunks),
+        in_specs=[ANY, ANY, vmem],
+        out_specs=[vmem, vmem, vmem],
+        out_shape=[
+            jax.ShapeDtypeStruct((rows // 2, 6 * half), F32),
+            jax.ShapeDtypeStruct((rows, attn.shape[1]), F32),
+            jax.ShapeDtypeStruct(small.shape, F32),
+        ],
+        scratch_shapes=[
+            pltpu.VMEM((4, 4, rows, mlp.shape[1]), BF16),
+            pltpu.VMEM((4, 4, rows, attn.shape[1]), BF16),
+            *buffers,
+            pltpu.VMEM((rows, mlp.shape[1]), F32),
+            pltpu.VMEM((rows // 2, mlp.shape[1]), F32),
+            pltpu.VMEM((3,) + small.shape, F32),
+            pltpu.VMEM((6,) + small.shape, F32),
+            pltpu.SemaphoreType.DMA((mlp_count + attn_count,)),
+            pltpu.SemaphoreType.DMA((mlp_count, 7)),
+            pltpu.SemaphoreType.DMA((mlp_count, 7)),
+            pltpu.SemaphoreType.DMA((attn_count, 7)),
+            pltpu.SemaphoreType.DMA((attn_count, 7)),
+            pltpu.SemaphoreType.DMA((6 + mlp_count,)),
+            pltpu.SemaphoreType.DMA((6 + mlp_count,)),
+        ],
+        compiler_params=pltpu.CompilerParams(
+            collective_id=1, has_side_effects=True, vmem_limit_bytes=58 << 20
+        ),
+        name="reduce_gradients",
+    )(mlp.reshape(4, 4, rows, -1), attn.reshape(4, 4, rows, -1), small)
+
+
 def swap(value):
     return lax.ppermute(value, "head", [(0, 1), (1, 0)])
 
@@ -295,11 +637,15 @@
     hidden = w_mlp.shape[1] // 3
     half = hidden // 2
     shard_rows = w_mlp.shape[0]
+    square = lax.axis_size("dp") == 16
 
     pieces = w_mlp.reshape(shard_rows, 3, 2, half)
     own_piece = half_of(pieces, here, 2).reshape(shard_rows, 3 * half)
-    other_piece = swap(half_of(pieces, 1 - here, 2).reshape(shard_rows, 3 * half))
-    weights = lax.all_gather(ordered(own_piece, other_piece, 0), "dp", axis=0, tiled=True)
+    other_piece = half_of(pieces, 1 - here, 2).reshape(shard_rows, 3 * half)
+    if square:
+        weights = gather_weights(own_piece, other_piece)
+    else:
+        weights = lax.all_gather(ordered(own_piece, swap(other_piece), 0), "dp", axis=0, tiled=True)
 
     tokens_own = tokens[0]
     tokens_wide = ordered(tokens_own, swap(tokens_own), 0).astype(F32)
@@ -347,7 +693,6 @@
         ],
         axis=1,
     )
-    grad_mlp = lax.psum_scatter(grad_mlp, "dp", scatter_dimension=0, tiled=True)
     resid_total = resid_grad + norm_backward(h_two_grad, norm_mlp_gain, normal_two, scale_two)
     gain_two_grad = jnp.sum(h_two_grad * normal_two, axis=0)
 
@@ -375,7 +720,6 @@
         ],
         axis=1,
     )
-    attn_grads = lax.psum_scatter(attn_grads, "dp", scatter_dimension=0, tiled=True).astype(F32)
     h_grad = sum_rows(
         dot(query_grad, w_query, 1, 1)
         + dot(key_grad, w_key, 1, 1)
@@ -399,18 +743,25 @@
             gain_one_grad, gain_two_grad, out_gain_grad.reshape(-1), low_in_grad.reshape(-1), slots.reshape(-1),
         ]
     )
-    packed = lax.psum(packed, ("dp", "head"))
+    if square:
+        packed = packed.reshape(-1, 128)
+        grad_mlp, attn_grads, packed = reduce_gradients(grad_mlp, attn_grads, packed)
+        packed = packed.reshape(-1)
+    else:
+        packed = lax.psum(packed, ("dp", "head"))
+        attn_grads = lax.psum_scatter(attn_grads, "dp", scatter_dimension=0, tiled=True).astype(F32)
+        grad_mlp = lax.psum_scatter(grad_mlp, "dp", scatter_dimension=0, tiled=True)
+        own_half = half_of(grad_mlp, here, 0)
+        other_half = swap(half_of(grad_mlp, 1 - here, 0))
+        grad_mlp = ordered(
+            own_half.reshape(shard_rows, 3, 1, half), other_half.reshape(shard_rows, 3, 1, half), 2
+        ).reshape(shard_rows, 3 * hidden).astype(F32)
     width = gain_one_grad.shape[0]
     edges = [width, 2 * width, 2 * width + VALUE_HEAD]
     edges.append(edges[-1] + width * low_rank_width)
     low_in_grad = packed[edges[2] : edges[3]].reshape(width, low_rank_width)
     decay_part = lax.dynamic_index_in_dim(packed[edges[3] :].reshape(slots.shape), here, 0, keepdims=False)
 
-    own_half = half_of(grad_mlp, here, 0)
-    other_half = swap(half_of(grad_mlp, 1 - here, 0))
-    grad_mlp = ordered(
-        own_half.reshape(shard_rows, 3, 1, half), other_half.reshape(shard_rows, 3, 1, half), 2
-    ).reshape(shard_rows, 3 * hidden).astype(F32)
     return (
         output,
         tokens_grad[None],

time: 638 us -> 410 us (0.64)
  waiting for transfers between devices: 431 us -> 2.52 us
  Pallas kernels: 20.6 us -> 252 us
  between operations: 15.7 us -> 2.39 us
  matrix products: 86.3 us -> 76.4 us
    pallas_call x0 -> x2, Pallas kernels: none -> 231 us  [the longest x1 132 us: reduce_gradients(): pl.pallas_call(functools.partial(reduce_kernel, half, mlp_chunks, attn_ch...]
    reduce_scatter x1 -> x0, waiting for transfers between devices: 169 us -> none  [per_device(): grad_mlp = lax.psum_scatter(grad_mlp, 'dp', scatter_dimension=0, tiled=True)]
    unnamed x5 -> x0, waiting for transfers between devices: 92 us -> none
    psum x1 -> x0, waiting for transfers between devices: 84.1 us -> none  [per_device(): packed = lax.psum(packed, ('dp', 'head'))]
    all_gather x1 -> x0, waiting for transfers between devices: 78 us -> none  [per_device(): lax.all_gather(ordered(own_piece, other_piece, 0), 'dp', axis=0, tiled=True)]
    dot_general x34, matrix products: 86.3 us -> 76.4 us  [dot(): lax.dot_general(left, right, (((left_dim,), (right_dim,)), ((), ())), pre...]
    unnamed x112 -> x116, local copies, waits for them, and re-layouts: 21.5 us -> 12 us
    concatenate x0 -> x1, local copies, waits for them, and re-layouts: none -> 6.77 us  [per_device(): jnp.concatenate([dot(h_low, query_grad, 0, 0).astype(BF16), dot(h_low, ke...]
  transfers between devices with their start and end apart: 14 -> 8, of which waited for: 9 -> 1; matrix products, arithmetic and copies ran while one was open for 13% -> 13% of each run, Pallas kernels for 1% -> 25%
where the time goes in v2:
time: 410 us; the launch traced here: 404 us
  Pallas kernels  252 us (61%)
  matrix products  76.4 us (19%)
  local copies, waits for them, and re-layouts  36 us (9%)
  other arithmetic  32.5 us (8%)
    pallas_call x1, Pallas kernels, reduce_gradients(): pl.pallas_call(functools.partial(reduce_kernel, half, mlp_chunks, attn_ch...  132 us
    pallas_call x1, Pallas kernels, gather_weights(): pl.pallas_call(functools.partial(gather_kernel, chunks), in_specs=[ANY, A...  98.9 us
    dot_general x34, matrix products, dot(): lax.dot_general(left, right, (((left_dim,), (right_dim,)), ((), ())), pre...  76.4 us
    unnamed x116, local copies, waits for them, and re-layouts  12 us
    pallas_call x1, Pallas kernels, attention_backward(): pl.pallas_call(backward_kernel, grid=(steps,), in_specs=[rows(values), ro...  11.7 us
    concatenate x3, other arithmetic, ordered(): joined = jnp.concatenate([own, other, own], axis=axis)  10.9 us
    pallas_call x1, Pallas kernels, attention_forward(): pl.pallas_call(forward_kernel, grid=(steps,), in_specs=[rows(keys), rows(...  8.87 us
  transfers between devices with their start and end apart: 8, of which 1 were waited for; matrix products, arithmetic and copies ran while one was open for 13% of the time, Pallas kernels for 25%

profile of v2, /device:TPU:0, one launch (start us, length us, event | category | flops | bytes accessed | tf_op | source)
XLA Modules:
  0.0 403.8 jit_solution(16703627533333356228)
XLA Ops:
  1.2 2.5 collective-permute-done
  3.7 2.6 fusion
  7.7 2.6 fusion.66.gate_ref
  14.9 8.9 %attention_forward.1 = (f32[1024,512]{1,0:T(8,128)}, bf16[1024,512]{1,0:T(8,128)(2,1)S(1)}, bf16[8,2,128,256]{3,2,1,0:T(8,128)(2,1)S(1)}) custom-call(bf16[1024,256]{1,0:T(8,128)(2,1)S(1)} %convolution_convert_fusion.10.query_ref, bf16[1024,256]{1,0:T(8,128)(2,1)S(1)} %convolution_convert_fusion.9.key_ref, ...), custom_call_target="tpu_custom_call" | custom-call | tf_op jit(solution)/shard_map/attention_forward/pallas_call | solution.py:110
  31.0 3.5 dynamic-slice_reduce_fusion
  36.0 98.9 %gather_weights.1 = bf16[4,4,64,4224]{3,2,1,0:T(8,128)(2,1)} custom-call(bf16[32,4224]{1,0:T(8,128)(2,1)} %bitcast.113, bf16[32,4224]{1,0:T(8,128)(2,1)} %bitcast.114), custom_call_target="tpu_custom_call" | custom-call | tf_op jit(solution)/shard_map/gather_weights/pallas_call | solution.py:383
  135.0 2.7 multiply_reduce_fusion.2
  138.1 3.9 fusion.28
  142.0 3.4 fusion.6
  145.4 3.6 fusion.30
  149.0 5.2 %fusion.12 = f32[1024,1408]{1,0:T(8,128)} fusion(bf16[1024,1024]{1,0:T(8,128)(2,1)S(1)} %fusion.30, bf16[1024,4224]{1,0:T(8,128)(2,1)S(1)} %bitcast.106), kind=kOutput, calls=%fused_computation.38 | convolution fusion | flops 2952790016 | bytes 10747904 | tf_op jit(solution)/shard_map/dot_general | solution.py:24
  154.2 9.6 %multiply_convert_fusion.1 = (bf16[1024,1408]{1,0:T(8,128)(2,1)}, bf16[1024,1408]{1,0:T(8,128)(2,1)}, bf16[1024,1408]{1,0:T(8,128)(2,1)}) fusion(f32[1024,1408]{1,0:T(8,128)S(1)} %fusion.6, f32[1024,1408]{1,0:T(8,128)} %fusion.12, bf16[1024,1024]{1,0:T(8,128)(2,1)S(1)} %fusion.30, bf16[1024,4224]{1,0:T(8,128)(2,1)S(1)} %bitcast.107), kind=kOutput, calls=%fused_computation.2 | convolution fusion | flops 2975858688 | bytes 25165824 | tf_op jit(solution)/shard_map/dot_general | solution.py:24
  163.9 5.4 %fusion.8 = f32[1024,1024]{1,0:T(8,128)S(1)} fusion(bf16[1024,1408]{1,0:T(8,128)(2,1)} %get-tuple-element.79, bf16[1024,4224]{1,0:T(8,128)(2,1)S(1)} %bitcast.108), kind=kOutput, calls=%fused_computation.34 | convolution fusion | flops 2952790016 | bytes 9961472 | tf_op jit(solution)/shard_map/dot_general | solution.py:24
  169.3 3.4 fusion.10
  172.8 3.5 fusion.35
  176.6 6.0 %convolution_convert_fusion.1 = bf16[1024,1408]{1,0:T(8,128)(2,1)S(1)} fusion(bf16[1024,1024]{1,0:T(8,128)(2,1)S(1)} %copy-done.36, bf16[1024,1408]{1,0:T(8,128)(2,1)} %get-tuple-element.80), kind=kOutput, calls=%fused_computation.12 | convolution fusion | flops 2954231808 | bytes 7864320 | tf_op jit(solution)/shard_map/dot_general | solution.py:24
  183.2 3.8 convolution_convert_fusion.2
  189.2 2.8 fusion.61
  192.1 3.7 convolution_convert_fusion
  195.8 3.7 pad_maximum_fusion
  199.6 3.4 fusion.26
  203.0 2.6 fusion.68.mixed_grad_ref
  205.6 11.7 %attention_backward.1 = (bf16[1024,256]{1,0:T(8,128)(2,1)S(1)}, bf16[1024,256]{1,0:T(8,128)(2,1)S(1)}, bf16[1024,512]{1,0:T(8,128)(2,1)S(1)}, bf16[1024,512]{1,0...) custom-call(f32[1024,512]{1,0:T(8,128)} %fusion.68.mixed_grad_ref, bf16[1024,256]{1,0:T(8,128)(2,1)S(1)} %copy-done.4, ...), custom_call_target="tpu_custom_call" | custom-call | tf_op jit(solution)/shard_map/attention_backward/pallas_call | solution.py:236
  217.8 2.8 fusion.69
  234.2 3.3 fusion.43
  237.5 2.3 fusion.40
  239.8 2.3 fusion.39
  242.1 2.3 fusion.38
  244.4 6.8 %copy.36 = bf16[1024,2048]{1,0:T(8,128)(2,1)} copy(bf16[1024,2048]{0,1:T(8,128)(2,1)} %fusion.38) | data formatting | bytes 8388608 | tf_op jit(solution)/shard_map/concatenate | solution.py:713
  251.2 2.5 fusion.23
  254.4 132.3 %reduce_gradients.1 = (f32[32,8448]{1,0:T(8,128)}, f32[64,2048]{1,0:T(8,128)}, f32[214,128]{1,0:T(8,128)}) custom-call(bf16[4,4,64,4224]{3,2,1,0:T(8,128)(2,1)} %bitcast.101, bf16[4,4,64,2048]{3,2,1,0:T(8,128)(2,1)} %bitcast.104, f32[214,128]{1,0:T(8,128)} %bitcast.115), custom_call_target="tpu_custom_call" | custom-call | tf_op jit(solution)/shard_map/reduce_gradients/pallas_call | solution.py:572
  398.2 4.3 %fusion.22 = f32[1,512,1024]{2,1,0:T(8,128)} fusion(f32[512,1024]{1,0:T(8,128)} %get-tuple-element.73, f32[512]{0:T(512)S(1)} %broadcast_multiply_fusion, f32[1024]{0:T(1024)S(1)} %copy-done.45, f32[512]{0:T(512)S(1)} %add_rsqrt_fusion.1, bf16[512,1024]{1,0:T(8,128)(2,1)S(1)} %collective-permute-done.7, f32[1024,1024]{1,0:T(8,128)} %copy-done.18, ...), kind=kLoop, calls=%fused_computation.48 | loop fusion | flops 4718592 | bytes 8396804 | tf_op jit(solution)/shard_map/broadcast_in_dim | solution.py:767
  (180 shorter events, 45.1 us)
Async XLA Ops:
  0.6 23.1 %copy-start = (bf16[512,1024]{1,0:T(8,128)(2,1)S(1)}, bf16[512,1024]{1,0:T(8,128)(2,1)}, u32[]{:S(2)}) copy-start(bf16[512,1024]{1,0:T(8,128)(2,1)} %param.28) | copy-start | bytes 3145732
  0.7 5.7 %copy-start.45 = (f32[1024]{0:T(1024)S(1)}, f32[1024]{0:T(1024)}, u32[]{:S(2)}) copy-start(f32[1024]{0:T(1024)} %param.19) | copy-start | bytes 12292
  0.7 3.0 collective-permute-start
  7.0 5.2 %copy-start.19 = (bf16[1024,1024]{1,0:T(8,128)(2,1)}, bf16[1024,1024]{1,0:T(8,128)(2,1)S(1)}, u32[]{:S(2)}) copy-start(bf16[1024,1024]{1,0:T(8,128)(2,1)S(1)} %fusion.2) | copy-start | bytes 6291460
  11.5 2.9 copy-start.2
  13.7 10.0 %copy-start.5 = (bf16[1024,256]{1,0:T(8,128)(2,1)}, bf16[1024,256]{1,0:T(8,128)(2,1)S(1)}, u32[]{:S(2)}) copy-start(bf16[1024,256]{1,0:T(8,128)(2,1)S(1)} %convolution_convert_fusion.9.key_ref) | copy-start | bytes 1572868
  14.4 10.6 %copy-start.1 = (f32[1024,256]{1,0:T(8,128)}, f32[1024,256]{1,0:T(8,128)S(1)}, u32[]{:S(2)}) copy-start(f32[1024,256]{1,0:T(8,128)S(1)} %fusion.41.logits_ref) | copy-start | bytes 3145732
  23.8 4.7 %copy-start.27 = (bf16[1,512,1024]{2,1,0:T(8,128)(2,1)S(1)}, bf16[1,512,1024]{2,1,0:T(8,128)(2,1)}, u32[]{:S(2)}) copy-start(bf16[1,512,1024]{2,1,0:T(8,128)(2,1)} %param.31) | copy-start | bytes 3145732
  27.4 107.5 %collective-permute-start.1 = (bf16[512,1024]{1,0:T(8,128)(2,1)}, bf16[512,1024]{1,0:T(8,128)(2,1)}, u32[]{:S(2)}, u32[]{:S(2)}) collective-permute-start(bf16[512,1024]{1,0:T(8,128)(2,1)} %dynamic-slice_convert_fusion.3), channel_id=1, source_target_pairs={{0,1},{1,0},{2,3},{3,2},{4,5},{5,4},{6,7},{7,6},{8,9},{9,8},{10,11... | collective-permute-start | bytes 3145736 | tf_op jit(solution)/shard_map/ppermute | solution.py:605
  29.7 108.3 %collective-permute-start.4 = (bf16[512,1024]{1,0:T(8,128)(2,1)}, bf16[512,1024]{1,0:T(8,128)(2,1)}, u32[]{:S(2)}, u32[]{:S(2)}) collective-permute-start(bf16[512,1024]{1,0:T(8,128)(2,1)} %fusion.34), channel_id=1, source_target_pairs={{0,1},{1,0},{2,3},{3,2},{4,5},{5,4},{6,7},{7,6},{8,9},{9,8},{10,11... | collective-permute-start | bytes 3145736 | tf_op jit(solution)/shard_map/ppermute | solution.py:605
  36.0 99.0 %copy-start.24 = (bf16[1,512,1024]{2,1,0:T(8,128)(2,1)S(1)}, bf16[1,512,1024]{2,1,0:T(8,128)(2,1)}, u32[]{:S(2)}) copy-start(bf16[1,512,1024]{2,1,0:T(8,128)(2,1)} %param.16) | copy-start | bytes 3145732
  135.0 7.0 %copy-start.26 = (bf16[4,4,64,4224]{3,2,1,0:T(8,128)(2,1)S(1)}, bf16[4,4,64,4224]{3,2,1,0:T(8,128)(2,1)}, u32[]{:S(2)}) copy-start(bf16[4,4,64,4224]{3,2,1,0:T(8,128)(2,1)} %gather_weights.1) | copy-start | bytes 25952260
  138.0 7.4 %collective-permute-start.2 = (bf16[512,1024]{1,0:T(8,128)(2,1)S(1)}, bf16[512,1024]{1,0:T(8,128)(2,1)S(1)}, u32[]{:S(2)}, u32[]{:S(2)}) collective-permute-start(bf16[512,1024]{1,0:T(8,128)(2,1)S(1)} %multiply_convert_fusion.4), channel_id=1, source_target_pairs={{0,1},{1,0},{2,3},{3,2},{4,5},{5,4},{6,7},{7,6},{8,9},{9,8},{10,11... | collective-permute-start | bytes 3145736 | tf_op jit(solution)/shard_map/ppermute | solution.py:605
  141.9 3.4 copy-start.33
  149.0 5.2 %copy-start.35 = (bf16[1024,1024]{1,0:T(8,128)(2,1)}, bf16[1024,1024]{1,0:T(8,128)(2,1)S(1)}, u32[]{:S(2)}) copy-start(bf16[1024,1024]{1,0:T(8,128)(2,1)S(1)} %fusion.30) | copy-start | bytes 6291460
  163.9 5.4 %copy-start.53 = (bf16[1024,1408]{1,0:T(8,128)(2,1)S(1)}, bf16[1024,1408]{1,0:T(8,128)(2,1)}, u32[]{:S(2)}) copy-start(bf16[1024,1408]{1,0:T(8,128)(2,1)} %get-tuple-element.80) | copy-start | bytes 8650756
  169.3 13.3 %copy-start.28 = (f32[1024,1024]{1,0:T(8,128)}, f32[1024,1024]{1,0:T(8,128)S(1)}, u32[]{:S(2)}) copy-start(f32[1024,1024]{1,0:T(8,128)S(1)} %fusion.8) | copy-start | bytes 12582916
  169.3 3.5 copy-start.51
  172.8 3.9 copy-start.36
  176.4 10.6 %collective-permute-start.5 = (bf16[512,1024]{1,0:T(8,128)(2,1)S(1)}, bf16[512,1024]{1,0:T(8,128)(2,1)S(1)}, u32[]{:S(2)}, u32[]{:S(2)}) collective-permute-start(bf16[512,1024]{1,0:T(8,128)(2,1)S(1)} %dynamic-slice_convert_fusion.1), channel_id=1, source_target_pairs={{0,1},{1,0},{2,3},{3,2},{4,5},{5,4},{6,7},{7,6},{8,9},{9,8},{10,11... | collective-permute-start | bytes 3145736 | tf_op jit(solution)/shard_map/ppermute | solution.py:605
  182.8 5.0 %collective-permute-start.3 = (bf16[512,1024]{1,0:T(8,128)(2,1)S(1)}, bf16[512,1024]{1,0:T(8,128)(2,1)S(1)}, u32[]{:S(2)}, u32[]{:S(2)}) collective-permute-start(bf16[512,1024]{1,0:T(8,128)(2,1)S(1)} %dynamic-slice_convert_fusion.2), channel_id=1, source_target_pairs={{0,1},{1,0},{2,3},{3,2},{4,5},{5,4},{6,7},{7,6},{8,9},{9,8},{10,11... | collective-permute-start | bytes 3145736 | tf_op jit(solution)/shard_map/ppermute | solution.py:605
  187.7 4.3 %copy-start.34 = (bf16[1024,1024]{1,0:T(8,128)(2,1)S(1)}, bf16[1024,1024]{1,0:T(8,128)(2,1)}, u32[]{:S(2)}) copy-start(bf16[1024,1024]{1,0:T(8,128)(2,1)} %copy-done.33) | copy-start | bytes 6291460
  187.8 4.3 %copy-start.52 = (bf16[1024,1408]{1,0:T(8,128)(2,1)S(1)}, bf16[1024,1408]{1,0:T(8,128)(2,1)}, u32[]{:S(2)}) copy-start(bf16[1024,1408]{1,0:T(8,128)(2,1)} %get-tuple-element.79) | copy-start | bytes 8650756
  191.9 7.7 %collective-permute-start.6 = (bf16[512,1024]{1,0:T(8,128)(2,1)S(1)}, bf16[512,1024]{1,0:T(8,128)(2,1)S(1)}, u32[]{:S(2)}, u32[]{:S(2)}) collective-permute-start(bf16[512,1024]{1,0:T(8,128)(2,1)S(1)} %get-tuple-element.72), channel_id=1, source_target_pairs={{0,1},{1,0},{2,3},{3,2},{4,5},{5,4},{6,7},{7,6},{8,9},{9,8},{10,11... | collective-permute-start | bytes 3145736 | tf_op jit(solution)/shard_map/ppermute | solution.py:605
  205.6 12.1 %copy-start.39 = (bf16[1024,256]{1,0:T(8,128)(2,1)S(1)}, bf16[1024,256]{1,0:T(8,128)(2,1)}, u32[]{:S(2)}) copy-start(bf16[1024,256]{1,0:T(8,128)(2,1)} %param.20) | copy-start | bytes 1572868
  217.3 3.3 copy-start.12
  217.3 3.3 copy-start.15
  233.6 17.6 %collective-permute-start.7 = (bf16[512,1024]{1,0:T(8,128)(2,1)}, bf16[512,1024]{1,0:T(8,128)(2,1)S(1)}, u32[]{:S(2)}, u32[]{:S(2)}) collective-permute-start(bf16[512,1024]{1,0:T(8,128)(2,1)} %dynamic-slice_convert_fusion), channel_id=1, source_target_pairs={{0,1},{1,0},{2,3},{3,2},{4,5},{5,4},{6,7},{7,6},{8,9},{9,8},{10,11... | collective-permute-start | bytes 3145736 | tf_op jit(solution)/shard_map/ppermute | solution.py:605
  234.1 3.3 copy-start.17
  234.2 3.3 copy-start.22
  244.4 6.8 %copy-start.25 = (bf16[1,512,1024]{2,1,0:T(8,128)(2,1)S(1)}, bf16[1,512,1024]{2,1,0:T(8,128)(2,1)}, u32[]{:S(2)}) copy-start(bf16[1,512,1024]{2,1,0:T(8,128)(2,1)} %param.16) | copy-start | bytes 3145732
  398.2 4.3 %copy-start.37 = (f32[32,8448]{1,0:T(8,128)S(1)}, f32[32,8448]{1,0:T(8,128)}, u32[]{:S(2)}) copy-start(f32[32,8448]{1,0:T(8,128)} %get-tuple-element.117) | copy-start | bytes 3244036
  (30 other events, 54.5 us)

commit v3 on v2

--- a/solution.py
+++ b/solution.py
@@ -305,94 +305,442 @@
     return [slice(start, start + size * 128) for start, size in zip(starts, sizes)]
 
 
+ROWS = 256
+
+
 class Gather:
-    def __init__(self, place, own, other, out, chunks, local_sem, out_sems, in_sems):
-        self.place, self.own, self.other, self.out, self.chunks = place, own, other, out, chunks
-        self.local_sem, self.out_sems, self.in_sems = local_sem, out_sems, in_sems
-        self.sent = []
-
-    def put(self, source, target, index, device):
-        chunk, slot = index
-        self.sent.append(send(source, target, self.out_sems.at[chunk, slot], self.in_sems.at[chunk, slot], device))
-
-    def wait(self, target, index):
-        chunk, slot = index
+    def __init__(self, place, pieces, others, blocks, local_sems, out_sems, in_sems):
+        self.place, self.pieces, self.others, self.blocks = place, pieces, others, blocks
+        self.local_sems, self.out_sems, self.in_sems = local_sems, out_sems, in_sems
+
+    def put(self, source, target, chunk, slot, device):
+        send(source, target, self.out_sems.at[chunk, slot], self.in_sems.at[chunk, slot], device)
+
+    def wait(self, target, chunk, slot):
         arrived(target, self.out_sems.at[chunk, slot], self.in_sems.at[chunk, slot], self.place.sibling)
 
     def start(self):
-        at, rows = self.place, self.own.shape[0]
-        count = len(self.chunks)
+        at, count = self.place, len(self.blocks)
+        rows = self.pieces[0].shape[0]
         mine = pl.ds(at.head * rows, rows)
         theirs = pl.ds((1 - at.head) * rows, rows)
-        copy = pltpu.make_async_copy(self.own, self.out.at[at.z, at.flat, mine], self.local_sem)
-        copy.start()
-        self.put(self.other, self.out.at[at.z, at.flat, mine], (count, 0), at.sibling)
-        copy.wait()
-        self.wait(self.out.at[at.z, at.flat, theirs], (count, 0))
+        for chunk in range(count):
+            target = self.blocks[chunk].at[at.z, at.flat, mine]
+            pltpu.make_async_copy(self.pieces[chunk], target, self.local_sems.at[chunk]).start()
+            self.put(self.others[chunk], target, chunk, 7, at.sibling)
+        for chunk in range(count):
+            target = self.blocks[chunk].at[at.z, at.flat, mine]
+            pltpu.make_async_copy(self.pieces[chunk], target, self.local_sems.at[chunk]).wait()
+            self.wait(self.blocks[chunk].at[at.z, at.flat, theirs], chunk, 7)
 
     def stage(self, number, chunk):
-        at, out, columns = self.place, self.out, self.chunks[chunk]
+        at, out = self.place, self.blocks[chunk]
         everything = slice(None)
         if number == 0:
-            block = out.at[at.z, at.flat, everything, columns]
+            block = out.at[at.z, at.flat]
             for i in range(3):
-                self.put(block, block, (chunk, i), at.along_z[i])
+                self.put(block, block, chunk, i, at.along_z[i])
         if number == 1:
             for i in range(3):
-                self.wait(out.at[(at.z + 3 - i) % 4, at.flat, everything, columns], (chunk, i))
-            block = out.at[everything, at.flat, everything, columns]
-            self.put(block, block, (chunk, 3), at.beside_x)
-            self.put(block, block, (chunk, 4), at.beside_y)
+                self.wait(out.at[(at.z + 3 - i) % 4, at.flat], chunk, i)
+            block = out.at[everything, at.flat]
+            self.put(block, block, chunk, 3, at.beside_x)
+            self.put(block, block, chunk, 4, at.beside_y)
         if number == 2:
-            self.wait(out.at[everything, at.flat_x, everything, columns], (chunk, 3))
-            block = out.at[pl.ds(0, 2), at.flat_x, everything, columns]
-            self.put(block, block, (chunk, 5), at.beside_y)
-            self.wait(out.at[everything, at.flat_y, everything, columns], (chunk, 4))
-            block = out.at[pl.ds(2, 2), at.flat_y, everything, columns]
-            self.put(block, block, (chunk, 6), at.beside_x)
+            self.wait(out.at[everything, at.flat_x], chunk, 3)
+            block = out.at[pl.ds(0, 2), at.flat_x]
+            self.put(block, block, chunk, 5, at.beside_y)
+            self.wait(out.at[everything, at.flat_y], chunk, 4)
+            block = out.at[pl.ds(2, 2), at.flat_y]
+            self.put(block, block, chunk, 6, at.beside_x)
         if number == 3:
-            self.wait(out.at[pl.ds(0, 2), at.flat_xy, everything, columns], (chunk, 5))
-            self.wait(out.at[pl.ds(2, 2), at.flat_xy, everything, columns], (chunk, 6))
+            self.wait(out.at[pl.ds(0, 2), at.flat_xy], chunk, 5)
+            self.wait(out.at[pl.ds(2, 2), at.flat_xy], chunk, 6)
+
+    def tick(self, number):
+        for stage in range(3, -1, -1):
+            if 0 <= number - stage < len(self.blocks):
+                self.stage(stage, number - stage)
 
     def finish(self):
-        for copy in self.sent:
-            copy.wait_send()
-
-
-def gather_kernel(chunks, own_ref, other_ref, out_ref, local_sem, out_sems, in_sems):
-    place = Place()
-    place.meet()
-    gather = Gather(place, own_ref, other_ref, out_ref, chunks, local_sem, out_sems, in_sems)
-    gather.start()
-    count = len(chunks)
-    for tick in range(count + 3):
-        for number in range(3, -1, -1):
-            if 0 <= tick - number < count:
-                gather.stage(number, tick - number)
-    gather.finish()
-
-
-def gather_weights(own, other):
-    rows, width = own.shape
-    tiles = width // 128
-    count = 6
-    first = max(tiles // 12, 1)
-    rest = tiles - first
-    sizes = [first] + [rest // (count - 1) + (1 if i < rest % (count - 1) else 0) for i in range(count - 1)]
-    chunks = chunk_columns(width, sizes)
+        for chunk, block in enumerate(self.blocks):
+            everything = slice(None)
+            shapes = [block.at[0, 0]] * 3 + [block.at[everything, 0]] * 2 + [block.at[pl.ds(0, 2), 0]] * 2
+            shapes.append(self.others[chunk])
+            for slot, ref in enumerate(shapes):
+                sent(ref, self.out_sems.at[chunk, slot], self.in_sems.at[chunk, slot], self.place.sibling)
+
+
+def sent(source, out_sem, in_sem, device):
+    pltpu.make_async_remote_copy(
+        src_ref=source, dst_ref=source, send_sem=out_sem, recv_sem=in_sem, device_id=device, device_id_type=MESH
+    ).wait_send()
+
+
+def forward_block(query, key, value, logits, gate, gain, memory, states):
+    rise, fall, early, late, decay = decay_terms(logits)
+    lower = triangle(True)
+    attended_parts = []
+    mixed_parts = []
+    for head in range(memory.shape[0]):
+        keys_at = slice(head * KEY_HEAD, (head + 1) * KEY_HEAD)
+        values_at = slice(head * VALUE_HEAD, (head + 1) * VALUE_HEAD)
+        query_wide = query[:, keys_at].astype(F32)
+        key_wide = key[:, keys_at].astype(F32)
+        value_head = value[:, values_at]
+        state = memory[head]
+        state_low = state.astype(BF16)
+        states[head] = state_low
+        scores = dot(
+            (query_wide * rise[:, keys_at]).astype(BF16), (key_wide * fall[:, keys_at]).astype(BF16), 1, 1
+        )
+        scores = jnp.where(lower, scores, 0.0).astype(BF16)
+        left = jnp.concatenate([scores, (query_wide * early[:, keys_at]).astype(BF16)], axis=1)
+        attended = dot(left, jnp.concatenate([value_head, state_low], axis=0))
+        memory[head] = as_column(decay[:, keys_at], VALUE_HEAD) * state + dot(
+            (key_wide * late[:, keys_at]).astype(BF16), value_head, 0, 0
+        )
+        scale = lax.rsqrt(jnp.mean(attended * attended, axis=1, keepdims=True) + EPSILON)
+        gate_head = gate[:, values_at]
+        attended_parts.append(attended)
+        mixed_parts.append((attended * scale * gain * gate_head * sigmoid(gate_head)).astype(BF16))
+    return jnp.concatenate(attended_parts, axis=1), jnp.concatenate(mixed_parts, axis=1)
+
+
+def layer_kernel(
+    count,
+    tokens_ref, low_ref, mask_ref, gain_one_ref, gain_two_ref, gain_out_ref, bias_ref, start_ref,
+    w_query, w_key, w_value, w_gate, w_low_in, w_low_out, w_out, piece_zero, pieces, other_zero, others,
+    h_ref, query_ref, key_ref, value_ref, gate_ref, logits_ref, low_rank_ref, attended_ref, mixed_ref, states_ref,
+    grad_zero_ref, grad_ref, output_ref, total_ref, attn_ref, gain_grad_ref,
+    tokens, low, low_turned, h_two, h_two_turned, weights_zero, weights, resid, part_out, part_in,
+    mlp_sum, grad_sum, inner_all, pair_all, sums_out, sums_in, memory,
+    local_sems, gather_local, gather_out, gather_in, pair_out, pair_in,
+):
+    step = pl.program_id(0)
+    at = Place()
+    own = tokens_ref.shape[0]
+    length = 2 * own
+    tiles = length // ROWS
+    own_tiles = own // ROWS
+    own_at = at.head * own
+    gather = Gather(
+        at,
+        [piece_zero] + [pieces.at[i] for i in range(count - 1)],
+        [other_zero] + [others.at[i] for i in range(count - 1)],
+        [weights_zero] + [weights.at[i] for i in range(count - 1)],
+        gather_local, gather_out, gather_in,
+    )
+    attention_steps = tiles
+    first_step = attention_steps + 1
+    last_step = first_step + count - 1
+
+    def own_rows(i, size=ROWS):
+        return pl.ds(pl.multiple_of(own_at + i * ROWS, ROWS), size)
+
+    def other_rows(i, size=ROWS):
+        return pl.ds(pl.multiple_of(own - own_at + i * ROWS, ROWS), size)
+
+    def put(source, target, slot):
+        send(source, target, pair_out.at[slot], pair_in.at[slot], at.sibling)
+
+    def wait(target, slot):
+        arrived(target, pair_out.at[slot], pair_in.at[slot], at.sibling)
+
+    @pl.when(step == 0)
+    def _():
+        at.meet()
+        put(tokens_ref, tokens.at[own_rows(0, own)], 0)
+        put(low_ref, low.at[own_rows(0, own)], 1)
+        here = [
+            pltpu.make_async_copy(tokens_ref, tokens.at[own_rows(0, own)], local_sems.at[0]),
+            pltpu.make_async_copy(low_ref, low.at[own_rows(0, own)], local_sems.at[1]),
+        ]
+        for copy in here:
+            copy.start()
+        memory[...] = start_ref[...]
+        gain_grad_ref[...] = jnp.zeros_like(gain_grad_ref)
+        gather.start()
+        gather.tick(0)
+        for copy in here:
+            copy.wait()
+        wait(tokens.at[other_rows(0, own)], 0)
+        wait(low.at[other_rows(0, own)], 1)
+
+    for number in range(1, count + 3):
+
+        @pl.when(step == number)
+        def _():
+            gather.tick(number)
+
+    @pl.when(step < attention_steps)
+    def _():
+        rows = pl.ds(pl.multiple_of(step * ROWS, ROWS), ROWS)
+        wide = tokens[rows, :].astype(F32)
+        scale = lax.rsqrt(jnp.mean(wide * wide, axis=1, keepdims=True) + EPSILON)
+        h_low = (wide * scale * gain_one_ref[...]).astype(BF16)
+        h_ref[...] = h_low
+        query = dot(h_low, w_query[...]).astype(BF16)
+        key = dot(h_low, w_key[...]).astype(BF16)
+        value = dot(h_low, w_value[...]).astype(BF16)
+        gate = dot(h_low, w_gate[...])
+        low_rank = dot(h_low, w_low_in[...])
+        high, rest = split_low(low_rank)
+        logits = dot(high, w_low_out[...]) + dot(rest, w_low_out[...]) + bias_ref[...]
+        query_ref[...] = query
+        key_ref[...] = key
+        value_ref[...] = value
+        gate_ref[...] = gate
+        low_rank_ref[...] = low_rank
+        logits_ref[...] = logits
+        for i in range(ROWS // BLOCK):
+            block = slice(i * BLOCK, (i + 1) * BLOCK)
+            attended, mixed = forward_block(
+                query[block], key[block], value[block], logits[block], gate[block], gain_out_ref[...],
+                memory, states_ref.at[i],
+            )
+            attended_ref[block, :] = attended
+            mixed_ref[block, :] = mixed
+        part = dot(mixed_ref[...], w_out[...])
+        tile = step % own_tiles
+        tile_rows = pl.ds(pl.multiple_of(tile * ROWS, ROWS), ROWS)
+        mine = step // own_tiles == at.head
+
+        @pl.when(mine)
+        def _():
+            resid[tile_rows, :] = part
+
+        @pl.when(jnp.logical_not(mine))
+        def _():
+            part_out[tile_rows, :] = part.astype(BF16)
+            put(part_out.at[tile_rows], part_in.at[tile_rows], 2 + tile)
+
+    @pl.when(step == attention_steps)
+    def _():
+        for i in range(own_tiles):
+            rows = pl.ds(i * ROWS, ROWS)
+            wait(part_in.at[rows], 2 + i)
+            full = tokens[own_rows(i), :].astype(F32) + resid[rows, :] + part_in[rows, :].astype(F32)
+            resid[rows, :] = full
+            scale = lax.rsqrt(jnp.mean(full * full, axis=1, keepdims=True) + EPSILON)
+            h_two[own_rows(i), :] = (full * scale * gain_two_ref[...]).astype(BF16)
+            put(h_two.at[own_rows(i)], h_two.at[own_rows(i)], 4 + i)
+
+        def turn(i, carry):
+            rows = pl.ds(pl.multiple_of(i * ROWS, ROWS), ROWS)
+            low_turned[:, rows] = jnp.transpose(low[rows, :])
+            return carry
+
+        lax.fori_loop(0, tiles, turn, 0)
+        for i in range(own_tiles):
+            wait(h_two.at[other_rows(i)], 4 + i)
+
+        def turn_two(i, carry):
+            rows = pl.ds(pl.multiple_of(i * ROWS, ROWS), ROWS)
+            h_two_turned[:, rows] = jnp.transpose(h_two[rows, :])
+            return carry
+
+        lax.fori_loop(0, tiles, turn_two, 0)
+
+    def hidden_rows(block, first):
+        width = block.shape[3] // 3
+
+        def body(i, carry):
+            rows = pl.ds(pl.multiple_of(i * ROWS, ROWS), ROWS)
+            w_pair = block[:, :, :, : 2 * width].reshape(-1, 2 * width)
+            w_down = block[:, :, :, 2 * width :].reshape(-1, width)
+            pair = dot(h_two[rows, :], w_pair)
+            inner_grad = dot(low[rows, :], w_down)
+            pre_gate = pair[:, :width]
+            up_part = pair[:, width:]
+            pre_sigmoid = sigmoid(pre_gate)
+            swish = pre_gate * pre_sigmoid
+            inner = (swish * up_part).astype(BF16)
+            pre_grad = inner_grad * up_part * pre_sigmoid * (1.0 + pre_gate * (1.0 - pre_sigmoid))
+            both = jnp.concatenate([pre_grad.astype(BF16), (inner_grad * swish).astype(BF16)], axis=1)
+            inner_all[rows, :width] = inner
+            pair_all[rows, : 2 * width] = both
+            out_part = dot(inner, w_down, 1, 1)
+            grad_part = dot(both, w_pair, 1, 1)
+            if first:
+                mlp_sum[rows, :] = out_part
+                grad_sum[rows, :] = grad_part
+            else:
+                mlp_sum[rows, :] += out_part
+                grad_sum[rows, :] += grad_part
+            return carry
+
+        lax.fori_loop(0, tiles, body, 0)
+
+    def weight_rows(block, target):
+        width = block.shape[3] // 3
+
+        def body(i, carry):
+            rows = pl.ds(pl.multiple_of(i * ROWS, ROWS), ROWS)
+            shape = (target.shape[1], target.shape[2], -1)
+            target[i, :, :, : 2 * width] = (
+                dot(h_two_turned[rows, :], pair_all[:, : 2 * width]).astype(BF16).reshape(shape)
+            )
+            target[i, :, :, 2 * width :] = (
+                dot(low_turned[rows, :], inner_all[:, :width]).astype(BF16).reshape(shape)
+            )
+            return carry
+
+        lax.fori_loop(0, tiles, body, 0)
+
+    @pl.when(step == first_step)
+    def _():
+        hidden_rows(weights_zero, True)
+        weight_rows(weights_zero, grad_zero_ref)
+
+    @pl.when(step > first_step)
+    def _():
+        block = weights.at[step - first_step - 1]
+        hidden_rows(block, False)
+
+        @pl.when(step == last_step)
+        def _():
+            for i in range(own_tiles):
+                rows = pl.ds(i * ROWS, ROWS)
+                for k, source in enumerate((mlp_sum, grad_sum)):
+                    sums_out[k, rows, :] = source[other_rows(i), :].astype(BF16)
+                    put(sums_out.at[k, rows], sums_in.at[k, rows], 6 + 2 * i + k)
+
+        weight_rows(block, grad_ref.at[0])
+
+    @pl.when(step == last_step)
+    def _():
+        for i in range(own_tiles):
+            sent(h_two.at[pl.ds(0, ROWS)], pair_out.at[4 + i], pair_in.at[4 + i], at.sibling)
+        for i in range(own_tiles):
+            rows = pl.ds(i * ROWS, ROWS)
+            for k in range(2):
+                wait(sums_in.at[k, rows], 6 + 2 * i + k)
+            full = resid[rows, :]
+            scale = lax.rsqrt(jnp.mean(full * full, axis=1, keepdims=True) + EPSILON)
+            normal = full * scale
+            mlp_out = mlp_sum[own_rows(i), :] + sums_in[0, rows, :].astype(F32)
+            output_ref[rows, :] = (mask_ref[rows, :] * (full + mlp_out)).astype(BF16)
+            grad = grad_sum[own_rows(i), :] + sums_in[1, rows, :].astype(F32)
+            total = low[own_rows(i), :].astype(F32) + norm_backward(grad, gain_two_ref[...], normal, scale)
+            total_ref[rows, :] = total
+            gain_grad_ref[...] += jnp.sum(grad * normal, axis=0, keepdims=True)
+            h_two[own_rows(i), :] = total.astype(BF16)
+            put(h_two.at[own_rows(i)], h_two.at[own_rows(i)], 10 + i)
+            pltpu.make_async_copy(h_two.at[own_rows(i)], attn_ref.at[own_rows(i)], local_sems.at[i]).start()
+        gather.finish()
+        for i in range(own_tiles):
+            wait(h_two.at[other_rows(i)], 10 + i)
+            pltpu.make_async_copy(
+                h_two.at[other_rows(i)], attn_ref.at[other_rows(i)], local_sems.at[own_tiles + i]
+            ).start()
+        for slot, ref in enumerate(
+            [tokens_ref, low_ref] + [part_out.at[pl.ds(0, ROWS)]] * 8 + [h_two.at[pl.ds(0, ROWS)]] * 2
+        ):
+            if slot not in (4, 5):
+                sent(ref, pair_out.at[slot], pair_in.at[slot], at.sibling)
+        for i in range(tiles):
+            rows = own_rows(i) if i < own_tiles else other_rows(i - own_tiles)
+            pltpu.make_async_copy(h_two.at[rows], attn_ref.at[rows], local_sems.at[i]).wait()
+
+
+def whole(shape):
+    return pl.BlockSpec(shape, lambda i: (0,) * len(shape), pipeline_mode=pl.Buffered(1))
+
+
+def chunked(pieces, first):
+    rows, _, half = pieces.shape
+    rest = pieces[:, :, first:].reshape(rows, 3, -1, 2 * first)
+    return pieces[:, :, :first].reshape(rows, -1), rest.transpose(2, 0, 1, 3).reshape(-1, rows, 6 * first)
+
+
+def layer(
+    tokens, low, mask, gain_one, gain_two, gain_out, bias, start,
+    w_query, w_key, w_value, w_gate, w_low_in, w_low_out, w_out, own_piece, other_piece,
+):
+    own, width = tokens.shape
+    length = 2 * own
+    keys, values, heads = w_query.shape[1], w_value.shape[1], start.shape[0]
+    rank = w_low_in.shape[1]
+    piece_zero, pieces = chunked(own_piece, 128)
+    other_zero, others = chunked(other_piece, 128)
+    count = pieces.shape[0] + 1
+    group = 2 * piece_zero.shape[0]
+    tiles = length // ROWS
+    first_step = tiles + 1
+    steps = first_step + count
+
+    def rows_spec(columns):
+        return pl.BlockSpec((ROWS, columns), lambda i: (jnp.minimum(i, tiles - 1), 0))
+
+    vmem = pl.BlockSpec(memory_space=pltpu.VMEM)
+    row_shapes = [
+        (width, BF16), (keys, BF16), (keys, BF16), (values, BF16), (values, F32), (keys, F32), (rank, F32),
+        (values, F32), (values, BF16),
+    ]
+    blocks = ROWS // BLOCK
     return pl.pallas_call(
-        functools.partial(gather_kernel, chunks),
-        in_specs=[ANY, ANY],
-        out_specs=ANY,
-        out_shape=jax.ShapeDtypeStruct((4, 4, 2 * rows, width), own.dtype),
+        functools.partial(layer_kernel, count),
+        grid=(steps,),
+        in_specs=[
+            ANY, ANY, whole(mask.shape), whole((1, width)), whole((1, width)), whole((1, VALUE_HEAD)),
+            whole((1, keys)), whole(start.shape), whole(w_query.shape), whole(w_key.shape), whole(w_value.shape),
+            whole(w_gate.shape), whole(w_low_in.shape), whole(w_low_out.shape), whole(w_out.shape),
+            ANY, ANY, ANY, ANY,
+        ],
+        out_specs=[rows_spec(columns) for columns, _ in row_shapes]
+        + [
+            pl.BlockSpec((blocks, heads, KEY_HEAD, VALUE_HEAD), lambda i: (jnp.minimum(i, tiles - 1), 0, 0, 0)),
+            whole((4, 4, group, 384)),
+            pl.BlockSpec(
+                (1, 4, 4, group, 768), lambda i: (jnp.clip(i - first_step - 1, 0, count - 2), 0, 0, 0, 0)
+            ),
+            vmem, vmem, ANY, vmem,
+        ],
+        out_shape=[jax.ShapeDtypeStruct((length, columns), kind) for columns, kind in row_shapes]
+        + [
+            jax.ShapeDtypeStruct((length // BLOCK, heads, KEY_HEAD, VALUE_HEAD), BF16),
+            jax.ShapeDtypeStruct((4, 4, group, 384), BF16),
+            jax.ShapeDtypeStruct((count - 1, 4, 4, group, 768), BF16),
+            jax.ShapeDtypeStruct((own, width), BF16),
+            jax.ShapeDtypeStruct((own, width), F32),
+            jax.ShapeDtypeStruct((length, width), BF16),
+            jax.ShapeDtypeStruct((1, width), F32),
+        ],
         scratch_shapes=[
-            pltpu.SemaphoreType.DMA,
-            pltpu.SemaphoreType.DMA((count + 1, 7)),
-            pltpu.SemaphoreType.DMA((count + 1, 7)),
-        ],
-        compiler_params=pltpu.CompilerParams(collective_id=0, has_side_effects=True),
-        name="gather_weights",
-    )(own, other).reshape(32 * rows, width)
+            pltpu.VMEM((length, width), BF16),
+            pltpu.VMEM((length, width), BF16),
+            pltpu.VMEM((width, length), BF16),
+            pltpu.VMEM((length, width), BF16),
+            pltpu.VMEM((width, length), BF16),
+            pltpu.VMEM((4, 4, group, 384), BF16),
+            pltpu.VMEM((count - 1, 4, 4, group, 768), BF16),
+            pltpu.VMEM((own, width), F32),
+            pltpu.VMEM((own, width), BF16),
+            pltpu.VMEM((own, width), BF16),
+            pltpu.VMEM((length, width), F32),
+            pltpu.VMEM((length, width), F32),
+            pltpu.VMEM((length, 256), BF16),
+            pltpu.VMEM((length, 512), BF16),
+            pltpu.VMEM((2, own, width), BF16),
+            pltpu.VMEM((2, own, width), BF16),
+            pltpu.VMEM((heads, KEY_HEAD, VALUE_HEAD), F32),
+            pltpu.SemaphoreType.DMA((tiles,)),
+            pltpu.SemaphoreType.DMA((count,)),
+            pltpu.SemaphoreType.DMA((count, 8)),
+            pltpu.SemaphoreType.DMA((count, 8)),
+            pltpu.SemaphoreType.DMA((12,)),
+            pltpu.SemaphoreType.DMA((12,)),
+        ],
+        compiler_params=pltpu.CompilerParams(
+            collective_id=0, has_side_effects=True, vmem_limit_bytes=63 << 20
+        ),
+        name="layer",
+    )(
+        tokens, low, mask, gain_one.reshape(1, -1), gain_two.reshape(1, -1), gain_out.reshape(1, -1),
+        bias.reshape(1, -1), start, w_query, w_key, w_value, w_gate, w_low_in, w_low_out, w_out,
+        piece_zero, pieces, other_zero, others,
+    )
 
 
 class Reduce:
@@ -454,7 +802,7 @@
 
 
 def reduce_kernel(
-    half, mlp_chunks, attn_chunks, mlp_ref, attn_ref, small_ref, mlp_out, attn_out, small_out,
+    half, mlp_chunks, attn_chunks, zero_ref, mlp_ref, attn_ref, small_ref, mlp_out, attn_out, small_out,
     mlp, attn, mlp_via_x, mlp_via_y, mlp_from_x, mlp_from_y, mlp_from_z,
     attn_via_x, attn_via_y, attn_from_x, attn_from_y, attn_from_z, summed, swapped, small_in, small_z,
     load_sems, mlp_sems_out, mlp_sems_in, attn_sems_out, attn_sems_in, other_sems_out, other_sems_in,
@@ -462,7 +810,8 @@
     at = Place()
     loads = []
     for i, columns in enumerate(mlp_chunks):
-        loads.append(pltpu.make_async_copy(mlp_ref.at[:, :, :, columns], mlp.at[:, :, :, columns], load_sems.at[i]))
+        source = mlp_ref.at[i - 1] if i else zero_ref
+        loads.append(pltpu.make_async_copy(source, mlp.at[:, :, :, columns], load_sems.at[i]))
     for i, columns in enumerate(attn_chunks):
         loads.append(
             pltpu.make_async_copy(
@@ -530,30 +879,33 @@
                 sides[side].stage(number, chunk)
         if tick < 5:
             small(tick)
-    for part in range(3):
-        columns = slice(part * half, (part + 1) * half)
-        mine = pl.ds(pl.multiple_of(part * 2 * half + at.head * half, 128), half)
-        mlp_out[:, mine] = summed[pl.ds(pl.multiple_of(at.head * rows, 8), rows), columns]
+    def spread(source, head):
+        offset = 0
+        for columns in mlp_chunks:
+            size = (columns.stop - columns.start) // 3
+            for part in range(3):
+                start = columns.start + part * size
+                target = pl.ds(pl.multiple_of(part * 2 * half + head * half + offset, 128), size)
+                mlp_out[:, target] = source[:, start : start + size]
+            offset += size
+
+    spread(summed.at[pl.ds(pl.multiple_of(at.head * rows, 8), rows)], at.head)
     for chunk, columns in enumerate(mlp_chunks):
         wait(swapped.at[:, columns], 6 + chunk)
-    for part in range(3):
-        columns = slice(part * half, (part + 1) * half)
-        other = pl.ds(pl.multiple_of(part * 2 * half + (1 - at.head) * half, 128), half)
-        mlp_out[:, other] = swapped[:, columns]
+    spread(swapped, 1 - at.head)
     for copy in sent:
         copy.wait_send()
     for side in sides:
         side.finish()
 
 
-def reduce_gradients(mlp, attn, small):
-    rows = mlp.shape[0] // 16
-    half = mlp.shape[1] // 3
-    tiles = mlp.shape[1] // 128
-    mlp_count = 6
-    mlp_chunks = chunk_columns(
-        mlp.shape[1], [tiles // mlp_count + (1 if i < tiles % mlp_count else 0) for i in range(mlp_count)]
-    )
+def reduce_gradients(zero, mlp, attn, small):
+    rows = attn.shape[0] // 16
+    mlp_count = mlp.shape[0] + 1
+    edges = [0] + [zero.shape[-1] + i * mlp.shape[-1] for i in range(mlp_count)]
+    mlp_chunks = [slice(edges[i], edges[i + 1]) for i in range(mlp_count)]
+    width = edges[-1]
+    half = width // 3
     attn_tiles = attn.shape[1] // 128
     attn_count = 4
     attn_chunks = chunk_columns(
@@ -561,17 +913,17 @@
     )
     vmem = pl.BlockSpec(memory_space=pltpu.VMEM)
     buffers = []
-    for width in (mlp.shape[1], attn.shape[1]):
+    for columns in (width, attn.shape[1]):
         buffers += [
-            pltpu.VMEM((2, rows, width), BF16),
-            pltpu.VMEM((2, rows, width), BF16),
-            pltpu.VMEM((4, rows, width), BF16),
-            pltpu.VMEM((4, rows, width), BF16),
-            pltpu.VMEM((3, rows, width), BF16),
+            pltpu.VMEM((2, rows, columns), BF16),
+            pltpu.VMEM((2, rows, columns), BF16),
+            pltpu.VMEM((4, rows, columns), BF16),
+            pltpu.VMEM((4, rows, columns), BF16),
+            pltpu.VMEM((3, rows, columns), BF16),
         ]
     return pl.pallas_call(
         functools.partial(reduce_kernel, half, mlp_chunks, attn_chunks),
-        in_specs=[ANY, ANY, vmem],
+        in_specs=[ANY, ANY, ANY, vmem],
         out_specs=[vmem, vmem, vmem],
         out_shape=[
             jax.ShapeDtypeStruct((rows // 2, 6 * half), F32),
@@ -579,11 +931,11 @@
             jax.ShapeDtypeStruct(small.shape, F32),
         ],
         scratch_shapes=[
-            pltpu.VMEM((4, 4, rows, mlp.shape[1]), BF16),
+            pltpu.VMEM((4, 4, rows, width), BF16),
             pltpu.VMEM((4, 4, rows, attn.shape[1]), BF16),
             *buffers,
-            pltpu.VMEM((rows, mlp.shape[1]), F32),
-            pltpu.VMEM((rows // 2, mlp.shape[1]), F32),
+            pltpu.VMEM((rows, width), F32),
+            pltpu.VMEM((rows // 2, width), F32),
             pltpu.VMEM((3,) + small.shape, F32),
             pltpu.VMEM((6,) + small.shape, F32),
             pltpu.SemaphoreType.DMA((mlp_count + attn_count,)),
@@ -598,7 +950,7 @@
             collective_id=1, has_side_effects=True, vmem_limit_bytes=58 << 20
         ),
         name="reduce_gradients",
-    )(mlp.reshape(4, 4, rows, -1), attn.reshape(4, 4, rows, -1), small)
+    )(zero, mlp, attn.reshape(4, 4, rows, -1), small)
 
 
 def swap(value):
@@ -640,64 +992,73 @@
     square = lax.axis_size("dp") == 16
 
     pieces = w_mlp.reshape(shard_rows, 3, 2, half)
-    own_piece = half_of(pieces, here, 2).reshape(shard_rows, 3 * half)
-    other_piece = half_of(pieces, 1 - here, 2).reshape(shard_rows, 3 * half)
-    if square:
-        weights = gather_weights(own_piece, other_piece)
-    else:
-        weights = lax.all_gather(ordered(own_piece, swap(other_piece), 0), "dp", axis=0, tiled=True)
-
+    own_piece = lax.dynamic_index_in_dim(pieces, here, 2, keepdims=False)
+    other_piece = lax.dynamic_index_in_dim(pieces, 1 - here, 2, keepdims=False)
     tokens_own = tokens[0]
-    tokens_wide = ordered(tokens_own, swap(tokens_own), 0).astype(F32)
-    length = tokens_wide.shape[0]
-    scale_one = lax.rsqrt(jnp.mean(tokens_wide * tokens_wide, axis=1, keepdims=True) + EPSILON)
-    h_low = (tokens_wide * scale_one * norm_attn_gain).astype(BF16)
-    query = dot(h_low, w_query).astype(BF16)
-    key = dot(h_low, w_key).astype(BF16)
-    value = dot(h_low, w_value).astype(BF16)
-    gate = dot(h_low, w_gate_out)
-    low_rank = dot(h_low, w_low_in)
-    low_high, low_rest = split_low(low_rank)
-    logits = dot(low_high, w_low_out) + dot(low_rest, w_low_out) + decay_bias
-    attended, mixed, states = attention_forward(query, key, value, logits, gate, out_gain, initial_memory[0])
-    resid = tokens_own.astype(F32) + sum_rows(dot(mixed, w_out), here)
-
     positions = here * own_rows + lax.iota(jnp.int32, own_rows)
     row_mask = (positions < lengths[0]).astype(F32)[:, None]
-    scale_two = lax.rsqrt(jnp.mean(resid * resid, axis=1, keepdims=True) + EPSILON)
-    normal_two = resid * scale_two
-    h_two_own = (normal_two * norm_mlp_gain).astype(BF16)
-    h_two = ordered(h_two_own, swap(h_two_own), 0)
     resid_grad = row_mask * cotangent[0].astype(F32)
     low_own = resid_grad.astype(BF16)
-    resid_low = ordered(low_own, swap(low_own), 0)
-    pre_gate = dot(h_two, weights[:, :half])
-    up_part = dot(h_two, weights[:, half : 2 * half])
-    pre_sigmoid = sigmoid(pre_gate)
-    inner = (pre_gate * pre_sigmoid * up_part).astype(BF16)
-    inner_grad = dot(resid_low, weights[:, 2 * half :])
-    pre_grad = (
-        inner_grad * up_part * pre_sigmoid * (1.0 + pre_gate * (1.0 - pre_sigmoid))
-    ).astype(BF16)
-    up_grad = (inner_grad * pre_gate * pre_sigmoid).astype(BF16)
-    mlp_out = sum_rows(dot(inner, weights[:, 2 * half :], 1, 1), here)
-    output = (row_mask * (resid + mlp_out)).astype(BF16)[None]
-    h_two_grad = sum_rows(
-        dot(pre_grad, weights[:, :half], 1, 1) + dot(up_grad, weights[:, half : 2 * half], 1, 1), here
-    )
-    grad_mlp = jnp.concatenate(
-        [
-            dot(h_two, pre_grad, 0, 0).astype(BF16),
-            dot(h_two, up_grad, 0, 0).astype(BF16),
-            dot(resid_low, inner, 0, 0).astype(BF16),
-        ],
-        axis=1,
-    )
-    resid_total = resid_grad + norm_backward(h_two_grad, norm_mlp_gain, normal_two, scale_two)
-    gain_two_grad = jnp.sum(h_two_grad * normal_two, axis=0)
-
-    attn_own = resid_total.astype(BF16)
-    attn_low = ordered(attn_own, swap(attn_own), 0)
+    if square:
+        (
+            h_low, query, key, value, gate, logits, low_rank, attended, mixed, states,
+            grad_zero, grad_mlp, output, resid_total, attn_low, gain_two_grad,
+        ) = layer(
+            tokens_own, low_own, row_mask, norm_attn_gain, norm_mlp_gain, out_gain, decay_bias, initial_memory[0],
+            w_query, w_key, w_value, w_gate_out, w_low_in, w_low_out, w_out, own_piece, other_piece,
+        )
+        low_high, low_rest = split_low(low_rank)
+        output, gain_two_grad = output[None], gain_two_grad[0]
+    else:
+        pair = swap(other_piece.reshape(shard_rows, 3 * half))
+        weights = lax.all_gather(
+            ordered(own_piece.reshape(shard_rows, 3 * half), pair, 0), "dp", axis=0, tiled=True
+        )
+        tokens_wide = ordered(tokens_own, swap(tokens_own), 0).astype(F32)
+        length = tokens_wide.shape[0]
+        scale_one = lax.rsqrt(jnp.mean(tokens_wide * tokens_wide, axis=1, keepdims=True) + EPSILON)
+        h_low = (tokens_wide * scale_one * norm_attn_gain).astype(BF16)
+        query = dot(h_low, w_query).astype(BF16)
+        key = dot(h_low, w_key).astype(BF16)
+        value = dot(h_low, w_value).astype(BF16)
+        gate = dot(h_low, w_gate_out)
+        low_rank = dot(h_low, w_low_in)
+        low_high, low_rest = split_low(low_rank)
+        logits = dot(low_high, w_low_out) + dot(low_rest, w_low_out) + decay_bias
+        attended, mixed, states = attention_forward(query, key, value, logits, gate, out_gain, initial_memory[0])
+        resid = tokens_own.astype(F32) + sum_rows(dot(mixed, w_out), here)
+        scale_two = lax.rsqrt(jnp.mean(resid * resid, axis=1, keepdims=True) + EPSILON)
+        normal_two = resid * scale_two
+        h_two_own = (normal_two * norm_mlp_gain).astype(BF16)
+        h_two = ordered(h_two_own, swap(h_two_own), 0)
+        resid_low = ordered(low_own, swap(low_own), 0)
+        pre_gate = dot(h_two, weights[:, :half])
+        up_part = dot(h_two, weights[:, half : 2 * half])
+        pre_sigmoid = sigmoid(pre_gate)
+        inner = (pre_gate * pre_sigmoid * up_part).astype(BF16)
+        inner_grad = dot(resid_low, weights[:, 2 * half :])
+        pre_grad = (
+            inner_grad * up_part * pre_sigmoid * (1.0 + pre_gate * (1.0 - pre_sigmoid))
+        ).astype(BF16)
+        up_grad = (inner_grad * pre_gate * pre_sigmoid).astype(BF16)
+        mlp_out = sum_rows(dot(inner, weights[:, 2 * half :], 1, 1), here)
+        output = (row_mask * (resid + mlp_out)).astype(BF16)[None]
+        h_two_grad = sum_rows(
+            dot(pre_grad, weights[:, :half], 1, 1) + dot(up_grad, weights[:, half : 2 * half], 1, 1), here
+        )
+        grad_mlp = jnp.concatenate(
+            [
+                dot(h_two, pre_grad, 0, 0).astype(BF16),
+                dot(h_two, up_grad, 0, 0).astype(BF16),
+                dot(resid_low, inner, 0, 0).astype(BF16),
+            ],
+            axis=1,
+        )
+        resid_total = resid_grad + norm_backward(h_two_grad, norm_mlp_gain, normal_two, scale_two)
+        gain_two_grad = jnp.sum(h_two_grad * normal_two, axis=0)
+        attn_own = resid_total.astype(BF16)
+        attn_low = ordered(attn_own, swap(attn_own), 0)
+
     mixed_grad = dot(attn_low, w_out, 1, 1)
     out_grad = dot(attn_low, mixed, 0, 0)
     query_grad, key_grad, value_grad, gate_grad, logits_grad, out_gain_grad = attention_backward(
@@ -745,7 +1106,7 @@
     )
     if square:
         packed = packed.reshape(-1, 128)
-        grad_mlp, attn_grads, packed = reduce_gradients(grad_mlp, attn_grads, packed)
+        grad_mlp, attn_grads, packed = reduce_gradients(grad_zero, grad_mlp, attn_grads, packed)
         packed = packed.reshape(-1)
     else:
         packed = lax.psum(packed, ("dp", "head"))

time: 410 us -> 355 us (0.87); the launches traced: 404 us -> 354 us
  matrix products: 76.4 us -> 40.5 us
  other arithmetic: 32.5 us -> 9.18 us
  Pallas kernels: 252 us -> 268 us
    dot_general x34 -> x17, matrix products: 76.4 us -> 40.5 us  [dot(): lax.dot_general(left, right, (((left_dim,), (right_dim,)), ((), ())), pre...]
    pallas_call x2 -> x1, Pallas kernels: 108 us -> 127 us  [layer(): pl.pallas_call(functools.partial(layer_kernel, count), grid=(steps,), in_...]
    concatenate x4 -> x0, other arithmetic: 14.7 us -> none  [the longest x3 10.9 us: ordered(): joined = jnp.concatenate([own, other, own], axis=axis)]
    reduce_sum x3 -> x1, other arithmetic: 6.06 us -> 0.28 us  [per_device(): jnp.mean(own_wide * own_wide, axis=1, keepdims=True) + EPSILON]
    unnamed x116 -> x58, local copies, waits for them, and re-layouts: 12 us -> 9.11 us
  transfers between devices with their start and end apart: 8 -> 1, of which waited for: 1 -> 0; matrix products, arithmetic and copies ran while one was open for 13% -> 7% of each run, Pallas kernels for 25% -> 0%
where the time goes in v3:
time: 355 us; the launch traced here: 354 us
  Pallas kernels  268 us (75%)
  matrix products  40.5 us (11%)
  local copies, waits for them, and re-layouts  34.5 us (10%)
  other arithmetic  9.18 us (3%)
    pallas_call x1, Pallas kernels, reduce_gradients(): pl.pallas_call(functools.partial(reduce_kernel, half, mlp_chunks, attn_ch...  129 us
    pallas_call x1, Pallas kernels, layer(): pl.pallas_call(functools.partial(layer_kernel, count), grid=(steps,), in_...  127 us
    dot_general x17, matrix products, dot(): lax.dot_general(left, right, (((left_dim,), (right_dim,)), ((), ())), pre...  40.5 us
    pallas_call x1, Pallas kernels, attention_backward(): pl.pallas_call(backward_kernel, grid=(steps,), in_specs=[rows(values), ro...  11.7 us
    unnamed x58, local copies, waits for them, and re-layouts  9.11 us
  transfers between devices with their start and end apart: 1, of which 0 were waited for; matrix products, arithmetic and copies ran while one was open for 7% of the time, Pallas kernels for 0%

profile of v3, /device:TPU:0, one launch (start us, length us, event | category | flops | bytes accessed | tf_op | source)
XLA Modules:
  0.0 353.8 jit_solution(7089068107618240958)
XLA Ops:
  0.7 1.2 reshape.127
  1.9 1.1 constant_dynamic-slice_fusion.1
  7.1 1.0 reshape.130.pieces
  9.6 1.2 fusion.10.low_ref
  10.8 127.0 %layer.1 = (bf16[1024,1024]{1,0:T(8,128)(2,1)}, bf16[1024,256]{1,0:T(8,128)(2,1)}, bf16[1024,256]{1,0:T(8,128)(2,1)}, bf16[1024,512]{1,0:T(8,128)(2,1)}, f32[102...) custom-call(bf16[512,1024]{1,0:T(8,128)(2,1)} %bitcast.88, ...), custom_call_target="tpu_custom_call" | custom-call | tf_op jit(solution)/shard_map/layer/pallas_call | solution.py:682
  137.8 4.5 %fusion.31.mixed_grad_ref = f32[1024,512]{1,0:T(8,128)} fusion(bf16[1024,1024]{1,0:T(8,128)(2,1)} %get-tuple-element.41, bf16[512,1024]{1,0:T(8,128)(2,1)} %w_out.1), kind=kOutput, calls=%fused_computation.71 | convolution fusion | flops 1073741824 | bytes 5242880 | tf_op jit(solution)/shard_map/dot_general | solution.py:24
  142.4 11.7 %attention_backward.1 = (bf16[1024,256]{1,0:T(8,128)(2,1)S(1)}, bf16[1024,256]{1,0:T(8,128)(2,1)S(1)}, bf16[1024,512]{1,0:T(8,128)(2,1)S(1)}, bf16[1024,512]{1,0...) custom-call(f32[1024,512]{1,0:T(8,128)} %fusion.31.mixed_grad_ref, bf16[1024,256]{1,0:T(8,128)(2,1)S(1)} %copy-done, ...), custom_call_target="tpu_custom_call" | custom-call | tf_op jit(solution)/shard_map/attention_backward/pallas_call | solution.py:236
  154.6 1.1 copy-done.16
  155.7 3.3 fusion.35
  159.0 3.2 fusion.34
  162.2 2.7 fusion.33
  164.9 2.7 fusion.32
  167.6 6.8 %add_add_fusion = f32[1024,1024]{1,0:T(8,128)S(1)} fusion(f32[1024,1024]{1,0:T(8,128)} %fusion.35, f32[1024,1024]{1,0:T(8,128)} %fusion.34, f32[1024,1024]{1,0:T(8,128)} %fusion.32, f32[1024,1024]{1,0:T(8,128)} %fusion.33, bf16[1024,16]{0,1:T(8,128)(2,1)S(1)} %fusion.16, bf16[1024,16]{0,1:T(8,128)(2,1)S(1)} %copy-done.18), kind=kOutput, calls=%fused_computation | convolution fusion | flops 37748736 | bytes 21037056 | tf_op jit(solution)/shard_map/dot_general | solution.py:24
  174.4 2.0 copy-done.5
  176.4 1.1 dynamic-slice_convert_fusion
  177.6 3.3 fusion.36
  180.8 1.5 fusion.14
  182.5 1.3 fusion.22
  184.3 1.2 reshape.136
  185.6 3.3 fusion.15
  188.9 2.3 fusion.13
  191.2 2.3 fusion.12
  193.5 2.3 fusion.11
  195.8 6.6 %copy.59 = bf16[1024,2048]{1,0:T(8,128)(2,1)} copy(bf16[1024,2048]{0,1:T(8,128)(2,1)} %fusion.11) | data formatting | bytes 8388608 | tf_op jit(solution)/shard_map/concatenate | solution.py:1074
  202.7 2.8 fusion.8
  206.2 129.3 %reduce_gradients.1 = (f32[32,8448]{1,0:T(8,128)}, f32[64,2048]{1,0:T(8,128)}, f32[214,128]{1,0:T(8,128)}) custom-call(bf16[4,4,64,384]{3,2,1,0:T(8,128)(2,1)} %get-tuple-element.54.zero_ref, bf16[5,4,4,64,768]{4,3,2,1,0:T(8,128)(2,1)} %get-tuple-element.55.mlp_ref, bf16[4,4,64,2048]{3,2,1,0:T(8,128)(2,1)} %bitcast.89, f32[214,128]{1,0:T(8,128)} %bitcast.94), custom_call_target="tpu_custom_call" | custom-call | tf_op jit(solution)/shard_map/reduce_gradients/pallas_call | solution.py:924
  335.6 1.4 slice_bitcast_fusion.5
  336.9 1.3 slice_bitcast_fusion.3
  339.9 1.5 fusion.30
  341.4 1.8 slice_bitcast_fusion
  345.4 1.8 copy.61
  347.2 4.0 %fusion.7 = f32[1,512,1024]{2,1,0:T(8,128)} fusion(f32[512,1024]{1,0:T(8,128)S(1)} %copy-done.8, f32[512]{0:T(512)S(1)} %broadcast_multiply_fusion, f32[1024]{0:T(1024)S(1)} %copy-done.21, f32[512]{0:T(512)S(1)} %add_rsqrt_fusion, bf16[512,1024]{1,0:T(8,128)(2,1)} %collective-permute-done, f32[1024,1024]{1,0:T(8,128)} %copy-done.5, s32[]{:T(128)S(6)} %select_n.18, ...), kind=kLoop, calls=%fused_computation.10 | loop fusion | flops 4718592 | bytes 8396804 | tf_op jit(solution)/shard_map/broadcast_in_dim | solution.py:1128
  (87 shorter events, 13.5 us)
Async XLA Ops:
  1.8 3.9 %copy-start.18 = (bf16[1024,16]{0,1:T(8,128)(2,1)S(1)}, bf16[1024,16]{0,1:T(8,128)(2,1)}, u32[]{:S(2)}) copy-start(bf16[1024,16]{0,1:T(8,128)(2,1)} %param.24) | copy-start | bytes 98308
  5.7 3.9 %copy-start.14 = (bf16[1,512,1024]{2,1,0:T(8,128)(2,1)S(1)}, bf16[1,512,1024]{2,1,0:T(8,128)(2,1)}, u32[]{:S(2)}) copy-start(bf16[1,512,1024]{2,1,0:T(8,128)(2,1)} %param.31) | copy-start | bytes 3145732
  137.8 4.6 %copy-start = (bf16[1024,256]{1,0:T(8,128)(2,1)S(1)}, bf16[1024,256]{1,0:T(8,128)(2,1)}, u32[]{:S(2)}) copy-start(bf16[1024,256]{1,0:T(8,128)(2,1)} %get-tuple-element.42.query_ref) | copy-start | bytes 1572868
  137.8 4.6 %copy-start.1 = (bf16[1024,256]{1,0:T(8,128)(2,1)S(1)}, bf16[1024,256]{1,0:T(8,128)(2,1)}, u32[]{:S(2)}) copy-start(bf16[1024,256]{1,0:T(8,128)(2,1)} %get-tuple-element.43.key_ref) | copy-start | bytes 1572868
  137.8 4.6 %copy-start.2 = (f32[256]{0:T(256)S(1)}, f32[256]{0:T(256)}, u32[]{:S(2)}) copy-start(f32[256]{0:T(256)} %param.27) | copy-start | bytes 3076
  142.3 11.8 %copy-start.20 = (bf16[16,256]{1,0:T(8,128)(2,1)S(1)}, bf16[16,256]{1,0:T(8,128)(2,1)}, u32[]{:S(2)}) copy-start(bf16[16,256]{1,0:T(8,128)(2,1)} %w_low_out.1) | copy-start | bytes 24580
  154.1 4.9 %copy-start.3 = (bf16[1024,512]{1,0:T(8,128)(2,1)}, bf16[1024,512]{1,0:T(8,128)(2,1)S(1)}, u32[]{:S(2)}) copy-start(bf16[1024,512]{1,0:T(8,128)(2,1)S(1)} %get-tuple-element.51) | copy-start | bytes 3145732
  154.1 1.6 copy-start.16
  155.7 3.3 copy-start.17
  159.0 3.2 copy-start.9
  162.2 2.7 copy-start.10
  174.4 2.0 copy-start.5
  177.6 25.2 %collective-permute-start = (bf16[512,1024]{1,0:T(8,128)(2,1)}, bf16[512,1024]{1,0:T(8,128)(2,1)}, u32[]{:S(2)}, u32[]{:S(2)}) collective-permute-start(bf16[512,1024]{1,0:T(8,128)(2,1)} %dynamic-slice_convert_fusion), channel_id=1, source_target_pairs={{0,1},{1,0},{2,3},{3,2},{4,5},{5,4},{6,7},{7,6},{8,9},{9,8},{10,11... | collective-permute-start | bytes 3145736 | tf_op jit(solution)/shard_map/ppermute | solution.py:957
  177.6 3.3 copy-start.11
  182.4 1.4 copy-start.7
  185.6 3.3 copy-start.4
  185.6 3.3 copy-start.12
  191.2 2.3 copy-start.23
  191.2 2.3 copy-start.24
  195.8 6.6 %copy-start.6 = (bf16[1,512,1024]{2,1,0:T(8,128)(2,1)S(1)}, bf16[1,512,1024]{2,1,0:T(8,128)(2,1)}, u32[]{:S(2)}) copy-start(bf16[1,512,1024]{2,1,0:T(8,128)(2,1)} %param.16) | copy-start | bytes 3145732
  195.8 6.9 %copy-start.21 = (f32[1024]{0:T(1024)S(1)}, f32[1024]{0:T(1024)}, u32[]{:S(2)}) copy-start(f32[1024]{0:T(1024)} %param.19) | copy-start | bytes 12292
  202.7 2.8 copy-start.22
  205.6 0.6 copy-start.19
  335.5 11.7 %copy-start.8 = (f32[512,1024]{1,0:T(8,128)S(1)}, f32[512,1024]{1,0:T(8,128)}, u32[]{:S(2)}) copy-start(f32[512,1024]{1,0:T(8,128)} %get-tuple-element.40) | copy-start | bytes 6291460
  347.2 4.0 %copy-start.15 = (bf16[512,1024]{1,0:T(8,128)(2,1)S(1)}, bf16[512,1024]{1,0:T(8,128)(2,1)}, u32[]{:S(2)}) copy-start(bf16[512,1024]{1,0:T(8,128)(2,1)} %get-tuple-element.39) | copy-start | bytes 3145732
  351.2 1.6 copy-start.13

commit v4 on v3

--- a/solution.py
+++ b/solution.py
@@ -64,38 +64,48 @@
     return jnp.concatenate([column] * (width // KEY_HEAD), axis=1)
 
 
+def forward_block(query, key, value, logits, gate, gain, memory, states):
+    rise, fall, early, late, decay = decay_terms(logits)
+    lower = triangle(True)
+    attended_parts = []
+    mixed_parts = []
+    for head in range(memory.shape[0]):
+        keys_at = slice(head * KEY_HEAD, (head + 1) * KEY_HEAD)
+        values_at = slice(head * VALUE_HEAD, (head + 1) * VALUE_HEAD)
+        query_wide = query[:, keys_at].astype(F32)
+        key_wide = key[:, keys_at].astype(F32)
+        value_head = value[:, values_at]
+        state = memory[head]
+        state_low = state.astype(BF16)
+        states[head] = state_low
+        scores = dot(
+            (query_wide * rise[:, keys_at]).astype(BF16), (key_wide * fall[:, keys_at]).astype(BF16), 1, 1
+        )
+        scores = jnp.where(lower, scores, 0.0).astype(BF16)
+        left = jnp.concatenate([scores, (query_wide * early[:, keys_at]).astype(BF16)], axis=1)
+        attended = dot(left, jnp.concatenate([value_head, state_low], axis=0))
+        memory[head] = as_column(decay[:, keys_at], VALUE_HEAD) * state + dot(
+            (key_wide * late[:, keys_at]).astype(BF16), value_head, 0, 0
+        )
+        scale = lax.rsqrt(jnp.mean(attended * attended, axis=1, keepdims=True) + EPSILON)
+        gate_head = gate[:, values_at]
+        attended_parts.append(attended)
+        mixed_parts.append((attended * scale * gain * gate_head * sigmoid(gate_head)).astype(BF16))
+    return jnp.concatenate(attended_parts, axis=1), jnp.concatenate(mixed_parts, axis=1)
+
+
 def forward_kernel(
     query_ref, key_ref, value_ref, logits_ref, gate_ref, gain_ref, start_ref,
     attended_ref, mixed_ref, states_ref, memory
 ):
-    heads = start_ref.shape[0]
-
     @pl.when(pl.program_id(0) == 0)
     def _():
         memory[...] = start_ref[...]
 
-    rise, fall, early, late, decay = decay_terms(logits_ref[...])
-    lower = triangle(True)
-    for head in range(heads):
-        keys_at = slice(head * KEY_HEAD, (head + 1) * KEY_HEAD)
-        values_at = slice(head * VALUE_HEAD, (head + 1) * VALUE_HEAD)
-        query = query_ref[:, keys_at].astype(F32)
-        key = key_ref[:, keys_at].astype(F32)
-        value = value_ref[:, values_at]
-        state = memory[head]
-        state_low = state.astype(BF16)
-        states_ref[0, head] = state_low
-        scores = dot((query * rise[:, keys_at]).astype(BF16), (key * fall[:, keys_at]).astype(BF16), 1, 1)
-        scores = jnp.where(lower, scores, 0.0).astype(BF16)
-        left = jnp.concatenate([scores, (query * early[:, keys_at]).astype(BF16)], axis=1)
-        attended = dot(left, jnp.concatenate([value, state_low], axis=0))
-        memory[head] = as_column(decay[:, keys_at], VALUE_HEAD) * state + dot(
-            (key * late[:, keys_at]).astype(BF16), value, 0, 0
-        )
-        attended_ref[:, values_at] = attended
-        scale = lax.rsqrt(jnp.mean(attended * attended, axis=1, keepdims=True) + EPSILON)
-        gate = gate_ref[:, values_at]
-        mixed_ref[:, values_at] = (attended * scale * gain_ref[...] * gate * sigmoid(gate)).astype(BF16)
+    attended_ref[...], mixed_ref[...] = forward_block(
+        query_ref[...], key_ref[...], value_ref[...], logits_ref[...], gate_ref[...], gain_ref[...],
+        memory, states_ref.at[0],
+    )
 
 
 def attention_forward(query, key, value, logits, gate, gain, start):
@@ -130,80 +140,63 @@
     )(query, key, value, logits, gate, gain.reshape(1, -1), start)
 
 
-def backward_kernel(
-    mixed_grad_ref, query_ref, key_ref, value_ref, logits_ref, gate_ref, attended_ref, states_ref, gain_ref,
-    query_grad_ref, key_grad_ref, value_grad_ref, gate_grad_ref, logits_grad_ref, gain_grad_ref, memory_grad
-):
-    heads = memory_grad.shape[0]
-
-    @pl.when(pl.program_id(0) == 0)
-    def _():
-        memory_grad[...] = jnp.zeros_like(memory_grad)
-        gain_grad_ref[...] = jnp.zeros_like(gain_grad_ref)
-
-    logits = logits_ref[...]
+def backward_block(mixed_grad, query, key, value, logits, gate, attended, states, gain, memory_grad):
     rise, fall, early, late, decay = decay_terms(logits)
     lower = triangle(True)
     upper = triangle(False)
     last = lax.broadcasted_iota(jnp.int32, (BLOCK, KEY_HEAD), 0) == BLOCK - 1
-    total_grads = []
+    query_grads, key_grads, value_grads, gate_grads, total_grads = [], [], [], [], []
     gain_grad = jnp.zeros((1, VALUE_HEAD), F32)
-    for head in range(heads):
+    for head in range(memory_grad.shape[0]):
         keys_at = slice(head * KEY_HEAD, (head + 1) * KEY_HEAD)
         values_at = slice(head * VALUE_HEAD, (head + 1) * VALUE_HEAD)
-        attended = attended_ref[:, values_at]
-        scale = lax.rsqrt(jnp.mean(attended * attended, axis=1, keepdims=True) + EPSILON)
-        normal = attended * scale
-        gain = gain_ref[...]
-        gate = gate_ref[:, values_at]
-        gate_sigmoid = sigmoid(gate)
-        mixed_grad = mixed_grad_ref[:, values_at]
-        gate_grad_ref[:, values_at] = (
-            mixed_grad * normal * gain * gate_sigmoid * (1.0 + gate * (1.0 - gate_sigmoid))
-        ).astype(BF16)
-        normed_grad = mixed_grad * gate * gate_sigmoid
+        attended_head = attended[:, values_at]
+        scale = lax.rsqrt(jnp.mean(attended_head * attended_head, axis=1, keepdims=True) + EPSILON)
+        normal = attended_head * scale
+        gate_head = gate[:, values_at]
+        gate_sigmoid = sigmoid(gate_head)
+        mixed_head = mixed_grad[:, values_at]
+        gate_grads.append(
+            (mixed_head * normal * gain * gate_sigmoid * (1.0 + gate_head * (1.0 - gate_sigmoid))).astype(BF16)
+        )
+        normed_grad = mixed_head * gate_head * gate_sigmoid
         gain_grad += jnp.sum(normed_grad * normal, axis=0, keepdims=True)
         scaled = normed_grad * gain
         attended_grad = (
             scale * (scaled - normal * jnp.mean(scaled * normal, axis=1, keepdims=True))
         ).astype(BF16)
 
-        query = query_ref[:, keys_at].astype(F32)
-        key = key_ref[:, keys_at].astype(F32)
-        value = value_ref[:, values_at]
-        query_middle = query * rise[:, keys_at]
-        key_middle = key * fall[:, keys_at]
-        query_early = query * early[:, keys_at]
-        key_late = key * late[:, keys_at]
+        query_wide = query[:, keys_at].astype(F32)
+        key_wide = key[:, keys_at].astype(F32)
+        value_head = value[:, values_at]
+        query_middle = query_wide * rise[:, keys_at]
+        key_middle = key_wide * fall[:, keys_at]
+        query_early = query_wide * early[:, keys_at]
+        key_late = key_wide * late[:, keys_at]
         query_middle_low = query_middle.astype(BF16)
         key_middle_low = key_middle.astype(BF16)
-        state = states_ref[0, head]
+        state = states[head]
         after = memory_grad[head]
-        after_low = after.astype(BF16)
 
         scores_turned = jnp.where(upper, dot(key_middle_low, query_middle_low, 1, 1), 0.0).astype(BF16)
-        from_values = dot(attended_grad, jnp.concatenate([value, state], axis=0), 1, 1)
-        to_values = jnp.concatenate([attended_grad, after_low], axis=0)
-        from_grads = dot(value, to_values, 1, 1)
+        from_values = dot(attended_grad, jnp.concatenate([value_head, state], axis=0), 1, 1)
+        to_values = jnp.concatenate([attended_grad, after.astype(BF16)], axis=0)
+        from_grads = dot(value_head, to_values, 1, 1)
         scores_grad = jnp.where(lower, from_values[:, :BLOCK], 0.0).astype(BF16)
         scores_grad_turned = jnp.where(upper, from_grads[:, :BLOCK], 0.0).astype(BF16)
         query_early_grad = from_values[:, BLOCK:]
         key_late_grad = from_grads[:, BLOCK:]
         query_middle_grad = dot(scores_grad, key_middle_low)
         key_middle_grad = dot(scores_grad_turned, query_middle_low)
-        value_grad_ref[:, values_at] = dot(
-            jnp.concatenate([scores_turned, key_late.astype(BF16)], axis=1), to_values
-        ).astype(BF16)
-        decay_column = as_column(decay[:, keys_at], VALUE_HEAD)
-        carried = decay_column * after
+        value_grads.append(
+            dot(jnp.concatenate([scores_turned, key_late.astype(BF16)], axis=1), to_values).astype(BF16)
+        )
+        carried = as_column(decay[:, keys_at], VALUE_HEAD) * after
         memory_grad[head] = carried + dot(query_early.astype(BF16), attended_grad, 0, 0)
-
-        query_grad_ref[:, keys_at] = (
-            query_early_grad * early[:, keys_at] + query_middle_grad * rise[:, keys_at]
-        ).astype(BF16)
-        key_grad_ref[:, keys_at] = (
-            key_middle_grad * fall[:, keys_at] + key_late_grad * late[:, keys_at]
-        ).astype(BF16)
+        query_grads.append(
+            (query_early_grad * early[:, keys_at] + query_middle_grad * rise[:, keys_at]).astype(BF16)
+        )
+        key_grads.append((key_middle_grad * fall[:, keys_at] + key_late_grad * late[:, keys_at]).astype(BF16))
         late_part = key_late_grad * key_late
         end_high, end_low = split_low(carried * state.astype(F32))
         ones = jnp.ones((8, VALUE_HEAD), BF16)
@@ -217,11 +210,32 @@
             - late_part
             + jnp.where(last, end_grad, 0.0)
         )
+    ones = jnp.where(upper, 1.0, 0.0).astype(BF16)
+    high, rest = split_low(jnp.concatenate(total_grads, axis=1))
+    logits_grad = (dot(ones, high) + dot(ones, rest)) * sigmoid(-logits) * (1.0 / 16.0)
+    grads = query_grads + key_grads + value_grads + gate_grads
+    return jnp.concatenate(grads, axis=1), logits_grad, gain_grad
+
+
+def backward_kernel_plain(
+    mixed_grad_ref, query_ref, key_ref, value_ref, logits_ref, gate_ref, attended_ref, states_ref, gain_ref,
+    query_grad_ref, key_grad_ref, value_grad_ref, gate_grad_ref, logits_grad_ref, gain_grad_ref, memory_grad
+):
+    @pl.when(pl.program_id(0) == 0)
+    def _():
+        memory_grad[...] = jnp.zeros_like(memory_grad)
+        gain_grad_ref[...] = jnp.zeros_like(gain_grad_ref)
+
+    grads, logits_grad, gain_grad = backward_block(
+        mixed_grad_ref[...], query_ref[...], key_ref[...], value_ref[...], logits_ref[...], gate_ref[...],
+        attended_ref[...], states_ref[0], gain_ref[...], memory_grad,
+    )
+    start = 0
+    for ref in (query_grad_ref, key_grad_ref, value_grad_ref, gate_grad_ref):
+        ref[...] = grads[:, start : start + ref.shape[1]]
+        start += ref.shape[1]
+    logits_grad_ref[...] = logits_grad
     gain_grad_ref[...] += gain_grad
-    ones = jnp.where(upper, 1.0, 0.0).astype(BF16)
-    high, low = split_low(jnp.concatenate(total_grads, axis=1))
-    decay_grad = dot(ones, high) + dot(ones, low)
-    logits_grad_ref[...] = decay_grad * sigmoid(-logits) * (1.0 / 16.0)
 
 
 def attention_backward(mixed_grad, query, key, value, logits, gate, attended, states, gain):
@@ -234,7 +248,7 @@
         return pl.BlockSpec((BLOCK, width), lambda i: (steps - 1 - i, 0))
 
     return pl.pallas_call(
-        backward_kernel,
+        backward_kernel_plain,
         grid=(steps,),
         in_specs=[
             rows(values), rows(keys), rows(keys), rows(values), rows(keys), rows(values), rows(values),
@@ -375,36 +389,6 @@
     pltpu.make_async_remote_copy(
         src_ref=source, dst_ref=source, send_sem=out_sem, recv_sem=in_sem, device_id=device, device_id_type=MESH
     ).wait_send()
-
-
-def forward_block(query, key, value, logits, gate, gain, memory, states):
-    rise, fall, early, late, decay = decay_terms(logits)
-    lower = triangle(True)
-    attended_parts = []
-    mixed_parts = []
-    for head in range(memory.shape[0]):
-        keys_at = slice(head * KEY_HEAD, (head + 1) * KEY_HEAD)
-        values_at = slice(head * VALUE_HEAD, (head + 1) * VALUE_HEAD)
-        query_wide = query[:, keys_at].astype(F32)
-        key_wide = key[:, keys_at].astype(F32)
-        value_head = value[:, values_at]
-        state = memory[head]
-        state_low = state.astype(BF16)
-        states[head] = state_low
-        scores = dot(
-            (query_wide * rise[:, keys_at]).astype(BF16), (key_wide * fall[:, keys_at]).astype(BF16), 1, 1
-        )
-        scores = jnp.where(lower, scores, 0.0).astype(BF16)
-        left = jnp.concatenate([scores, (query_wide * early[:, keys_at]).astype(BF16)], axis=1)
-        attended = dot(left, jnp.concatenate([value_head, state_low], axis=0))
-        memory[head] = as_column(decay[:, keys_at], VALUE_HEAD) * state + dot(
-            (key_wide * late[:, keys_at]).astype(BF16), value_head, 0, 0
-        )
-        scale = lax.rsqrt(jnp.mean(attended * attended, axis=1, keepdims=True) + EPSILON)
-        gate_head = gate[:, values_at]
-        attended_parts.append(attended)
-        mixed_parts.append((attended * scale * gain * gate_head * sigmoid(gate_head)).astype(BF16))
-    return jnp.concatenate(attended_parts, axis=1), jnp.concatenate(mixed_parts, axis=1)
 
 
 def layer_kernel(
@@ -748,13 +732,12 @@
         self.place, self.partial, self.chunks = place, partial, chunks
         self.via_x, self.via_y, self.from_x, self.from_y, self.from_z = via_x, via_y, from_x, from_y, from_z
         self.out_sems, self.in_sems = out_sems, in_sems
-        self.sent = []
-
-    def put(self, source, target, index, device):
-        self.sent.append(send(source, target, self.out_sems.at[index], self.in_sems.at[index], device))
-
-    def wait(self, target, index):
-        arrived(target, self.out_sems.at[index], self.in_sems.at[index], self.place.sibling)
+
+    def put(self, source, target, chunk, slot, device):
+        send(source, target, self.out_sems.at[chunk, slot], self.in_sems.at[chunk, slot], device)
+
+    def wait(self, target, chunk, slot):
+        arrived(target, self.out_sems.at[chunk, slot], self.in_sems.at[chunk, slot], self.place.sibling)
 
     def stage(self, number, chunk):
         at, partial, columns = self.place, self.partial, self.chunks[chunk]
@@ -762,20 +745,24 @@
         low, high = pl.ds(0, 2), pl.ds(2, 2)
         view = (everything, everything, columns)
         if number == 0:
-            self.put(partial.at[low, at.flat_xy, everything, columns], self.via_x.at[view], (chunk, 0), at.beside_x)
-            self.put(partial.at[high, at.flat_xy, everything, columns], self.via_y.at[view], (chunk, 1), at.beside_y)
+            self.put(partial.at[low, at.flat_xy, everything, columns], self.via_x.at[view], chunk, 0, at.beside_x)
+            self.put(partial.at[high, at.flat_xy, everything, columns], self.via_y.at[view], chunk, 1, at.beside_y)
         if number == 1:
-            self.wait(self.via_x.at[view], (chunk, 0))
+            self.wait(self.via_x.at[view], chunk, 0)
             block = (low, at.flat_y, everything, columns)
             partial[block] = (partial[block].astype(F32) + self.via_x[view].astype(F32)).astype(BF16)
-            self.put(partial.at[everything, at.flat_y, everything, columns], self.from_y.at[view], (chunk, 2), at.beside_y)
-            self.wait(self.via_y.at[view], (chunk, 1))
+            self.put(
+                partial.at[everything, at.flat_y, everything, columns], self.from_y.at[view], chunk, 2, at.beside_y
+            )
+            self.wait(self.via_y.at[view], chunk, 1)
             block = (high, at.flat_x, everything, columns)
             partial[block] = (partial[block].astype(F32) + self.via_y[view].astype(F32)).astype(BF16)
-            self.put(partial.at[everything, at.flat_x, everything, columns], self.from_x.at[view], (chunk, 3), at.beside_x)
+            self.put(
+                partial.at[everything, at.flat_x, everything, columns], self.from_x.at[view], chunk, 3, at.beside_x
+            )
         if number == 2:
-            self.wait(self.from_y.at[view], (chunk, 2))
-            self.wait(self.from_x.at[view], (chunk, 3))
+            self.wait(self.from_y.at[view], chunk, 2)
+            self.wait(self.from_x.at[view], chunk, 3)
             block = (everything, at.flat, everything, columns)
             partial[block] = (
                 partial[block].astype(F32) + self.from_x[view].astype(F32) + self.from_y[view].astype(F32)
@@ -784,7 +771,8 @@
                 self.put(
                     partial.at[(at.z + 1 + i) % 4, at.flat, everything, columns],
                     self.from_z.at[i, everything, columns],
-                    (chunk, 4 + i),
+                    chunk,
+                    4 + i,
                     at.along_z[i],
                 )
 
@@ -792,35 +780,47 @@
         at, columns = self.place, self.chunks[chunk]
         total = self.partial[at.z, at.flat, :, columns].astype(F32)
         for i in range(3):
-            self.wait(self.from_z.at[i, :, columns], (chunk, 4 + i))
+            self.wait(self.from_z.at[i, :, columns], chunk, 4 + i)
             total += self.from_z[i, :, columns].astype(F32)
         return total
 
     def finish(self):
-        for copy in self.sent:
-            copy.wait_send()
-
-
-def reduce_kernel(
-    half, mlp_chunks, attn_chunks, zero_ref, mlp_ref, attn_ref, small_ref, mlp_out, attn_out, small_out,
+        for chunk, columns in enumerate(self.chunks):
+            pair, four, one = [self.partial.at[pl.ds(0, n), 0, :, columns] for n in (2, 4, 1)]
+            for slot, ref in enumerate([pair] * 2 + [four] * 2 + [one] * 3):
+                sent(ref, self.out_sems.at[chunk, slot], self.in_sems.at[chunk, slot], self.place.sibling)
+
+
+GAIN_ONE, GAIN_TWO, GAIN_OUT, LOW_IN = 0, 8, 16, 24
+
+
+def small_rows(width, rank, keys):
+    decay = LOW_IN + rank * width // 128
+    slot = -(-(rank + 1) * keys // 128 // 8) * 8
+    return decay, slot, decay + 2 * slot
+
+
+def backward_kernel(
+    half, mlp_chunks, attn_chunks,
+    zero_ref, groups_ref, attn_ref, h_ref, query_ref, key_ref, value_ref, gate_ref, logits_ref, low_rank_ref,
+    attended_ref, mixed_ref, states_ref, w_query, w_key, w_value, w_gate, w_low_in, w_low_out, w_out,
+    tokens_ref, total_ref, gain_one_ref, gain_out_ref, gain_two_grad_ref,
+    mlp_out, attn_out, small_out, tokens_out,
     mlp, attn, mlp_via_x, mlp_via_y, mlp_from_x, mlp_from_y, mlp_from_z,
-    attn_via_x, attn_via_y, attn_from_x, attn_from_y, attn_from_z, summed, swapped, small_in, small_z,
-    load_sems, mlp_sems_out, mlp_sems_in, attn_sems_out, attn_sems_in, other_sems_out, other_sems_in,
+    attn_via_x, attn_via_y, attn_from_x, attn_from_y, attn_from_z, summed, swapped,
+    small_own, small_in, small_z, h_turned, attn_turned, right, mixed_all, h_grad, h_grad_out, h_grad_in,
+    memory_grad, gain_out_sum, low_in_sum, low_out_sum, bias_sum,
+    load_sems, mlp_sems_out, mlp_sems_in, attn_sems_out, attn_sems_in, pair_out, pair_in, small_sems_out, small_sems_in,
 ):
+    step = pl.program_id(0)
     at = Place()
-    loads = []
-    for i, columns in enumerate(mlp_chunks):
-        source = mlp_ref.at[i - 1] if i else zero_ref
-        loads.append(pltpu.make_async_copy(source, mlp.at[:, :, :, columns], load_sems.at[i]))
-    for i, columns in enumerate(attn_chunks):
-        loads.append(
-            pltpu.make_async_copy(
-                attn_ref.at[:, :, :, columns], attn.at[:, :, :, columns], load_sems.at[len(mlp_chunks) + i]
-            )
-        )
-    for load in loads:
-        load.start()
-    at.meet()
+    own = tokens_ref.shape[0]
+    own_tiles = own // ROWS
+    tiles = 2 * own_tiles
+    keys, values = w_query.shape[1], w_value.shape[1]
+    rank, width = w_low_out.shape[0], tokens_ref.shape[1]
+    decay_at, decay_slot, _ = small_rows(width, rank, keys)
+    last_step = 2 * tiles
     sides = [
         Reduce(at, mlp, mlp_via_x, mlp_via_y, mlp_from_x, mlp_from_y, mlp_from_z, mlp_chunks, mlp_sems_out, mlp_sems_in),
         Reduce(
@@ -831,31 +831,42 @@
     order = [(0, i) for i in range(len(mlp_chunks))] + [(1, i) for i in range(len(attn_chunks))]
     count = len(order)
     rows = mlp.shape[2] // 2
-    sent = []
-
-    def put(source, target, slot, device):
-        sent.append(send(source, target, other_sems_out.at[slot], other_sems_in.at[slot], device))
+
+    def load(chunk):
+        source = groups_ref.at[chunk - 1] if chunk else zero_ref
+        return pltpu.make_async_copy(source, mlp.at[:, :, :, mlp_chunks[chunk]], load_sems.at[chunk])
+
+    def put(source, target, slot):
+        send(source, target, pair_out.at[slot], pair_in.at[slot], at.sibling)
 
     def wait(target, slot):
-        arrived(target, other_sems_out.at[slot], other_sems_in.at[slot], at.sibling)
-
-    def small(step):
-        if step == 0:
-            put(small_ref, small_in.at[0], 0, at.sibling)
-        elif step in (1, 2):
-            source = small_ref if step == 1 else small_z.at[step - 2]
-            wait(small_in.at[step - 1], step - 1)
-            small_z[step - 1] = source[...] + small_in[step - 1]
-            put(small_z.at[step - 1], small_in.at[step], step, at.beside_x if step == 1 else at.beside_y)
-        elif step == 3:
-            wait(small_in.at[2], 2)
+        arrived(target, pair_out.at[slot], pair_in.at[slot], at.sibling)
+
+    def small(number):
+        def put_small(source, target, slot, device):
+            send(source, target, small_sems_out.at[slot], small_sems_in.at[slot], device)
+
+        def wait_small(target, slot):
+            arrived(target, small_sems_out.at[slot], small_sems_in.at[slot], at.sibling)
+
+        if number == 0:
+            put_small(small_own, small_in.at[0], 0, at.sibling)
+        elif number in (1, 2):
+            source = small_own if number == 1 else small_z.at[number - 2]
+            wait_small(small_in.at[number - 1], number - 1)
+            small_z[number - 1] = source[...] + small_in[number - 1]
+            put_small(small_z.at[number - 1], small_in.at[number], number, at.beside_x if number == 1 else at.beside_y)
+        elif number == 3:
+            wait_small(small_in.at[2], 2)
             small_z[2 + at.z] = small_z[1] + small_in[2]
             for i in range(3):
-                put(small_z.at[2 + at.z], small_z.at[2 + at.z], 3 + i, at.along_z[i])
-        elif step == 4:
+                put_small(small_z.at[2 + at.z], small_z.at[2 + at.z], 3 + i, at.along_z[i])
+        elif number == 4:
             for i in range(3):
-                wait(small_z.at[2 + (at.z + 3 - i) % 4], 3 + i)
+                wait_small(small_z.at[2 + (at.z + 3 - i) % 4], 3 + i)
             small_out[...] = small_z[2] + small_z[3] + small_z[4] + small_z[5]
+            for slot in range(6):
+                sent(small_own, small_sems_out.at[slot], small_sems_in.at[slot], at.sibling)
 
     def result(side, chunk):
         total = sides[side].result(chunk)
@@ -863,22 +874,138 @@
             columns = mlp_chunks[chunk]
             summed[:, columns] = total
             put(
-                summed.at[pl.ds((1 - at.head) * rows, rows), columns], swapped.at[:, columns], 6 + chunk, at.sibling
+                summed.at[pl.ds(pl.multiple_of((1 - at.head) * rows, 8), rows), columns], swapped.at[:, columns],
+                2 + chunk,
             )
         else:
             attn_out[:, attn_chunks[chunk]] = total
 
-    for tick in range(count + 3):
-        if 0 <= tick - 3 < count:
-            result(*order[tick - 3])
-        for number in range(2, -1, -1):
-            if 0 <= tick - number < count:
-                if number == 0:
-                    loads[tick].wait()
-                side, chunk = order[tick - number]
-                sides[side].stage(number, chunk)
-        if tick < 5:
-            small(tick)
+    def tick(number):
+        if 0 <= number - 3 < count:
+            result(*order[number - 3])
+        for stage in range(2, -1, -1):
+            if 0 <= number - stage < count:
+                side, chunk = order[number - stage]
+                if stage == 0 and side == 0:
+                    load(chunk).wait()
+                sides[side].stage(stage, chunk)
+
+    def own_rows(i):
+        return pl.ds(pl.multiple_of(i * ROWS, ROWS), ROWS)
+
+    @pl.when(step == 0)
+    def _():
+        for chunk in range(len(mlp_chunks)):
+            load(chunk).start()
+        memory_grad[...] = jnp.zeros_like(memory_grad)
+        gain_out_sum[...] = jnp.zeros_like(gain_out_sum)
+        low_in_sum[...] = jnp.zeros_like(low_in_sum)
+        low_out_sum[...] = jnp.zeros_like(low_out_sum)
+        bias_sum[...] = jnp.zeros_like(bias_sum)
+        at.meet()
+
+    early_ticks = min(len(mlp_chunks), last_step)
+    for number in range(early_ticks):
+
+        @pl.when(step == number)
+        def _():
+            tick(number)
+
+    @pl.when(step < tiles)
+    def _():
+        tile = tiles - 1 - step
+        here = pl.ds(pl.multiple_of(tile * ROWS, ROWS), ROWS)
+        attn_tile = attn_ref[...]
+        h_tile = h_ref[...]
+        attn_turned[:, here] = jnp.transpose(attn_tile)
+        h_turned[:, here] = jnp.transpose(h_tile)
+        mixed_all[here, :] = mixed_ref[...]
+        mixed_grad = dot(attn_tile, w_out[...], 1, 1)
+        logits_parts = []
+        for i in range(ROWS // BLOCK - 1, -1, -1):
+            block = slice(i * BLOCK, (i + 1) * BLOCK)
+            grads, logits_grad, gain_grad = backward_block(
+                mixed_grad[block], query_ref[block, :], key_ref[block, :], value_ref[block, :], logits_ref[block, :],
+                gate_ref[block, :], attended_ref[block, :], states_ref[i], gain_out_ref[...], memory_grad,
+            )
+            right[pl.ds(pl.multiple_of(tile * ROWS + i * BLOCK, BLOCK), BLOCK), :] = grads
+            gain_out_sum[...] += gain_grad
+            logits_parts.append(logits_grad)
+        logits_grad = jnp.concatenate(logits_parts[::-1], axis=0)
+        high, rest = split_low(logits_grad)
+        rank_high, rank_rest = split_low(low_rank_ref[...])
+        bias_sum[...] += jnp.sum(logits_grad, axis=0, keepdims=True)
+        low_out_sum[...] += dot(rank_high, high, 0, 0) + dot(rank_rest, high, 0, 0) + dot(rank_high, rest, 0, 0)
+        low_rank_low = (dot(high, w_low_out[...], 1, 1) + dot(rest, w_low_out[...], 1, 1)).astype(BF16)
+        low_in_sum[...] += dot(low_rank_low, h_tile, 0, 0)
+        grads = right[here, :]
+        part = (
+            dot(grads[:, :keys], w_query[...], 1, 1)
+            + dot(grads[:, keys : 2 * keys], w_key[...], 1, 1)
+            + dot(grads[:, 2 * keys : 2 * keys + values], w_value[...], 1, 1)
+            + dot(grads[:, 2 * keys + values :], w_gate[...], 1, 1)
+            + dot(low_rank_low, w_low_in[...], 1, 1)
+        )
+        place = tile % own_tiles
+        mine = tile // own_tiles == at.head
+
+        @pl.when(mine)
+        def _():
+            h_grad[own_rows(place), :] = part
+
+        @pl.when(jnp.logical_not(mine))
+        def _():
+            h_grad_out[own_rows(place), :] = part.astype(BF16)
+            put(h_grad_out.at[own_rows(place)], h_grad_in.at[own_rows(place)], place)
+
+    @pl.when(step == tiles)
+    def _():
+        gain_one = jnp.zeros((1, width), F32)
+        for i in range(own_tiles):
+            here = own_rows(i)
+            wait(h_grad_in.at[here], i)
+            wide = tokens_ref[here, :].astype(F32)
+            scale = lax.rsqrt(jnp.mean(wide * wide, axis=1, keepdims=True) + EPSILON)
+            normal = wide * scale
+            grad = h_grad[here, :] + h_grad_in[here, :].astype(F32)
+            tokens_out[here, :] = total_ref[here, :] + norm_backward(grad, gain_one_ref[...], normal, scale)
+            gain_one += jnp.sum(grad * normal, axis=0, keepdims=True)
+        small_own[...] = jnp.zeros_like(small_own)
+        for i in range(width // 128):
+            columns = slice(i * 128, (i + 1) * 128)
+            small_own[GAIN_ONE + i : GAIN_ONE + i + 1, :] = gain_one[:, columns]
+            small_own[GAIN_TWO + i : GAIN_TWO + i + 1, :] = gain_two_grad_ref[:, columns]
+            small_own[LOW_IN + i * rank : LOW_IN + (i + 1) * rank, :] = low_in_sum[:, columns]
+        for i in range(VALUE_HEAD // 128):
+            small_own[GAIN_OUT + i : GAIN_OUT + i + 1, :] = gain_out_sum[:, i * 128 : (i + 1) * 128]
+        for head in range(2):
+
+            @pl.when(at.head == head)
+            def _():
+                base = decay_at + head * decay_slot
+                for i in range(keys // 128):
+                    columns = slice(i * 128, (i + 1) * 128)
+                    small_own[base + i * rank : base + (i + 1) * rank, :] = low_out_sum[:, columns]
+                    bias_at = base + keys // 128 * rank + i
+                    small_own[bias_at : bias_at + 1, :] = bias_sum[:, columns]
+
+        small(0)
+
+    for number in range(1, 5):
+
+        @pl.when(step == tiles + number)
+        def _():
+            small(number)
+
+    @pl.when(jnp.logical_and(step >= tiles, step < 2 * tiles))
+    def _():
+        part = step - tiles
+        here = pl.ds(pl.multiple_of(part * ROWS, ROWS), ROWS)
+        shape = (attn.shape[1], attn.shape[2], -1)
+        edge = right.shape[1]
+        attn[part, :, :, :edge] = dot(h_turned[here, :], right[...]).astype(BF16).reshape(shape)
+        attn[part, :, :, edge:] = dot(attn_turned[here, :], mixed_all[...]).astype(BF16).reshape(shape)
+
     def spread(source, head):
         offset = 0
         for columns in mlp_chunks:
@@ -889,68 +1016,108 @@
                 mlp_out[:, target] = source[:, start : start + size]
             offset += size
 
-    spread(summed.at[pl.ds(pl.multiple_of(at.head * rows, 8), rows)], at.head)
-    for chunk, columns in enumerate(mlp_chunks):
-        wait(swapped.at[:, columns], 6 + chunk)
-    spread(swapped, 1 - at.head)
-    for copy in sent:
-        copy.wait_send()
-    for side in sides:
-        side.finish()
-
-
-def reduce_gradients(zero, mlp, attn, small):
-    rows = attn.shape[0] // 16
-    mlp_count = mlp.shape[0] + 1
-    edges = [0] + [zero.shape[-1] + i * mlp.shape[-1] for i in range(mlp_count)]
+    @pl.when(step == last_step)
+    def _():
+        for number in range(early_ticks, count + 3):
+            tick(number)
+            if number == len(mlp_chunks) + 3:
+                spread(summed.at[pl.ds(pl.multiple_of(at.head * rows, 8), rows)], at.head)
+                for chunk, columns in enumerate(mlp_chunks):
+                    wait(swapped.at[:, columns], 2 + chunk)
+                spread(swapped, 1 - at.head)
+        for i in range(own_tiles):
+            sent(h_grad_out.at[own_rows(i)], pair_out.at[i], pair_in.at[i], at.sibling)
+        for chunk, columns in enumerate(mlp_chunks):
+            sent(swapped.at[:, columns], pair_out.at[2 + chunk], pair_in.at[2 + chunk], at.sibling)
+        for side in sides:
+            side.finish()
+
+
+def backward(
+    zero, groups, attn_low, h_low, query, key, value, gate, logits, low_rank, attended, mixed, states,
+    w_query, w_key, w_value, w_gate, w_low_in, w_low_out, w_out, tokens, total, gain_one, gain_out, gain_two_grad,
+):
+    length, width = h_low.shape
+    keys, values, heads = query.shape[1], value.shape[1], states.shape[1]
+    rank = w_low_out.shape[0]
+    own = tokens.shape[0]
+    tiles = length // ROWS
+    rows = width // 16
+    mlp_count = groups.shape[0] + 1
+    edges = [0] + [zero.shape[-1] + i * groups.shape[-1] for i in range(mlp_count)]
     mlp_chunks = [slice(edges[i], edges[i + 1]) for i in range(mlp_count)]
-    width = edges[-1]
-    half = width // 3
-    attn_tiles = attn.shape[1] // 128
+    mlp_width = edges[-1]
+    attn_width = 2 * keys + 3 * values
     attn_count = 4
-    attn_chunks = chunk_columns(
-        attn.shape[1], [attn_tiles // attn_count + (1 if i < attn_tiles % attn_count else 0) for i in range(attn_count)]
-    )
+    attn_chunks = chunk_columns(attn_width, [attn_width // 128 // attn_count] * attn_count)
+    small_shape = (small_rows(width, rank, keys)[2], 128)
     vmem = pl.BlockSpec(memory_space=pltpu.VMEM)
+
+    def rows_spec(columns):
+        return pl.BlockSpec((ROWS, columns), lambda i: (jnp.maximum(tiles - 1 - i, 0), 0))
+
     buffers = []
-    for columns in (width, attn.shape[1]):
-        buffers += [
-            pltpu.VMEM((2, rows, columns), BF16),
-            pltpu.VMEM((2, rows, columns), BF16),
-            pltpu.VMEM((4, rows, columns), BF16),
-            pltpu.VMEM((4, rows, columns), BF16),
-            pltpu.VMEM((3, rows, columns), BF16),
+    for columns in (mlp_width, attn_width):
+        buffers += [pltpu.VMEM((n, rows, columns), BF16) for n in (2, 2, 4, 4, 3)]
+    streamed = [attn_low, h_low, query, key, value, gate, logits, low_rank, attended, mixed]
+    constant = [
+        w_query, w_key, w_value, w_gate, w_low_in, w_low_out, w_out, tokens, total,
+        gain_one.reshape(1, -1), gain_out.reshape(1, -1), gain_two_grad.reshape(1, -1),
+    ]
+    return pl.pallas_call(
+        functools.partial(backward_kernel, mlp_width // 3, mlp_chunks, attn_chunks),
+        grid=(2 * tiles + 1,),
+        in_specs=[ANY, ANY]
+        + [rows_spec(a.shape[1]) for a in streamed]
+        + [
+            pl.BlockSpec(
+                (ROWS // BLOCK, heads, KEY_HEAD, VALUE_HEAD), lambda i: (jnp.maximum(tiles - 1 - i, 0), 0, 0, 0)
+            )
         ]
-    return pl.pallas_call(
-        functools.partial(reduce_kernel, half, mlp_chunks, attn_chunks),
-        in_specs=[ANY, ANY, ANY, vmem],
-        out_specs=[vmem, vmem, vmem],
+        + [whole(a.shape) for a in constant],
+        out_specs=[vmem, vmem, vmem, vmem],
         out_shape=[
-            jax.ShapeDtypeStruct((rows // 2, 6 * half), F32),
-            jax.ShapeDtypeStruct((rows, attn.shape[1]), F32),
-            jax.ShapeDtypeStruct(small.shape, F32),
+            jax.ShapeDtypeStruct((rows // 2, 2 * mlp_width), F32),
+            jax.ShapeDtypeStruct((rows, attn_width), F32),
+            jax.ShapeDtypeStruct(small_shape, F32),
+            jax.ShapeDtypeStruct((own, width), F32),
         ],
         scratch_shapes=[
-            pltpu.VMEM((4, 4, rows, width), BF16),
-            pltpu.VMEM((4, 4, rows, attn.shape[1]), BF16),
+            pltpu.VMEM((4, 4, rows, mlp_width), BF16),
+            pltpu.VMEM((4, 4, rows, attn_width), BF16),
             *buffers,
-            pltpu.VMEM((rows, width), F32),
-            pltpu.VMEM((rows // 2, width), F32),
-            pltpu.VMEM((3,) + small.shape, F32),
-            pltpu.VMEM((6,) + small.shape, F32),
-            pltpu.SemaphoreType.DMA((mlp_count + attn_count,)),
+            pltpu.VMEM((rows, mlp_width), F32),
+            pltpu.VMEM((rows // 2, mlp_width), F32),
+            pltpu.VMEM(small_shape, F32),
+            pltpu.VMEM((3,) + small_shape, F32),
+            pltpu.VMEM((6,) + small_shape, F32),
+            pltpu.VMEM((width, length), BF16),
+            pltpu.VMEM((width, length), BF16),
+            pltpu.VMEM((length, 2 * keys + 2 * values), BF16),
+            pltpu.VMEM((length, values), BF16),
+            pltpu.VMEM((own, width), F32),
+            pltpu.VMEM((own, width), BF16),
+            pltpu.VMEM((own, width), BF16),
+            pltpu.VMEM((heads, KEY_HEAD, VALUE_HEAD), F32),
+            pltpu.VMEM((1, VALUE_HEAD), F32),
+            pltpu.VMEM((rank, width), F32),
+            pltpu.VMEM((rank, keys), F32),
+            pltpu.VMEM((1, keys), F32),
+            pltpu.SemaphoreType.DMA((mlp_count,)),
             pltpu.SemaphoreType.DMA((mlp_count, 7)),
             pltpu.SemaphoreType.DMA((mlp_count, 7)),
             pltpu.SemaphoreType.DMA((attn_count, 7)),
             pltpu.SemaphoreType.DMA((attn_count, 7)),
-            pltpu.SemaphoreType.DMA((6 + mlp_count,)),
-            pltpu.SemaphoreType.DMA((6 + mlp_count,)),
+            pltpu.SemaphoreType.DMA((2 + mlp_count,)),
+            pltpu.SemaphoreType.DMA((2 + mlp_count,)),
+            pltpu.SemaphoreType.DMA((6,)),
+            pltpu.SemaphoreType.DMA((6,)),
         ],
         compiler_params=pltpu.CompilerParams(
-            collective_id=1, has_side_effects=True, vmem_limit_bytes=58 << 20
+            collective_id=1, has_side_effects=True, vmem_limit_bytes=63 << 20
         ),
-        name="reduce_gradients",
-    )(zero, mlp, attn.reshape(4, 4, rows, -1), small)
+        name="backward",
+    )(zero, groups, *streamed, states, *constant)
 
 
 def swap(value):
@@ -1007,8 +1174,23 @@
             tokens_own, low_own, row_mask, norm_attn_gain, norm_mlp_gain, out_gain, decay_bias, initial_memory[0],
             w_query, w_key, w_value, w_gate_out, w_low_in, w_low_out, w_out, own_piece, other_piece,
         )
-        low_high, low_rest = split_low(low_rank)
-        output, gain_two_grad = output[None], gain_two_grad[0]
+        grad_mlp, attn_grads, packed, tokens_grad = backward(
+            grad_zero, grad_mlp, attn_low, h_low, query, key, value, gate, logits, low_rank, attended, mixed, states,
+            w_query, w_key, w_value, w_gate_out, w_low_in, w_low_out, w_out, tokens_own, resid_total,
+            norm_attn_gain, out_gain, gain_two_grad,
+        )
+        output = output[None]
+        rank = w_low_out.shape[0]
+        model = tokens_own.shape[1]
+        decay_at, decay_slot, _ = small_rows(model, rank, keys)
+        gain_one_grad = packed[GAIN_ONE : GAIN_ONE + model // 128].reshape(-1)
+        gain_two_grad = packed[GAIN_TWO : GAIN_TWO + model // 128].reshape(-1)
+        out_gain_grad = packed[GAIN_OUT : GAIN_OUT + VALUE_HEAD // 128].reshape(-1)
+        low_in_grad = packed[LOW_IN:decay_at].reshape(-1, rank, 128).transpose(0, 2, 1).reshape(model, rank)
+        decay_part = lax.dynamic_slice_in_dim(packed, decay_at + here * decay_slot, decay_slot, 0)
+        edge = keys // 128 * rank
+        low_out_grad = decay_part[:edge].reshape(-1, rank, 128).transpose(1, 0, 2).reshape(rank, keys)
+        bias_grad = decay_part[edge : edge + keys // 128].reshape(-1)
     else:
         pair = swap(other_piece.reshape(shard_rows, 3 * half))
         weights = lax.all_gather(
@@ -1059,56 +1241,50 @@
         attn_own = resid_total.astype(BF16)
         attn_low = ordered(attn_own, swap(attn_own), 0)
 
-    mixed_grad = dot(attn_low, w_out, 1, 1)
-    out_grad = dot(attn_low, mixed, 0, 0)
-    query_grad, key_grad, value_grad, gate_grad, logits_grad, out_gain_grad = attention_backward(
-        mixed_grad, query, key, value, logits, gate, attended, states, out_gain
-    )
-    bias_grad = jnp.sum(logits_grad, axis=0)
-    grad_high, grad_rest = split_low(logits_grad)
-    low_out_grad = (
-        dot(low_high, grad_high, 0, 0) + dot(low_rest, grad_high, 0, 0) + dot(low_high, grad_rest, 0, 0)
-    )
-    low_rank_low = (dot(grad_high, w_low_out, 1, 1) + dot(grad_rest, w_low_out, 1, 1)).astype(BF16)
-    low_in_grad = dot(h_low, low_rank_low, 0, 0)
-    attn_grads = jnp.concatenate(
-        [
-            dot(h_low, query_grad, 0, 0).astype(BF16),
-            dot(h_low, key_grad, 0, 0).astype(BF16),
-            dot(h_low, value_grad, 0, 0).astype(BF16),
-            dot(h_low, gate_grad, 0, 0).astype(BF16),
-            out_grad.astype(BF16),
-        ],
-        axis=1,
-    )
-    h_grad = sum_rows(
-        dot(query_grad, w_query, 1, 1)
-        + dot(key_grad, w_key, 1, 1)
-        + dot(value_grad, w_value, 1, 1)
-        + dot(gate_grad, w_gate_out, 1, 1)
-        + dot(low_rank_low, w_low_in, 1, 1),
-        here,
-    )
-    own_wide = tokens_own.astype(F32)
-    own_scale = lax.rsqrt(jnp.mean(own_wide * own_wide, axis=1, keepdims=True) + EPSILON)
-    normal_own = own_wide * own_scale
-    tokens_grad = resid_total + norm_backward(h_grad, norm_attn_gain, normal_own, own_scale)
-    gain_one_grad = jnp.sum(h_grad * normal_own, axis=0)
-
-    low_rank_width = w_low_out.shape[0]
-    decay_part = jnp.concatenate([low_out_grad, bias_grad[None]], axis=0)
-    slots = jnp.zeros((2,) + decay_part.shape, F32)
-    slots = lax.dynamic_update_slice(slots, decay_part[None], (here, 0, 0))
-    packed = jnp.concatenate(
-        [
-            gain_one_grad, gain_two_grad, out_gain_grad.reshape(-1), low_in_grad.reshape(-1), slots.reshape(-1),
-        ]
-    )
-    if square:
-        packed = packed.reshape(-1, 128)
-        grad_mlp, attn_grads, packed = reduce_gradients(grad_zero, grad_mlp, attn_grads, packed)
-        packed = packed.reshape(-1)
-    else:
+        mixed_grad = dot(attn_low, w_out, 1, 1)
+        out_grad = dot(attn_low, mixed, 0, 0)
+        query_grad, key_grad, value_grad, gate_grad, logits_grad, out_gain_grad = attention_backward(
+            mixed_grad, query, key, value, logits, gate, attended, states, out_gain
+        )
+        bias_grad = jnp.sum(logits_grad, axis=0)
+        grad_high, grad_rest = split_low(logits_grad)
+        low_out_grad = (
+            dot(low_high, grad_high, 0, 0) + dot(low_rest, grad_high, 0, 0) + dot(low_high, grad_rest, 0, 0)
+        )
+        low_rank_low = (dot(grad_high, w_low_out, 1, 1) + dot(grad_rest, w_low_out, 1, 1)).astype(BF16)
+        low_in_grad = dot(h_low, low_rank_low, 0, 0)
+        attn_grads = jnp.concatenate(
+            [
+                dot(h_low, query_grad, 0, 0).astype(BF16),
+                dot(h_low, key_grad, 0, 0).astype(BF16),
+                dot(h_low, value_grad, 0, 0).astype(BF16),
+                dot(h_low, gate_grad, 0, 0).astype(BF16),
+                out_grad.astype(BF16),
+            ],
+            axis=1,
+        )
+        h_grad = sum_rows(
+            dot(query_grad, w_query, 1, 1)
+            + dot(key_grad, w_key, 1, 1)
+            + dot(value_grad, w_value, 1, 1)
+            + dot(gate_grad, w_gate_out, 1, 1)
+            + dot(low_rank_low, w_low_in, 1, 1),
+            here,
+        )
+        own_wide = tokens_own.astype(F32)
+        own_scale = lax.rsqrt(jnp.mean(own_wide * own_wide, axis=1, keepdims=True) + EPSILON)
+        normal_own = own_wide * own_scale
+        tokens_grad = resid_total + norm_backward(h_grad, norm_attn_gain, normal_own, own_scale)
+        gain_one_grad = jnp.sum(h_grad * normal_own, axis=0)
+        low_rank_width = w_low_out.shape[0]
+        decay_part = jnp.concatenate([low_out_grad, bias_grad[None]], axis=0)
+        slots = jnp.zeros((2,) + decay_part.shape, F32)
+        slots = lax.dynamic_update_slice(slots, decay_part[None], (here, 0, 0))
+        packed = jnp.concatenate(
+            [
+                gain_one_grad, gain_two_grad, out_gain_grad.reshape(-1), low_in_grad.reshape(-1), slots.reshape(-1),
+            ]
+        )
         packed = lax.psum(packed, ("dp", "head"))
         attn_grads = lax.psum_scatter(attn_grads, "dp", scatter_dimension=0, tiled=True).astype(F32)
         grad_mlp = lax.psum_scatter(grad_mlp, "dp", scatter_dimension=0, tiled=True)
@@ -1117,26 +1293,28 @@
         grad_mlp = ordered(
             own_half.reshape(shard_rows, 3, 1, half), other_half.reshape(shard_rows, 3, 1, half), 2
         ).reshape(shard_rows, 3 * hidden).astype(F32)
-    width = gain_one_grad.shape[0]
-    edges = [width, 2 * width, 2 * width + VALUE_HEAD]
-    edges.append(edges[-1] + width * low_rank_width)
-    low_in_grad = packed[edges[2] : edges[3]].reshape(width, low_rank_width)
-    decay_part = lax.dynamic_index_in_dim(packed[edges[3] :].reshape(slots.shape), here, 0, keepdims=False)
-
+        width = gain_one_grad.shape[0]
+        edges = [width, 2 * width, 2 * width + VALUE_HEAD]
+        edges.append(edges[-1] + width * low_rank_width)
+        low_in_grad = packed[edges[2] : edges[3]].reshape(width, low_rank_width)
+        decay_part = lax.dynamic_index_in_dim(packed[edges[3] :].reshape(slots.shape), here, 0, keepdims=False)
+        low_out_grad, bias_grad = decay_part[:low_rank_width], decay_part[low_rank_width]
+        gain_one_grad, gain_two_grad = packed[: edges[0]], packed[edges[0] : edges[1]]
+        out_gain_grad = packed[edges[1] : edges[2]]
     return (
         output,
         tokens_grad[None],
-        packed[: edges[0]],
+        gain_one_grad,
         attn_grads[:, :keys],
         attn_grads[:, keys : 2 * keys],
         attn_grads[:, 2 * keys : 2 * keys + values],
         attn_grads[:, 2 * keys + values : 2 * keys + 2 * values],
         low_in_grad,
-        decay_part[:low_rank_width],
-        decay_part[low_rank_width],
-        packed[edges[1] : edges[2]],
+        low_out_grad,
+        bias_grad,
+        out_gain_grad,
         attn_grads[:, 2 * keys + 2 * values :].T,
-        packed[edges[0] : edges[1]],
+        gain_two_grad,
         grad_mlp,
     )
 

time: 355 us -> 299 us (0.84)
  matrix products: 40.5 us -> 0 us
  local copies, waits for them, and re-layouts: 34.5 us -> 20.5 us
  other arithmetic: 9.18 us -> 3.18 us
  Pallas kernels: 268 us -> 273 us
    dot_general x17 -> x0, matrix products: 40.5 us -> none  [dot(): lax.dot_general(left, right, (((left_dim,), (right_dim,)), ((), ())), pre...]
    concatenate x2 -> x0, local copies, waits for them, and re-layouts: 6.57 us -> none  [the longest x1 6.56 us: per_device(): jnp.concatenate([dot(h_low, query_grad, 0, 0).astype(BF16), dot(h_low, ke...]
    pallas_call x2 -> x1, Pallas kernels: 141 us -> 147 us  [backward(): pl.pallas_call(functools.partial(backward_kernel, mlp_width // 3, mlp_chu...]
    broadcast_in_dim x1 -> x0, other arithmetic: 4.02 us -> none  [per_device(): tokens_grad[None]]
    slice x6 -> x2, local copies, waits for them, and re-layouts: 5.5 us -> 1.56 us  [the longest x1 0.84 us: per_device(): packed[LOW_IN:decay_at].reshape(-1, rank, 128).transpose(0, 2, 1)]
    unnamed x58 -> x12, local copies, waits for them, and re-layouts: 9.11 us -> 6.09 us
  transfers between devices with their start and end apart: 1 -> 0, of which waited for: 0 -> 0; matrix products, arithmetic and copies ran while one was open for 7% -> 0% of each run, Pallas kernels for 0% -> 0%
where the time goes in v4:
time: 299 us; the launch traced here: 298 us
  Pallas kernels  273 us (91%)
  local copies, waits for them, and re-layouts  20.5 us (7%)
  other arithmetic  3.18 us (1%)
    pallas_call x1, Pallas kernels, backward(): pl.pallas_call(functools.partial(backward_kernel, mlp_width // 3, mlp_chu...  147 us
    pallas_call x1, Pallas kernels, layer(): pl.pallas_call(functools.partial(layer_kernel, count), grid=(steps,), in_...  127 us
    unnamed x12, local copies, waits for them, and re-layouts  6.09 us

profile of v4, /device:TPU:0, one launch (start us, length us, event | category | flops | bytes accessed | tf_op | source)
XLA Modules:
  0.0 298.4 jit_solution(9628713566268447035)
XLA Ops:
  0.6 0.0 copy-start.3
  0.7 0.0 copy-start.2
  1.4 2.4 fusion.low_ref
  3.8 0.7 fusion.1.mask_ref
  4.6 0.0 copy-done.3
  4.6 0.8 copy.59.w_low_in
  5.4 0.1 reshape.107
  5.6 1.1 constant_dynamic-slice_fusion.1
  6.7 0.1 copy_bitcast_fusion
  6.8 0.6 copy_bitcast_fusion.4.piece_zero
  7.4 0.3 reshape.109
  7.7 0.2 copy.55
  7.9 1.0 reshape.110.pieces
  8.9 0.6 copy_bitcast_fusion.3.other_zero
  9.5 0.3 reshape.112
  9.8 0.2 copy.58
  10.1 1.0 reshape.113.others
  11.0 126.8 %layer.1 = (bf16[1024,1024]{1,0:T(8,128)(2,1)}, bf16[1024,256]{1,0:T(8,128)(2,1)}, bf16[1024,256]{1,0:T(8,128)(2,1)}, bf16[1024,512]{1,0:T(8,128)(2,1)}, f32[102...) custom-call(bf16[512,1024]{1,0:T(8,128)(2,1)} %bitcast.58, ...), custom_call_target="tpu_custom_call" | custom-call | tf_op jit(solution)/shard_map/layer/pallas_call | solution.py:666
  137.8 146.5 %backward.1 = (f32[32,8448]{1,0:T(8,128)}, f32[64,2048]{1,0:T(8,128)}, f32[232,128]{1,0:T(8,128)}, f32[512,1024]{1,0:T(8,128)}) custom-call(bf16[4,4,64,384]{3,2,1,0:T(8,128)(2,1)} %get-tuple-element.35.zero_ref, bf16[5,4,4,64,768]{4,3,2,1,0:T(8,128)(2,1)} %get-tuple-element.36.groups_ref, bf16[1024,1024]{1,0:T(8,128)(2,1)} %get-tuple-element.37.attn_ref, ...), custom_call_target="tpu_custom_call" | custom-call | tf_op jit(solution)/shard_map/backward/pallas_call | solution.py:1067
  284.3 1.4 slice_bitcast_fusion.3
  285.8 1.5 fusion.3
  287.3 1.8 slice_bitcast_fusion
  289.1 0.8 slice.54
  289.9 0.6 copy.73
  290.5 0.7 constant_dynamic-slice_fusion
  291.3 0.6 copy.74
  291.9 1.3 slice_bitcast_fusion.5
  293.2 2.3 copy.79
  295.4 0.0 copy-done
  295.4 1.3 copy.80
  296.7 0.7 copy-done.1
  297.4 1.0 copy.81
  (6 shorter events, 0.0 us)
Async XLA Ops:
  0.6 3.9 %copy-start.3 = (bf16[1024,16]{0,1:T(8,128)(2,1)S(1)}, bf16[1024,16]{0,1:T(8,128)(2,1)}, u32[]{:S(2)}) copy-start(bf16[1024,16]{0,1:T(8,128)(2,1)} %param.24) | copy-start | bytes 98308
  0.7 4.8 %copy-start.2 = (bf16[32,8448]{1,0:T(8,128)(2,1)S(1)}, bf16[32,8448]{1,0:T(8,128)(2,1)}, u32[]{:S(2)}) copy-start(bf16[32,8448]{1,0:T(8,128)(2,1)} %param.30) | copy-start | bytes 1622020
  284.3 11.1 %copy-start = (f32[512,1024]{1,0:T(8,128)S(1)}, f32[512,1024]{1,0:T(8,128)}, u32[]{:S(2)}) copy-start(f32[512,1024]{1,0:T(8,128)} %get-tuple-element.50) | copy-start | bytes 6291460
  295.4 2.0 copy-start.1

commit v5 on v4

--- a/solution.py
+++ b/solution.py
@@ -323,9 +323,13 @@
 
 
 class Gather:
-    def __init__(self, place, pieces, others, blocks, local_sems, out_sems, in_sems):
-        self.place, self.pieces, self.others, self.blocks = place, pieces, others, blocks
-        self.local_sems, self.out_sems, self.in_sems = local_sems, out_sems, in_sems
+    LAGS = (0, 1, 3)
+
+    def __init__(self, place, source, targets, blocks, local_sems, swap_out, swap_in, out_sems, in_sems):
+        self.place, self.source, self.targets, self.blocks = place, source, targets, blocks
+        self.local_sems, self.swap_out, self.swap_in = local_sems, swap_out, swap_in
+        self.out_sems, self.in_sems = out_sems, in_sems
+        self.ticks = len(blocks) + self.LAGS[-1]
 
     def put(self, source, target, chunk, slot, device):
         send(source, target, self.out_sems.at[chunk, slot], self.in_sems.at[chunk, slot], device)
@@ -334,18 +338,25 @@
         arrived(target, self.out_sems.at[chunk, slot], self.in_sems.at[chunk, slot], self.place.sibling)
 
     def start(self):
-        at, count = self.place, len(self.blocks)
-        rows = self.pieces[0].shape[0]
+        at, source = self.place, self.source
+        rows, half = source.shape[0], source.shape[1] // 6
         mine = pl.ds(at.head * rows, rows)
         theirs = pl.ds((1 - at.head) * rows, rows)
-        for chunk in range(count):
-            target = self.blocks[chunk].at[at.z, at.flat, mine]
-            pltpu.make_async_copy(self.pieces[chunk], target, self.local_sems.at[chunk]).start()
-            self.put(self.others[chunk], target, chunk, 7, at.sibling)
-        for chunk in range(count):
-            target = self.blocks[chunk].at[at.z, at.flat, mine]
-            pltpu.make_async_copy(self.pieces[chunk], target, self.local_sems.at[chunk]).wait()
-            self.wait(self.blocks[chunk].at[at.z, at.flat, theirs], chunk, 7)
+        offset = 0
+        for i, block in enumerate(self.targets):
+            size = block.shape[3] // 3
+            for part in range(3):
+                target = block.at[at.z, at.flat, mine, part * size : (part + 1) * size]
+                base = 2 * part * half + offset
+                here = pl.ds(pl.multiple_of(base + at.head * half, 128), size)
+                there = pl.ds(pl.multiple_of(base + (1 - at.head) * half, 128), size)
+                pltpu.make_async_copy(source.at[:, here], target, self.local_sems.at[i]).start()
+                send(source.at[:, there], target, self.swap_out.at[i], self.swap_in.at[i], at.sibling)
+            offset += size
+        for i, block in enumerate(self.targets):
+            target = block.at[at.z, at.flat, mine]
+            pltpu.make_async_copy(target, target, self.local_sems.at[i]).wait()
+            arrived(block.at[at.z, at.flat, theirs], self.swap_out.at[i], self.swap_in.at[i], at.sibling)
 
     def stage(self, number, chunk):
         at, out = self.place, self.blocks[chunk]
@@ -367,22 +378,27 @@
             self.wait(out.at[everything, at.flat_y], chunk, 4)
             block = out.at[pl.ds(2, 2), at.flat_y]
             self.put(block, block, chunk, 6, at.beside_x)
-        if number == 3:
-            self.wait(out.at[pl.ds(0, 2), at.flat_xy], chunk, 5)
-            self.wait(out.at[pl.ds(2, 2), at.flat_xy], chunk, 6)
+
+    def complete(self, chunk):
+        at, out = self.place, self.blocks[chunk]
+        self.wait(out.at[pl.ds(0, 2), at.flat_xy], chunk, 5)
+        self.wait(out.at[pl.ds(2, 2), at.flat_xy], chunk, 6)
 
     def tick(self, number):
-        for stage in range(3, -1, -1):
-            if 0 <= number - stage < len(self.blocks):
-                self.stage(stage, number - stage)
+        for stage in (2, 1, 0):
+            chunk = number - self.LAGS[stage]
+            if 0 <= chunk < len(self.blocks):
+                self.stage(stage, chunk)
 
     def finish(self):
+        everything = slice(None)
         for chunk, block in enumerate(self.blocks):
-            everything = slice(None)
             shapes = [block.at[0, 0]] * 3 + [block.at[everything, 0]] * 2 + [block.at[pl.ds(0, 2), 0]] * 2
-            shapes.append(self.others[chunk])
             for slot, ref in enumerate(shapes):
                 sent(ref, self.out_sems.at[chunk, slot], self.in_sems.at[chunk, slot], self.place.sibling)
+        rows = self.source.shape[0]
+        for i, block in enumerate(self.targets):
+            sent(block.at[0, 0, pl.ds(0, rows)], self.swap_out.at[i], self.swap_in.at[i], self.place.sibling)
 
 
 def sent(source, out_sem, in_sem, device):
@@ -393,13 +409,13 @@
 
 def layer_kernel(
     count,
-    tokens_ref, low_ref, mask_ref, gain_one_ref, gain_two_ref, gain_out_ref, bias_ref, start_ref,
-    w_query, w_key, w_value, w_gate, w_low_in, w_low_out, w_out, piece_zero, pieces, other_zero, others,
+    tokens_ref, cotangent_ref, length_ref, gain_one_ref, gain_two_ref, gain_out_ref, bias_ref, start_ref,
+    w_query, w_key, w_value, w_gate, w_low_in, w_low_out, w_out, w_mlp,
     h_ref, query_ref, key_ref, value_ref, gate_ref, logits_ref, low_rank_ref, attended_ref, mixed_ref, states_ref,
     grad_zero_ref, grad_ref, output_ref, total_ref, attn_ref, gain_grad_ref,
     tokens, low, low_turned, h_two, h_two_turned, weights_zero, weights, resid, part_out, part_in,
     mlp_sum, grad_sum, inner_all, pair_all, sums_out, sums_in, memory,
-    local_sems, gather_local, gather_out, gather_in, pair_out, pair_in,
+    local_sems, gather_local, swap_out, swap_in, gather_out, gather_in, pair_out, pair_in,
 ):
     step = pl.program_id(0)
     at = Place()
@@ -410,11 +426,16 @@
     own_at = at.head * own
     gather = Gather(
         at,
-        [piece_zero] + [pieces.at[i] for i in range(count - 1)],
-        [other_zero] + [others.at[i] for i in range(count - 1)],
+        w_mlp,
         [weights_zero] + [weights.at[i] for i in range(count - 1)],
-        gather_local, gather_out, gather_in,
-    )
+        [weights_zero]
+        + [weights.at[i, :, :, :, j * 384 : (j + 1) * 384] for i in range(count - 1) for j in range(2)],
+        gather_local, swap_out, swap_in, gather_out, gather_in,
+    )
+    plan = {(0, 0): (0, 1), (1, 0): (2,), (2, 0): (3,), (3, 0): (4,), (4, 0): (5,), (4, 1): (6,)}
+    places = [(5, 1), (6, 0), (6, 1), (7, 1), (8, 0), (8, 1), (9, 1)]
+    for i, key in enumerate(places):
+        plan[key] = (7 + i,) if i < len(places) - 1 else tuple(range(7 + i, gather.ticks))
     attention_steps = tiles
     first_step = attention_steps + 1
     last_step = first_step + count - 1
@@ -425,6 +446,10 @@
     def other_rows(i, size=ROWS):
         return pl.ds(pl.multiple_of(own - own_at + i * ROWS, ROWS), size)
 
+    def row_mask(i):
+        positions = own_at + i * ROWS + lax.broadcasted_iota(jnp.int32, (ROWS, 1), 0)
+        return jnp.where(positions < length_ref[0], 1.0, 0.0)
+
     def put(source, target, slot):
         send(source, target, pair_out.at[slot], pair_in.at[slot], at.sibling)
 
@@ -433,30 +458,36 @@
 
     @pl.when(step == 0)
     def _():
-        at.meet()
-        put(tokens_ref, tokens.at[own_rows(0, own)], 0)
-        put(low_ref, low.at[own_rows(0, own)], 1)
         here = [
+            pltpu.make_async_copy(cotangent_ref, low.at[own_rows(0, own)], local_sems.at[1]),
             pltpu.make_async_copy(tokens_ref, tokens.at[own_rows(0, own)], local_sems.at[0]),
-            pltpu.make_async_copy(low_ref, low.at[own_rows(0, own)], local_sems.at[1]),
         ]
         for copy in here:
             copy.start()
+        at.meet()
+        put(tokens_ref, tokens.at[own_rows(0, own)], 0)
         memory[...] = start_ref[...]
         gain_grad_ref[...] = jnp.zeros_like(gain_grad_ref)
         gather.start()
-        gather.tick(0)
+        for number in plan[0, 0]:
+            gather.tick(number)
         for copy in here:
             copy.wait()
+        for i in range(own_tiles):
+            low[own_rows(i), :] = (low[own_rows(i), :].astype(F32) * row_mask(i)).astype(BF16)
+        put(low.at[own_rows(0, own)], low.at[own_rows(0, own)], 1)
         wait(tokens.at[other_rows(0, own)], 0)
-        wait(low.at[other_rows(0, own)], 1)
-
-    for number in range(1, count + 3):
-
-        @pl.when(step == number)
-        def _():
-            gather.tick(number)
-
+
+    def gather_at(inside, among):
+        for (when, which), numbers in plan.items():
+            if which == inside and when in among:
+
+                @pl.when(step == when)
+                def _():
+                    for number in numbers:
+                        gather.tick(number)
+
+    gather_at(0, range(1, attention_steps + 1))
     @pl.when(step < attention_steps)
     def _():
         rows = pl.ds(pl.multiple_of(step * ROWS, ROWS), ROWS)
@@ -468,7 +499,7 @@
         key = dot(h_low, w_key[...]).astype(BF16)
         value = dot(h_low, w_value[...]).astype(BF16)
         gate = dot(h_low, w_gate[...])
-        low_rank = dot(h_low, w_low_in[...])
+        low_rank = dot(h_low, w_low_in[...], 1, 1)
         high, rest = split_low(low_rank)
         logits = dot(high, w_low_out[...]) + dot(rest, w_low_out[...]) + bias_ref[...]
         query_ref[...] = query
@@ -501,6 +532,7 @@
 
     @pl.when(step == attention_steps)
     def _():
+        wait(low.at[other_rows(0, own)], 1)
         for i in range(own_tiles):
             rows = pl.ds(i * ROWS, ROWS)
             wait(part_in.at[rows], 2 + i)
@@ -509,6 +541,7 @@
             scale = lax.rsqrt(jnp.mean(full * full, axis=1, keepdims=True) + EPSILON)
             h_two[own_rows(i), :] = (full * scale * gain_two_ref[...]).astype(BF16)
             put(h_two.at[own_rows(i)], h_two.at[own_rows(i)], 4 + i)
+        gather_at(1, [attention_steps])
 
         def turn(i, carry):
             rows = pl.ds(pl.multiple_of(i * ROWS, ROWS), ROWS)
@@ -574,13 +607,24 @@
 
     @pl.when(step == first_step)
     def _():
+        gather.complete(0)
         hidden_rows(weights_zero, True)
+        gather_at(1, [first_step])
         weight_rows(weights_zero, grad_zero_ref)
+
+    for group in range(1, count):
+
+        @pl.when(step == first_step + group)
+        def _():
+            gather_at(0, [first_step + group])
+            gather.complete(2 * group - 1)
+            gather.complete(2 * group)
 
     @pl.when(step > first_step)
     def _():
         block = weights.at[step - first_step - 1]
         hidden_rows(block, False)
+        gather_at(1, range(first_step + 1, last_step))
 
         @pl.when(step == last_step)
         def _():
@@ -604,7 +648,7 @@
             scale = lax.rsqrt(jnp.mean(full * full, axis=1, keepdims=True) + EPSILON)
             normal = full * scale
             mlp_out = mlp_sum[own_rows(i), :] + sums_in[0, rows, :].astype(F32)
-            output_ref[rows, :] = (mask_ref[rows, :] * (full + mlp_out)).astype(BF16)
+            output_ref[rows, :] = (row_mask(i) * (full + mlp_out)).astype(BF16)
             grad = grad_sum[own_rows(i), :] + sums_in[1, rows, :].astype(F32)
             total = low[own_rows(i), :].astype(F32) + norm_backward(grad, gain_two_ref[...], normal, scale)
             total_ref[rows, :] = total
@@ -619,7 +663,7 @@
                 h_two.at[other_rows(i)], attn_ref.at[other_rows(i)], local_sems.at[own_tiles + i]
             ).start()
         for slot, ref in enumerate(
-            [tokens_ref, low_ref] + [part_out.at[pl.ds(0, ROWS)]] * 8 + [h_two.at[pl.ds(0, ROWS)]] * 2
+            [tokens_ref, low.at[pl.ds(0, own)]] + [part_out.at[pl.ds(0, ROWS)]] * 8 + [h_two.at[pl.ds(0, ROWS)]] * 2
         ):
             if slot not in (4, 5):
                 sent(ref, pair_out.at[slot], pair_in.at[slot], at.sibling)
@@ -632,24 +676,16 @@
     return pl.BlockSpec(shape, lambda i: (0,) * len(shape), pipeline_mode=pl.Buffered(1))
 
 
-def chunked(pieces, first):
-    rows, _, half = pieces.shape
-    rest = pieces[:, :, first:].reshape(rows, 3, -1, 2 * first)
-    return pieces[:, :, :first].reshape(rows, -1), rest.transpose(2, 0, 1, 3).reshape(-1, rows, 6 * first)
-
-
 def layer(
-    tokens, low, mask, gain_one, gain_two, gain_out, bias, start,
-    w_query, w_key, w_value, w_gate, w_low_in, w_low_out, w_out, own_piece, other_piece,
+    tokens, cotangent, lengths, gain_one, gain_two, gain_out, bias, start,
+    w_query, w_key, w_value, w_gate, w_low_in, w_low_out, w_out, w_mlp,
 ):
     own, width = tokens.shape
     length = 2 * own
     keys, values, heads = w_query.shape[1], w_value.shape[1], start.shape[0]
-    rank = w_low_in.shape[1]
-    piece_zero, pieces = chunked(own_piece, 128)
-    other_zero, others = chunked(other_piece, 128)
-    count = pieces.shape[0] + 1
-    group = 2 * piece_zero.shape[0]
+    rank = w_low_in.shape[0]
+    count = (w_mlp.shape[1] // 6 - 128) // 256 + 1
+    group = 2 * w_mlp.shape[0]
     tiles = length // ROWS
     first_step = tiles + 1
     steps = first_step + count
@@ -667,10 +703,10 @@
         functools.partial(layer_kernel, count),
         grid=(steps,),
         in_specs=[
-            ANY, ANY, whole(mask.shape), whole((1, width)), whole((1, width)), whole((1, VALUE_HEAD)),
+            ANY, ANY, pl.BlockSpec(memory_space=pltpu.SMEM), whole((1, width)), whole((1, width)), whole((1, VALUE_HEAD)),
             whole((1, keys)), whole(start.shape), whole(w_query.shape), whole(w_key.shape), whole(w_value.shape),
             whole(w_gate.shape), whole(w_low_in.shape), whole(w_low_out.shape), whole(w_out.shape),
-            ANY, ANY, ANY, ANY,
+            ANY,
         ],
         out_specs=[rows_spec(columns) for columns, _ in row_shapes]
         + [
@@ -711,8 +747,10 @@
             pltpu.VMEM((heads, KEY_HEAD, VALUE_HEAD), F32),
             pltpu.SemaphoreType.DMA((tiles,)),
             pltpu.SemaphoreType.DMA((count,)),
-            pltpu.SemaphoreType.DMA((count, 8)),
-            pltpu.SemaphoreType.DMA((count, 8)),
+            pltpu.SemaphoreType.DMA((count,)),
+            pltpu.SemaphoreType.DMA((count,)),
+            pltpu.SemaphoreType.DMA((2 * count - 1, 7)),
+            pltpu.SemaphoreType.DMA((2 * count - 1, 7)),
             pltpu.SemaphoreType.DMA((12,)),
             pltpu.SemaphoreType.DMA((12,)),
         ],
@@ -721,9 +759,9 @@
         ),
         name="layer",
     )(
-        tokens, low, mask, gain_one.reshape(1, -1), gain_two.reshape(1, -1), gain_out.reshape(1, -1),
+        tokens, cotangent, lengths, gain_one.reshape(1, -1), gain_two.reshape(1, -1), gain_out.reshape(1, -1),
         bias.reshape(1, -1), start, w_query, w_key, w_value, w_gate, w_low_in, w_low_out, w_out,
-        piece_zero, pieces, other_zero, others,
+        w_mlp,
     )
 
 
@@ -832,9 +870,17 @@
     count = len(order)
     rows = mlp.shape[2] // 2
 
+    loads = [0] + list(range(1, len(mlp_chunks), 2))
+    ticks = count + 6
+    slots = [(i, j) for i in range(tiles) for j in range(2)] + [(tiles + i, 0) for i in range(tiles)]
+    early = min(len(slots), len(mlp_chunks))
+    plan = {slot: (i,) for i, slot in enumerate(slots[:early])}
+
     def load(chunk):
-        source = groups_ref.at[chunk - 1] if chunk else zero_ref
-        return pltpu.make_async_copy(source, mlp.at[:, :, :, mlp_chunks[chunk]], load_sems.at[chunk])
+        if chunk == 0:
+            return pltpu.make_async_copy(zero_ref, mlp.at[:, :, :, mlp_chunks[0]], load_sems.at[0])
+        columns = slice(mlp_chunks[chunk].start, mlp_chunks[chunk + 1].stop)
+        return pltpu.make_async_copy(groups_ref.at[chunk // 2], mlp.at[:, :, :, columns], load_sems.at[chunk])
 
     def put(source, target, slot):
         send(source, target, pair_out.at[slot], pair_in.at[slot], at.sibling)
@@ -881,21 +927,26 @@
             attn_out[:, attn_chunks[chunk]] = total
 
     def tick(number):
-        if 0 <= number - 3 < count:
-            result(*order[number - 3])
-        for stage in range(2, -1, -1):
-            if 0 <= number - stage < count:
-                side, chunk = order[number - stage]
-                if stage == 0 and side == 0:
+        for stage, lag in ((3, 6), (2, 4), (1, 2), (0, 0)):
+            if 0 <= number - lag < count:
+                side, chunk = order[number - lag]
+                if stage == 3:
+                    result(side, chunk)
+                    continue
+                if stage == 0 and side == 0 and chunk in loads:
                     load(chunk).wait()
                 sides[side].stage(stage, chunk)
 
+    def ticks_at(where, inside):
+        for number in plan.get((where, inside), ()):
+            tick(number)
+
     def own_rows(i):
         return pl.ds(pl.multiple_of(i * ROWS, ROWS), ROWS)
 
     @pl.when(step == 0)
     def _():
-        for chunk in range(len(mlp_chunks)):
+        for chunk in loads:
             load(chunk).start()
         memory_grad[...] = jnp.zeros_like(memory_grad)
         gain_out_sum[...] = jnp.zeros_like(gain_out_sum)
@@ -904,12 +955,11 @@
         bias_sum[...] = jnp.zeros_like(bias_sum)
         at.meet()
 
-    early_ticks = min(len(mlp_chunks), last_step)
-    for number in range(early_ticks):
-
-        @pl.when(step == number)
+    for where in range(2 * tiles):
+
+        @pl.when(step == where)
         def _():
-            tick(number)
+            ticks_at(where, 0)
 
     @pl.when(step < tiles)
     def _():
@@ -931,6 +981,13 @@
             right[pl.ds(pl.multiple_of(tile * ROWS + i * BLOCK, BLOCK), BLOCK), :] = grads
             gain_out_sum[...] += gain_grad
             logits_parts.append(logits_grad)
+            if i == ROWS // BLOCK - 1:
+                for where in range(tiles):
+
+                    @pl.when(step == where)
+                    def _():
+                        ticks_at(where, 1)
+
         logits_grad = jnp.concatenate(logits_parts[::-1], axis=0)
         high, rest = split_low(logits_grad)
         rank_high, rank_rest = split_low(low_rank_ref[...])
@@ -944,7 +1001,7 @@
             + dot(grads[:, keys : 2 * keys], w_key[...], 1, 1)
             + dot(grads[:, 2 * keys : 2 * keys + values], w_value[...], 1, 1)
             + dot(grads[:, 2 * keys + values :], w_gate[...], 1, 1)
-            + dot(low_rank_low, w_low_in[...], 1, 1)
+            + dot(low_rank_low, w_low_in[...])
         )
         place = tile % own_tiles
         mine = tile // own_tiles == at.head
@@ -1007,20 +1064,19 @@
         attn[part, :, :, edge:] = dot(attn_turned[here, :], mixed_all[...]).astype(BF16).reshape(shape)
 
     def spread(source, head):
-        offset = 0
-        for columns in mlp_chunks:
-            size = (columns.stop - columns.start) // 3
+        offset, start = 0, 0
+        for size in [mlp_chunks[0].stop // 3] + [2 * mlp_chunks[0].stop // 3] * (len(mlp_chunks) // 2):
             for part in range(3):
-                start = columns.start + part * size
                 target = pl.ds(pl.multiple_of(part * 2 * half + head * half + offset, 128), size)
                 mlp_out[:, target] = source[:, start : start + size]
+                start += size
             offset += size
 
     @pl.when(step == last_step)
     def _():
-        for number in range(early_ticks, count + 3):
+        for number in range(early, ticks):
             tick(number)
-            if number == len(mlp_chunks) + 3:
+            if number == len(mlp_chunks) + 7:
                 spread(summed.at[pl.ds(pl.multiple_of(at.head * rows, 8), rows)], at.head)
                 for chunk, columns in enumerate(mlp_chunks):
                     wait(swapped.at[:, columns], 2 + chunk)
@@ -1043,13 +1099,14 @@
     own = tokens.shape[0]
     tiles = length // ROWS
     rows = width // 16
-    mlp_count = groups.shape[0] + 1
-    edges = [0] + [zero.shape[-1] + i * groups.shape[-1] for i in range(mlp_count)]
-    mlp_chunks = [slice(edges[i], edges[i + 1]) for i in range(mlp_count)]
-    mlp_width = edges[-1]
+    mlp_count = 2 * groups.shape[0] + 1
+    mlp_width = zero.shape[-1] * mlp_count
+    mlp_chunks = chunk_columns(mlp_width, [zero.shape[-1] // 128] * mlp_count)
     attn_width = 2 * keys + 3 * values
-    attn_count = 4
-    attn_chunks = chunk_columns(attn_width, [attn_width // 128 // attn_count] * attn_count)
+    attn_tiles = attn_width // 128
+    sizes = [3] * ((attn_tiles - 4) // 3) + [(attn_tiles - 4) % 3 + 1, 2, 1]
+    attn_chunks = chunk_columns(attn_width, sizes)
+    attn_count = len(attn_chunks)
     small_shape = (small_rows(width, rank, keys)[2], 128)
     vmem = pl.BlockSpec(memory_space=pltpu.VMEM)
 
@@ -1120,6 +1177,77 @@
     )(zero, groups, *streamed, states, *constant)
 
 
+def emit_kernel(
+    half, edges, mlp_ref, attn_ref, small_ref, tokens_ref, output_ref,
+    output_out, tokens_out, gain_one_out, query_out, key_out, value_out, gate_out, low_in_out, low_out_out, bias_out,
+    gain_out_out, out_out, gain_two_out, mlp_out, tokens, output, mlp, attn, load_sems, sems,
+):
+    staged = [(attn_ref, attn), (mlp_ref, mlp), (output_ref, output), (tokens_ref, tokens)]
+    loads = [pltpu.make_async_copy(source, target, load_sems.at[i]) for i, (source, target) in enumerate(staged)]
+    for load in loads:
+        load.start()
+    moves = []
+    for i, target in enumerate((query_out, key_out, value_out, gate_out, out_out)):
+        moves.append((attn.at[:, edges[i] : edges[i + 1]], target))
+    moves += [(mlp, mlp_out), (output, output_out), (tokens, tokens_out)]
+    copies = [pltpu.make_async_copy(source, target, sems.at[i]) for i, (source, target) in enumerate(moves)]
+    for i, load in enumerate(loads):
+        load.wait()
+        for copy in copies[:5] if i == 0 else copies[4 + i : 5 + i]:
+            copy.start()
+    rank, width = low_in_out.shape
+    keys = low_out_out.shape[1]
+    decay_at, decay_slot, _ = small_rows(width, rank, keys)
+    for i in range(width // 128):
+        columns = slice(i * 128, (i + 1) * 128)
+        gain_one_out[:, columns] = small_ref[GAIN_ONE + i : GAIN_ONE + i + 1, :]
+        gain_two_out[:, columns] = small_ref[GAIN_TWO + i : GAIN_TWO + i + 1, :]
+        low_in_out[:, columns] = small_ref[LOW_IN + i * rank : LOW_IN + (i + 1) * rank, :]
+    for i in range(VALUE_HEAD // 128):
+        gain_out_out[:, i * 128 : (i + 1) * 128] = small_ref[GAIN_OUT + i : GAIN_OUT + i + 1, :]
+    for head in range(2):
+
+        @pl.when(lax.axis_index("head") == head)
+        def _():
+            base = decay_at + head * decay_slot
+            for i in range(keys // 128):
+                columns = slice(i * 128, (i + 1) * 128)
+                low_out_out[:, columns] = small_ref[base + i * rank : base + (i + 1) * rank, :]
+                bias_at = base + keys // 128 * rank + i
+                bias_out[:, columns] = small_ref[bias_at : bias_at + 1, :]
+
+    for copy in copies:
+        copy.wait()
+
+
+def emit(mlp, attn, small, tokens, output, keys, values, rank):
+    rows, width = attn.shape[0], tokens.shape[1]
+    edges = [0, keys, 2 * keys, 2 * keys + values, 2 * keys + 2 * values, 2 * keys + 3 * values]
+    vmem = pl.BlockSpec(memory_space=pltpu.VMEM)
+    shapes = [
+        (output.shape, BF16, ANY), (tokens.shape, F32, ANY), ((1, width), F32, vmem), ((rows, keys), F32, ANY),
+        ((rows, keys), F32, ANY), ((rows, values), F32, ANY), ((rows, values), F32, ANY), ((rank, width), F32, vmem),
+        ((rank, keys), F32, vmem), ((1, keys), F32, vmem), ((1, VALUE_HEAD), F32, vmem), ((rows, values), F32, ANY),
+        ((1, width), F32, vmem), (mlp.shape, F32, ANY),
+    ]
+    return pl.pallas_call(
+        functools.partial(emit_kernel, mlp.shape[1] // 6, edges),
+        in_specs=[ANY, ANY, vmem, ANY, ANY],
+        out_specs=[space for _, _, space in shapes],
+        out_shape=[jax.ShapeDtypeStruct(shape, kind) for shape, kind, _ in shapes],
+        scratch_shapes=[
+            pltpu.VMEM(tokens.shape, F32),
+            pltpu.VMEM(output.shape, BF16),
+            pltpu.VMEM(mlp.shape, F32),
+            pltpu.VMEM(attn.shape, F32),
+            pltpu.SemaphoreType.DMA((4,)),
+            pltpu.SemaphoreType.DMA((8,)),
+        ],
+        compiler_params=pltpu.CompilerParams(vmem_limit_bytes=60 << 20),
+        name="emit",
+    )(mlp, attn, small, tokens, output)
+
+
 def swap(value):
     return lax.ppermute(value, "head", [(0, 1), (1, 0)])
 
@@ -1158,149 +1286,145 @@
     shard_rows = w_mlp.shape[0]
     square = lax.axis_size("dp") == 16
 
-    pieces = w_mlp.reshape(shard_rows, 3, 2, half)
-    own_piece = lax.dynamic_index_in_dim(pieces, here, 2, keepdims=False)
-    other_piece = lax.dynamic_index_in_dim(pieces, 1 - here, 2, keepdims=False)
     tokens_own = tokens[0]
-    positions = here * own_rows + lax.iota(jnp.int32, own_rows)
-    row_mask = (positions < lengths[0]).astype(F32)[:, None]
-    resid_grad = row_mask * cotangent[0].astype(F32)
-    low_own = resid_grad.astype(BF16)
     if square:
         (
             h_low, query, key, value, gate, logits, low_rank, attended, mixed, states,
             grad_zero, grad_mlp, output, resid_total, attn_low, gain_two_grad,
         ) = layer(
-            tokens_own, low_own, row_mask, norm_attn_gain, norm_mlp_gain, out_gain, decay_bias, initial_memory[0],
-            w_query, w_key, w_value, w_gate_out, w_low_in, w_low_out, w_out, own_piece, other_piece,
+            tokens_own, cotangent[0], lengths, norm_attn_gain, norm_mlp_gain, out_gain, decay_bias,
+            initial_memory[0], w_query, w_key, w_value, w_gate_out, w_low_in.T, w_low_out, w_out, w_mlp,
         )
         grad_mlp, attn_grads, packed, tokens_grad = backward(
             grad_zero, grad_mlp, attn_low, h_low, query, key, value, gate, logits, low_rank, attended, mixed, states,
-            w_query, w_key, w_value, w_gate_out, w_low_in, w_low_out, w_out, tokens_own, resid_total,
+            w_query, w_key, w_value, w_gate_out, w_low_in.T, w_low_out, w_out, tokens_own, resid_total,
             norm_attn_gain, out_gain, gain_two_grad,
         )
-        output = output[None]
-        rank = w_low_out.shape[0]
-        model = tokens_own.shape[1]
-        decay_at, decay_slot, _ = small_rows(model, rank, keys)
-        gain_one_grad = packed[GAIN_ONE : GAIN_ONE + model // 128].reshape(-1)
-        gain_two_grad = packed[GAIN_TWO : GAIN_TWO + model // 128].reshape(-1)
-        out_gain_grad = packed[GAIN_OUT : GAIN_OUT + VALUE_HEAD // 128].reshape(-1)
-        low_in_grad = packed[LOW_IN:decay_at].reshape(-1, rank, 128).transpose(0, 2, 1).reshape(model, rank)
-        decay_part = lax.dynamic_slice_in_dim(packed, decay_at + here * decay_slot, decay_slot, 0)
-        edge = keys // 128 * rank
-        low_out_grad = decay_part[:edge].reshape(-1, rank, 128).transpose(1, 0, 2).reshape(rank, keys)
-        bias_grad = decay_part[edge : edge + keys // 128].reshape(-1)
-    else:
-        pair = swap(other_piece.reshape(shard_rows, 3 * half))
-        weights = lax.all_gather(
-            ordered(own_piece.reshape(shard_rows, 3 * half), pair, 0), "dp", axis=0, tiled=True
+        results = emit(grad_mlp, attn_grads, packed, tokens_grad, output, keys, values, w_low_out.shape[0])
+        (
+            output, tokens_grad, gain_one_grad, query_grad, key_grad, value_grad, gate_grad, low_in_grad, low_out_grad,
+            bias_grad, out_gain_grad, out_grad, gain_two_grad, grad_mlp,
+        ) = results
+        return (
+            output[None], tokens_grad[None], gain_one_grad[0], query_grad, key_grad, value_grad, gate_grad,
+            low_in_grad.T, low_out_grad, bias_grad[0], out_gain_grad[0], out_grad.T, gain_two_grad[0], grad_mlp,
         )
-        tokens_wide = ordered(tokens_own, swap(tokens_own), 0).astype(F32)
-        length = tokens_wide.shape[0]
-        scale_one = lax.rsqrt(jnp.mean(tokens_wide * tokens_wide, axis=1, keepdims=True) + EPSILON)
-        h_low = (tokens_wide * scale_one * norm_attn_gain).astype(BF16)
-        query = dot(h_low, w_query).astype(BF16)
-        key = dot(h_low, w_key).astype(BF16)
-        value = dot(h_low, w_value).astype(BF16)
-        gate = dot(h_low, w_gate_out)
-        low_rank = dot(h_low, w_low_in)
-        low_high, low_rest = split_low(low_rank)
-        logits = dot(low_high, w_low_out) + dot(low_rest, w_low_out) + decay_bias
-        attended, mixed, states = attention_forward(query, key, value, logits, gate, out_gain, initial_memory[0])
-        resid = tokens_own.astype(F32) + sum_rows(dot(mixed, w_out), here)
-        scale_two = lax.rsqrt(jnp.mean(resid * resid, axis=1, keepdims=True) + EPSILON)
-        normal_two = resid * scale_two
-        h_two_own = (normal_two * norm_mlp_gain).astype(BF16)
-        h_two = ordered(h_two_own, swap(h_two_own), 0)
-        resid_low = ordered(low_own, swap(low_own), 0)
-        pre_gate = dot(h_two, weights[:, :half])
-        up_part = dot(h_two, weights[:, half : 2 * half])
-        pre_sigmoid = sigmoid(pre_gate)
-        inner = (pre_gate * pre_sigmoid * up_part).astype(BF16)
-        inner_grad = dot(resid_low, weights[:, 2 * half :])
-        pre_grad = (
-            inner_grad * up_part * pre_sigmoid * (1.0 + pre_gate * (1.0 - pre_sigmoid))
-        ).astype(BF16)
-        up_grad = (inner_grad * pre_gate * pre_sigmoid).astype(BF16)
-        mlp_out = sum_rows(dot(inner, weights[:, 2 * half :], 1, 1), here)
-        output = (row_mask * (resid + mlp_out)).astype(BF16)[None]
-        h_two_grad = sum_rows(
-            dot(pre_grad, weights[:, :half], 1, 1) + dot(up_grad, weights[:, half : 2 * half], 1, 1), here
-        )
-        grad_mlp = jnp.concatenate(
-            [
-                dot(h_two, pre_grad, 0, 0).astype(BF16),
-                dot(h_two, up_grad, 0, 0).astype(BF16),
-                dot(resid_low, inner, 0, 0).astype(BF16),
-            ],
-            axis=1,
-        )
-        resid_total = resid_grad + norm_backward(h_two_grad, norm_mlp_gain, normal_two, scale_two)
-        gain_two_grad = jnp.sum(h_two_grad * normal_two, axis=0)
-        attn_own = resid_total.astype(BF16)
-        attn_low = ordered(attn_own, swap(attn_own), 0)
-
-        mixed_grad = dot(attn_low, w_out, 1, 1)
-        out_grad = dot(attn_low, mixed, 0, 0)
-        query_grad, key_grad, value_grad, gate_grad, logits_grad, out_gain_grad = attention_backward(
-            mixed_grad, query, key, value, logits, gate, attended, states, out_gain
-        )
-        bias_grad = jnp.sum(logits_grad, axis=0)
-        grad_high, grad_rest = split_low(logits_grad)
-        low_out_grad = (
-            dot(low_high, grad_high, 0, 0) + dot(low_rest, grad_high, 0, 0) + dot(low_high, grad_rest, 0, 0)
-        )
-        low_rank_low = (dot(grad_high, w_low_out, 1, 1) + dot(grad_rest, w_low_out, 1, 1)).astype(BF16)
-        low_in_grad = dot(h_low, low_rank_low, 0, 0)
-        attn_grads = jnp.concatenate(
-            [
-                dot(h_low, query_grad, 0, 0).astype(BF16),
-                dot(h_low, key_grad, 0, 0).astype(BF16),
-                dot(h_low, value_grad, 0, 0).astype(BF16),
-                dot(h_low, gate_grad, 0, 0).astype(BF16),
-                out_grad.astype(BF16),
-            ],
-            axis=1,
-        )
-        h_grad = sum_rows(
-            dot(query_grad, w_query, 1, 1)
-            + dot(key_grad, w_key, 1, 1)
-            + dot(value_grad, w_value, 1, 1)
-            + dot(gate_grad, w_gate_out, 1, 1)
-            + dot(low_rank_low, w_low_in, 1, 1),
-            here,
-        )
-        own_wide = tokens_own.astype(F32)
-        own_scale = lax.rsqrt(jnp.mean(own_wide * own_wide, axis=1, keepdims=True) + EPSILON)
-        normal_own = own_wide * own_scale
-        tokens_grad = resid_total + norm_backward(h_grad, norm_attn_gain, normal_own, own_scale)
-        gain_one_grad = jnp.sum(h_grad * normal_own, axis=0)
-        low_rank_width = w_low_out.shape[0]
-        decay_part = jnp.concatenate([low_out_grad, bias_grad[None]], axis=0)
-        slots = jnp.zeros((2,) + decay_part.shape, F32)
-        slots = lax.dynamic_update_slice(slots, decay_part[None], (here, 0, 0))
-        packed = jnp.concatenate(
-            [
-                gain_one_grad, gain_two_grad, out_gain_grad.reshape(-1), low_in_grad.reshape(-1), slots.reshape(-1),
-            ]
-        )
-        packed = lax.psum(packed, ("dp", "head"))
-        attn_grads = lax.psum_scatter(attn_grads, "dp", scatter_dimension=0, tiled=True).astype(F32)
-        grad_mlp = lax.psum_scatter(grad_mlp, "dp", scatter_dimension=0, tiled=True)
-        own_half = half_of(grad_mlp, here, 0)
-        other_half = swap(half_of(grad_mlp, 1 - here, 0))
-        grad_mlp = ordered(
-            own_half.reshape(shard_rows, 3, 1, half), other_half.reshape(shard_rows, 3, 1, half), 2
-        ).reshape(shard_rows, 3 * hidden).astype(F32)
-        width = gain_one_grad.shape[0]
-        edges = [width, 2 * width, 2 * width + VALUE_HEAD]
-        edges.append(edges[-1] + width * low_rank_width)
-        low_in_grad = packed[edges[2] : edges[3]].reshape(width, low_rank_width)
-        decay_part = lax.dynamic_index_in_dim(packed[edges[3] :].reshape(slots.shape), here, 0, keepdims=False)
-        low_out_grad, bias_grad = decay_part[:low_rank_width], decay_part[low_rank_width]
-        gain_one_grad, gain_two_grad = packed[: edges[0]], packed[edges[0] : edges[1]]
-        out_gain_grad = packed[edges[1] : edges[2]]
+    pieces = w_mlp.reshape(shard_rows, 3, 2, half)
+    own_piece = lax.dynamic_index_in_dim(pieces, here, 2, keepdims=False)
+    other_piece = lax.dynamic_index_in_dim(pieces, 1 - here, 2, keepdims=False)
+    positions = here * own_rows + lax.iota(jnp.int32, own_rows)
+    row_mask = (positions < lengths[0]).astype(F32)[:, None]
+    resid_grad = row_mask * cotangent[0].astype(F32)
+    low_own = resid_grad.astype(BF16)
+    pair = swap(other_piece.reshape(shard_rows, 3 * half))
+    weights = lax.all_gather(
+        ordered(own_piece.reshape(shard_rows, 3 * half), pair, 0), "dp", axis=0, tiled=True
+    )
+    tokens_wide = ordered(tokens_own, swap(tokens_own), 0).astype(F32)
+    length = tokens_wide.shape[0]
+    scale_one = lax.rsqrt(jnp.mean(tokens_wide * tokens_wide, axis=1, keepdims=True) + EPSILON)
+    h_low = (tokens_wide * scale_one * norm_attn_gain).astype(BF16)
+    query = dot(h_low, w_query).astype(BF16)
+    key = dot(h_low, w_key).astype(BF16)
+    value = dot(h_low, w_value).astype(BF16)
+    gate = dot(h_low, w_gate_out)
+    low_rank = dot(h_low, w_low_in)
+    low_high, low_rest = split_low(low_rank)
+    logits = dot(low_high, w_low_out) + dot(low_rest, w_low_out) + decay_bias
+    attended, mixed, states = attention_forward(query, key, value, logits, gate, out_gain, initial_memory[0])
+    resid = tokens_own.astype(F32) + sum_rows(dot(mixed, w_out), here)
+    scale_two = lax.rsqrt(jnp.mean(resid * resid, axis=1, keepdims=True) + EPSILON)
+    normal_two = resid * scale_two
+    h_two_own = (normal_two * norm_mlp_gain).astype(BF16)
+    h_two = ordered(h_two_own, swap(h_two_own), 0)
+    resid_low = ordered(low_own, swap(low_own), 0)
+    pre_gate = dot(h_two, weights[:, :half])
+    up_part = dot(h_two, weights[:, half : 2 * half])
+    pre_sigmoid = sigmoid(pre_gate)
+    inner = (pre_gate * pre_sigmoid * up_part).astype(BF16)
+    inner_grad = dot(resid_low, weights[:, 2 * half :])
+    pre_grad = (
+        inner_grad * up_part * pre_sigmoid * (1.0 + pre_gate * (1.0 - pre_sigmoid))
+    ).astype(BF16)
+    up_grad = (inner_grad * pre_gate * pre_sigmoid).astype(BF16)
+    mlp_out = sum_rows(dot(inner, weights[:, 2 * half :], 1, 1), here)
+    output = (row_mask * (resid + mlp_out)).astype(BF16)[None]
+    h_two_grad = sum_rows(
+        dot(pre_grad, weights[:, :half], 1, 1) + dot(up_grad, weights[:, half : 2 * half], 1, 1), here
+    )
+    grad_mlp = jnp.concatenate(
+        [
+            dot(h_two, pre_grad, 0, 0).astype(BF16),
+            dot(h_two, up_grad, 0, 0).astype(BF16),
+            dot(resid_low, inner, 0, 0).astype(BF16),
+        ],
+        axis=1,
+    )
+    resid_total = resid_grad + norm_backward(h_two_grad, norm_mlp_gain, normal_two, scale_two)
+    gain_two_grad = jnp.sum(h_two_grad * normal_two, axis=0)
+    attn_own = resid_total.astype(BF16)
+    attn_low = ordered(attn_own, swap(attn_own), 0)
+
+    mixed_grad = dot(attn_low, w_out, 1, 1)
+    out_grad = dot(attn_low, mixed, 0, 0)
+    query_grad, key_grad, value_grad, gate_grad, logits_grad, out_gain_grad = attention_backward(
+        mixed_grad, query, key, value, logits, gate, attended, states, out_gain
+    )
+    bias_grad = jnp.sum(logits_grad, axis=0)
+    grad_high, grad_rest = split_low(logits_grad)
+    low_out_grad = (
+        dot(low_high, grad_high, 0, 0) + dot(low_rest, grad_high, 0, 0) + dot(low_high, grad_rest, 0, 0)
+    )
+    low_rank_low = (dot(grad_high, w_low_out, 1, 1) + dot(grad_rest, w_low_out, 1, 1)).astype(BF16)
+    low_in_grad = dot(h_low, low_rank_low, 0, 0)
+    attn_grads = jnp.concatenate(
+        [
+            dot(h_low, query_grad, 0, 0).astype(BF16),
+            dot(h_low, key_grad, 0, 0).astype(BF16),
+            dot(h_low, value_grad, 0, 0).astype(BF16),
+            dot(h_low, gate_grad, 0, 0).astype(BF16),
+            out_grad.astype(BF16),
+        ],
+        axis=1,
+    )
+    h_grad = sum_rows(
+        dot(query_grad, w_query, 1, 1)
+        + dot(key_grad, w_key, 1, 1)
+        + dot(value_grad, w_value, 1, 1)
+        + dot(gate_grad, w_gate_out, 1, 1)
+        + dot(low_rank_low, w_low_in, 1, 1),
+        here,
+    )
+    own_wide = tokens_own.astype(F32)
+    own_scale = lax.rsqrt(jnp.mean(own_wide * own_wide, axis=1, keepdims=True) + EPSILON)
+    normal_own = own_wide * own_scale
+    tokens_grad = resid_total + norm_backward(h_grad, norm_attn_gain, normal_own, own_scale)
+    gain_one_grad = jnp.sum(h_grad * normal_own, axis=0)
+    low_rank_width = w_low_out.shape[0]
+    decay_part = jnp.concatenate([low_out_grad, bias_grad[None]], axis=0)
+    slots = jnp.zeros((2,) + decay_part.shape, F32)
+    slots = lax.dynamic_update_slice(slots, decay_part[None], (here, 0, 0))
+    packed = jnp.concatenate(
+        [
+            gain_one_grad, gain_two_grad, out_gain_grad.reshape(-1), low_in_grad.reshape(-1), slots.reshape(-1),
+        ]
+    )
+    packed = lax.psum(packed, ("dp", "head"))
+    attn_grads = lax.psum_scatter(attn_grads, "dp", scatter_dimension=0, tiled=True).astype(F32)
+    grad_mlp = lax.psum_scatter(grad_mlp, "dp", scatter_dimension=0, tiled=True)
+    own_half = half_of(grad_mlp, here, 0)
+    other_half = swap(half_of(grad_mlp, 1 - here, 0))
+    grad_mlp = ordered(
+        own_half.reshape(shard_rows, 3, 1, half), other_half.reshape(shard_rows, 3, 1, half), 2
+    ).reshape(shard_rows, 3 * hidden).astype(F32)
+    width = gain_one_grad.shape[0]
+    edges = [width, 2 * width, 2 * width + VALUE_HEAD]
+    edges.append(edges[-1] + width * low_rank_width)
+    low_in_grad = packed[edges[2] : edges[3]].reshape(width, low_rank_width)
+    decay_part = lax.dynamic_index_in_dim(packed[edges[3] :].reshape(slots.shape), here, 0, keepdims=False)
+    low_out_grad, bias_grad = decay_part[:low_rank_width], decay_part[low_rank_width]
+    gain_one_grad, gain_two_grad = packed[: edges[0]], packed[edges[0] : edges[1]]
+    out_gain_grad = packed[edges[1] : edges[2]]
     return (
         output,
         tokens_grad[None],

time: 299 us -> 251 us (0.84)
  Pallas kernels: 273 us -> 249 us
  local copies, waits for them, and re-layouts: 20.5 us -> 0 us
  other arithmetic: 3.18 us -> 0 us
    pallas_call x1, Pallas kernels: 127 us -> 107 us  [layer(): pl.pallas_call(functools.partial(layer_kernel, count), grid=(steps,), in_...]
    pallas_call x1, Pallas kernels: 147 us -> 136 us  [backward(): pl.pallas_call(functools.partial(backward_kernel, mlp_width // 3, mlp_chu...]
    reshape x11 -> x0, local copies, waits for them, and re-layouts: 7.82 us -> none  [the longest x2 1.95 us: chunked(): rest.transpose(2, 0, 1, 3).reshape(-1, rows, 6 * first)]
    unnamed x12 -> x0, local copies, waits for them, and re-layouts: 6.09 us -> none
    pallas_call x0 -> x1, Pallas kernels: none -> 6.07 us  [emit(): pl.pallas_call(functools.partial(emit_kernel, mlp.shape[1] // 6, edges),...]
    convert_element_type x3 -> x0, other arithmetic: 3.18 us -> none  [the longest x1 2.43 us: per_device(): low_own = resid_grad.astype(BF16)]
    slice x5 -> x0, local copies, waits for them, and re-layouts: 3.12 us -> none  [the longest x1 1.53 us: per_device(): attn_grads[:, keys:2 * keys]]
where the time goes in v5:
time: 251 us
  Pallas kernels  249 us (99%)
    pallas_call x1, Pallas kernels, backward(): pl.pallas_call(functools.partial(backward_kernel, mlp_width // 3, mlp_chu...  136 us
    pallas_call x1, Pallas kernels, layer(): pl.pallas_call(functools.partial(layer_kernel, count), grid=(steps,), in_...  107 us
    pallas_call x1, Pallas kernels, emit(): pl.pallas_call(functools.partial(emit_kernel, mlp.shape[1] // 6, edges),...  6.07 us

profile of v5, /device:TPU:0, one launch (start us, length us, event | category | flops | bytes accessed | tf_op | source)
XLA Modules:
  0.0 250.7 jit_solution(5614466002409554192)
XLA Ops:
  1.3 106.7 %layer.1 = (bf16[1024,1024]{1,0:T(8,128)(2,1)}, bf16[1024,256]{1,0:T(8,128)(2,1)}, bf16[1024,256]{1,0:T(8,128)(2,1)}, bf16[1024,512]{1,0:T(8,128)(2,1)}, f32[102...) custom-call(bf16[512,1024]{1,0:T(8,128)(2,1)} %bitcast.16, ...), custom_call_target="tpu_custom_call" | custom-call | tf_op jit(solution)/shard_map/layer/pallas_call | solution.py:702
  108.0 136.5 %backward.1 = (f32[32,8448]{1,0:T(8,128)}, f32[64,2048]{1,0:T(8,128)}, f32[232,128]{1,0:T(8,128)}, f32[512,1024]{1,0:T(8,128)}) custom-call(bf16[4,4,64,384]{3,2,1,0:T(8,128)(2,1)} %get-tuple-element.48.zero_ref, bf16[5,4,4,64,768]{4,3,2,1,0:T(8,128)(2,1)} %get-tuple-element.49.groups_ref, bf16[1024,1024]{1,0:T(8,128)(2,1)} %get-tuple-element.50.attn_ref, ...), custom_call_target="tpu_custom_call" | custom-call | tf_op jit(solution)/shard_map/backward/pallas_call | solution.py:1124
  244.5 6.1 %emit.1 = (bf16[512,1024]{1,0:T(8,128)(2,1)}, f32[512,1024]{1,0:T(8,128)}, f32[1,1024]{1,0:T(1,128)}, f32[64,256]{1,0:T(8,128)}, f32[64,256]{1,0:T(8,128)}, /*in...) custom-call(f32[32,8448]{1,0:T(8,128)} %get-tuple-element.63.mlp_ref, ...), custom_call_target="tpu_custom_call" | custom-call | tf_op jit(solution)/shard_map/emit/pallas_call | solution.py:1233

commit v6 on v5

--- a/solution.py
+++ b/solution.py
@@ -320,6 +320,7 @@
 
 
 ROWS = 256
+SMALL_TICKS = (0, 2, 5, 8)
 
 
 class Gather:
@@ -341,7 +342,6 @@
         at, source = self.place, self.source
         rows, half = source.shape[0], source.shape[1] // 6
         mine = pl.ds(at.head * rows, rows)
-        theirs = pl.ds((1 - at.head) * rows, rows)
         offset = 0
         for i, block in enumerate(self.targets):
             size = block.shape[3] // 3
@@ -353,15 +353,20 @@
                 pltpu.make_async_copy(source.at[:, here], target, self.local_sems.at[i]).start()
                 send(source.at[:, there], target, self.swap_out.at[i], self.swap_in.at[i], at.sibling)
             offset += size
-        for i, block in enumerate(self.targets):
-            target = block.at[at.z, at.flat, mine]
-            pltpu.make_async_copy(target, target, self.local_sems.at[i]).wait()
-            arrived(block.at[at.z, at.flat, theirs], self.swap_out.at[i], self.swap_in.at[i], at.sibling)
+    def pair_ready(self, i):
+        at, block = self.place, self.targets[i]
+        rows = self.source.shape[0]
+        target = block.at[at.z, at.flat, pl.ds(at.head * rows, rows)]
+        pltpu.make_async_copy(target, target, self.local_sems.at[i]).wait()
+        theirs = pl.ds((1 - at.head) * rows, rows)
+        arrived(block.at[at.z, at.flat, theirs], self.swap_out.at[i], self.swap_in.at[i], at.sibling)
 
     def stage(self, number, chunk):
         at, out = self.place, self.blocks[chunk]
         everything = slice(None)
         if number == 0:
+            if chunk % 2 == 0:
+                self.pair_ready(chunk // 2)
             block = out.at[at.z, at.flat]
             for i in range(3):
                 self.put(block, block, chunk, i, at.along_z[i])
@@ -427,13 +432,13 @@
     gather = Gather(
         at,
         w_mlp,
-        [weights_zero] + [weights.at[i] for i in range(count - 1)],
-        [weights_zero]
-        + [weights.at[i, :, :, :, j * 384 : (j + 1) * 384] for i in range(count - 1) for j in range(2)],
+        [weights.at[i] for i in range(count - 1)] + [weights_zero],
+        [weights.at[i, :, :, :, j * 384 : (j + 1) * 384] for i in range(count - 1) for j in range(2)]
+        + [weights_zero],
         gather_local, swap_out, swap_in, gather_out, gather_in,
     )
     plan = {(0, 0): (0, 1), (1, 0): (2,), (2, 0): (3,), (3, 0): (4,), (4, 0): (5,), (4, 1): (6,)}
-    places = [(5, 1), (6, 0), (6, 1), (7, 1), (8, 0), (8, 1), (9, 1)]
+    places = [(5, 0), (5, 1), (6, 1), (7, 0), (7, 1), (8, 1), (9, 1)]
     for i, key in enumerate(places):
         plan[key] = (7 + i,) if i < len(places) - 1 else tuple(range(7 + i, gather.ticks))
     attention_steps = tiles
@@ -559,11 +564,12 @@
 
         lax.fori_loop(0, tiles, turn_two, 0)
 
-    def hidden_rows(block, first):
+    def hidden_rows(block, first, last=False):
         width = block.shape[3] // 3
 
         def body(i, carry):
-            rows = pl.ds(pl.multiple_of(i * ROWS, ROWS), ROWS)
+            tile = (i + own_tiles * (1 - at.head)) % tiles if last else i
+            rows = pl.ds(pl.multiple_of(tile * ROWS, ROWS), ROWS)
             w_pair = block[:, :, :, : 2 * width].reshape(-1, 2 * width)
             w_down = block[:, :, :, 2 * width :].reshape(-1, width)
             pair = dot(h_two[rows, :], w_pair)
@@ -585,6 +591,15 @@
             else:
                 mlp_sum[rows, :] += out_part
                 grad_sum[rows, :] += grad_part
+            if last:
+
+                @pl.when(i < own_tiles)
+                def _():
+                    there = pl.ds(pl.multiple_of(i * ROWS, ROWS), ROWS)
+                    for k, source in enumerate((mlp_sum, grad_sum)):
+                        sums_out[k, there, :] = source[rows, :].astype(BF16)
+                        put(sums_out.at[k, there], sums_in.at[k, there], 6 + 2 * i + k)
+
             return carry
 
         lax.fori_loop(0, tiles, body, 0)
@@ -605,36 +620,31 @@
 
         lax.fori_loop(0, tiles, body, 0)
 
-    @pl.when(step == first_step)
-    def _():
-        gather.complete(0)
-        hidden_rows(weights_zero, True)
-        gather_at(1, [first_step])
-        weight_rows(weights_zero, grad_zero_ref)
-
-    for group in range(1, count):
+    for group in range(count):
 
         @pl.when(step == first_step + group)
         def _():
             gather_at(0, [first_step + group])
-            gather.complete(2 * group - 1)
             gather.complete(2 * group)
-
-    @pl.when(step > first_step)
+            if group < count - 1:
+                gather.complete(2 * group + 1)
+
+    @pl.when(step == first_step)
     def _():
-        block = weights.at[step - first_step - 1]
+        hidden_rows(weights.at[0], True)
+        gather_at(1, [first_step])
+        weight_rows(weights.at[0], grad_ref.at[0])
+
+    @pl.when(jnp.logical_and(step > first_step, step < last_step))
+    def _():
+        block = weights.at[step - first_step]
         hidden_rows(block, False)
         gather_at(1, range(first_step + 1, last_step))
-
-        @pl.when(step == last_step)
-        def _():
-            for i in range(own_tiles):
-                rows = pl.ds(i * ROWS, ROWS)
-                for k, source in enumerate((mlp_sum, grad_sum)):
-                    sums_out[k, rows, :] = source[other_rows(i), :].astype(BF16)
-                    put(sums_out.at[k, rows], sums_in.at[k, rows], 6 + 2 * i + k)
-
         weight_rows(block, grad_ref.at[0])
+
+    @pl.when(step == last_step)
+    def _():
+        hidden_rows(weights_zero, False, True)
 
     @pl.when(step == last_step)
     def _():
@@ -656,6 +666,7 @@
             h_two[own_rows(i), :] = total.astype(BF16)
             put(h_two.at[own_rows(i)], h_two.at[own_rows(i)], 10 + i)
             pltpu.make_async_copy(h_two.at[own_rows(i)], attn_ref.at[own_rows(i)], local_sems.at[i]).start()
+        weight_rows(weights_zero, grad_zero_ref)
         gather.finish()
         for i in range(own_tiles):
             wait(h_two.at[other_rows(i)], 10 + i)
@@ -713,7 +724,7 @@
             pl.BlockSpec((blocks, heads, KEY_HEAD, VALUE_HEAD), lambda i: (jnp.minimum(i, tiles - 1), 0, 0, 0)),
             whole((4, 4, group, 384)),
             pl.BlockSpec(
-                (1, 4, 4, group, 768), lambda i: (jnp.clip(i - first_step - 1, 0, count - 2), 0, 0, 0, 0)
+                (1, 4, 4, group, 768), lambda i: (jnp.clip(i - first_step, 0, count - 2), 0, 0, 0, 0)
             ),
             vmem, vmem, ANY, vmem,
         ],
@@ -835,7 +846,7 @@
 def small_rows(width, rank, keys):
     decay = LOW_IN + rank * width // 128
     slot = -(-(rank + 1) * keys // 128 // 8) * 8
-    return decay, slot, decay + 2 * slot
+    return decay, slot, -(-(decay + 2 * slot) // 16) * 16
 
 
 def backward_kernel(
@@ -870,15 +881,15 @@
     count = len(order)
     rows = mlp.shape[2] // 2
 
-    loads = [0] + list(range(1, len(mlp_chunks), 2))
+    loads = list(range(0, len(mlp_chunks), 2))
     ticks = count + 6
     slots = [(i, j) for i in range(tiles) for j in range(2)] + [(tiles + i, 0) for i in range(tiles)]
     early = min(len(slots), len(mlp_chunks))
     plan = {slot: (i,) for i, slot in enumerate(slots[:early])}
 
     def load(chunk):
-        if chunk == 0:
-            return pltpu.make_async_copy(zero_ref, mlp.at[:, :, :, mlp_chunks[0]], load_sems.at[0])
+        if chunk == len(mlp_chunks) - 1:
+            return pltpu.make_async_copy(zero_ref, mlp.at[:, :, :, mlp_chunks[chunk]], load_sems.at[chunk])
         columns = slice(mlp_chunks[chunk].start, mlp_chunks[chunk + 1].stop)
         return pltpu.make_async_copy(groups_ref.at[chunk // 2], mlp.at[:, :, :, columns], load_sems.at[chunk])
 
@@ -895,24 +906,35 @@
         def wait_small(target, slot):
             arrived(target, small_sems_out.at[slot], small_sems_in.at[slot], at.sibling)
 
+        count = small_own.shape[0] // 2
+        half = pl.ds(pl.multiple_of(at.head * count, 8), count)
+        other = pl.ds(pl.multiple_of((1 - at.head) * count, 8), count)
         if number == 0:
             put_small(small_own, small_in.at[0], 0, at.sibling)
-        elif number in (1, 2):
-            source = small_own if number == 1 else small_z.at[number - 2]
-            wait_small(small_in.at[number - 1], number - 1)
-            small_z[number - 1] = source[...] + small_in[number - 1]
-            put_small(small_z.at[number - 1], small_in.at[number], number, at.beside_x if number == 1 else at.beside_y)
+        elif number == 1:
+            wait_small(small_in.at[0], 0)
+            small_z[0, half] = small_own[half, :] + small_in[0, half]
+            put_small(small_z.at[0, half], small_in.at[1, half], 1, at.beside_x)
+        elif number == 2:
+            wait_small(small_in.at[1, half], 1)
+            small_z[1, half] = small_z[0, half] + small_in[1, half]
+            put_small(small_z.at[1, half], small_in.at[2, half], 2, at.beside_y)
         elif number == 3:
-            wait_small(small_in.at[2], 2)
-            small_z[2 + at.z] = small_z[1] + small_in[2]
+            wait_small(small_in.at[2, half], 2)
+            small_z[2 + at.z, half] = small_z[1, half] + small_in[2, half]
             for i in range(3):
-                put_small(small_z.at[2 + at.z], small_z.at[2 + at.z], 3 + i, at.along_z[i])
+                put_small(small_z.at[2 + at.z, half], small_z.at[2 + at.z, half], 3 + i, at.along_z[i])
         elif number == 4:
             for i in range(3):
-                wait_small(small_z.at[2 + (at.z + 3 - i) % 4], 3 + i)
-            small_out[...] = small_z[2] + small_z[3] + small_z[4] + small_z[5]
-            for slot in range(6):
-                sent(small_own, small_sems_out.at[slot], small_sems_in.at[slot], at.sibling)
+                wait_small(small_z.at[2 + (at.z + 3 - i) % 4, half], 3 + i)
+            small_z[6, half] = small_z[2, half] + small_z[3, half] + small_z[4, half] + small_z[5, half]
+            put_small(small_z.at[6, half], small_z.at[6, half], 6, at.sibling)
+        elif number == 5:
+            wait_small(small_z.at[6, other], 6)
+            small_out[...] = small_z[6]
+            for slot in range(7):
+                source = small_own if slot == 0 else small_z.at[0, half]
+                sent(source, small_sems_out.at[slot], small_sems_in.at[slot], at.sibling)
 
     def result(side, chunk):
         total = sides[side].result(chunk)
@@ -1048,12 +1070,6 @@
 
         small(0)
 
-    for number in range(1, 5):
-
-        @pl.when(step == tiles + number)
-        def _():
-            small(number)
-
     @pl.when(jnp.logical_and(step >= tiles, step < 2 * tiles))
     def _():
         part = step - tiles
@@ -1065,17 +1081,23 @@
 
     def spread(source, head):
         offset, start = 0, 0
-        for size in [mlp_chunks[0].stop // 3] + [2 * mlp_chunks[0].stop // 3] * (len(mlp_chunks) // 2):
+        for size in [2 * mlp_chunks[0].stop // 3] * (len(mlp_chunks) // 2) + [mlp_chunks[0].stop // 3]:
             for part in range(3):
                 target = pl.ds(pl.multiple_of(part * 2 * half + head * half + offset, 128), size)
                 mlp_out[:, target] = source[:, start : start + size]
                 start += size
             offset += size
 
+    @pl.when(step == last_step - 1)
+    def _():
+        small(1)
+
     @pl.when(step == last_step)
     def _():
         for number in range(early, ticks):
             tick(number)
+            if number - early in SMALL_TICKS:
+                small(2 + SMALL_TICKS.index(number - early))
             if number == len(mlp_chunks) + 7:
                 spread(summed.at[pl.ds(pl.multiple_of(at.head * rows, 8), rows)], at.head)
                 for chunk, columns in enumerate(mlp_chunks):
@@ -1147,7 +1169,7 @@
             pltpu.VMEM((rows // 2, mlp_width), F32),
             pltpu.VMEM(small_shape, F32),
             pltpu.VMEM((3,) + small_shape, F32),
-            pltpu.VMEM((6,) + small_shape, F32),
+            pltpu.VMEM((7,) + small_shape, F32),
             pltpu.VMEM((width, length), BF16),
             pltpu.VMEM((width, length), BF16),
             pltpu.VMEM((length, 2 * keys + 2 * values), BF16),
@@ -1167,8 +1189,8 @@
             pltpu.SemaphoreType.DMA((attn_count, 7)),
             pltpu.SemaphoreType.DMA((2 + mlp_count,)),
             pltpu.SemaphoreType.DMA((2 + mlp_count,)),
-            pltpu.SemaphoreType.DMA((6,)),
-            pltpu.SemaphoreType.DMA((6,)),
+            pltpu.SemaphoreType.DMA((7,)),
+            pltpu.SemaphoreType.DMA((7,)),
         ],
         compiler_params=pltpu.CompilerParams(
             collective_id=1, has_side_effects=True, vmem_limit_bytes=63 << 20

time: 251 us -> 239 us (0.952)
  Pallas kernels: 249 us -> 237 us
    pallas_call x1, Pallas kernels: 136 us -> 124 us  [backward(): pl.pallas_call(functools.partial(backward_kernel, mlp_width // 3, mlp_chu...]
where the time goes in v6:
time: 239 us
  Pallas kernels  237 us (99%)
    pallas_call x1, Pallas kernels, backward(): pl.pallas_call(functools.partial(backward_kernel, mlp_width // 3, mlp_chu...  124 us
    pallas_call x1, Pallas kernels, layer(): pl.pallas_call(functools.partial(layer_kernel, count), grid=(steps,), in_...  107 us
    pallas_call x1, Pallas kernels, emit(): pl.pallas_call(functools.partial(emit_kernel, mlp.shape[1] // 6, edges),...  6.07 us

profile of v6, /device:TPU:0, one launch (start us, length us, event | category | flops | bytes accessed | tf_op | source)
XLA Modules:
  0.0 238.8 jit_solution(9006593733230356261)
XLA Ops:
  1.3 107.1 %layer.1 = (bf16[1024,1024]{1,0:T(8,128)(2,1)}, bf16[1024,256]{1,0:T(8,128)(2,1)}, bf16[1024,256]{1,0:T(8,128)(2,1)}, bf16[1024,512]{1,0:T(8,128)(2,1)}, f32[102...) custom-call(bf16[512,1024]{1,0:T(8,128)(2,1)} %bitcast.16, ...), custom_call_target="tpu_custom_call" | custom-call | tf_op jit(solution)/shard_map/layer/pallas_call | solution.py:713
  108.4 124.2 %backward.1 = (f32[32,8448]{1,0:T(8,128)}, f32[64,2048]{1,0:T(8,128)}, f32[240,128]{1,0:T(8,128)}, f32[512,1024]{1,0:T(8,128)}) custom-call(bf16[4,4,64,384]{3,2,1,0:T(8,128)(2,1)} %get-tuple-element.48.zero_ref, bf16[5,4,4,64,768]{4,3,2,1,0:T(8,128)(2,1)} %get-tuple-element.49.groups_ref, bf16[1024,1024]{1,0:T(8,128)(2,1)} %get-tuple-element.50.attn_ref, ...), custom_call_target="tpu_custom_call" | custom-call | tf_op jit(solution)/shard_map/backward/pallas_call | solution.py:1146
  232.6 6.1 %emit.1 = (bf16[512,1024]{1,0:T(8,128)(2,1)}, f32[512,1024]{1,0:T(8,128)}, f32[1,1024]{1,0:T(1,128)}, f32[64,256]{1,0:T(8,128)}, f32[64,256]{1,0:T(8,128)}, /*in...) custom-call(f32[32,8448]{1,0:T(8,128)} %get-tuple-element.63.mlp_ref, ...), custom_call_target="tpu_custom_call" | custom-call | tf_op jit(solution)/shard_map/emit/pallas_call | solution.py:1255

commit v7 on v6

--- a/solution.py
+++ b/solution.py
@@ -415,12 +415,12 @@
 def layer_kernel(
     count,
     tokens_ref, cotangent_ref, length_ref, gain_one_ref, gain_two_ref, gain_out_ref, bias_ref, start_ref,
-    w_query, w_key, w_value, w_gate, w_low_in, w_low_out, w_out, w_mlp,
+    w_query_ref, w_key_ref, w_value_ref, w_gate_ref, w_low_in, w_low_out, w_out_ref, w_mlp,
     h_ref, query_ref, key_ref, value_ref, gate_ref, logits_ref, low_rank_ref, attended_ref, mixed_ref, states_ref,
     grad_zero_ref, grad_ref, output_ref, total_ref, attn_ref, gain_grad_ref,
     tokens, low, low_turned, h_two, h_two_turned, weights_zero, weights, resid, part_out, part_in,
     mlp_sum, grad_sum, inner_all, pair_all, sums_out, sums_in, memory,
-    local_sems, gather_local, swap_out, swap_in, gather_out, gather_in, pair_out, pair_in,
+    w_query, w_key, w_value, w_gate, w_out, load_sems, local_sems, gather_local, swap_out, swap_in, gather_out, gather_in, pair_out, pair_in,
 ):
     step = pl.program_id(0)
     at = Place()
@@ -467,7 +467,16 @@
             pltpu.make_async_copy(cotangent_ref, low.at[own_rows(0, own)], local_sems.at[1]),
             pltpu.make_async_copy(tokens_ref, tokens.at[own_rows(0, own)], local_sems.at[0]),
         ]
-        for copy in here:
+        loads = [
+            pltpu.make_async_copy(source, target, load_sems.at[i])
+            for i, (source, target) in enumerate(
+                (
+                    (w_query_ref, w_query), (w_key_ref, w_key), (w_value_ref, w_value), (w_gate_ref, w_gate),
+                    (w_out_ref, w_out),
+                )
+            )
+        ]
+        for copy in here + loads:
             copy.start()
         at.meet()
         put(tokens_ref, tokens.at[own_rows(0, own)], 0)
@@ -481,6 +490,8 @@
         for i in range(own_tiles):
             low[own_rows(i), :] = (low[own_rows(i), :].astype(F32) * row_mask(i)).astype(BF16)
         put(low.at[own_rows(0, own)], low.at[own_rows(0, own)], 1)
+        for copy in loads:
+            copy.wait()
         wait(tokens.at[other_rows(0, own)], 0)
 
     def gather_at(inside, among):
@@ -596,7 +607,7 @@
                 @pl.when(i < own_tiles)
                 def _():
                     there = pl.ds(pl.multiple_of(i * ROWS, ROWS), ROWS)
-                    for k, source in enumerate((mlp_sum, grad_sum)):
+                    for k, source in ((1, grad_sum), (0, mlp_sum)):
                         sums_out[k, there, :] = source[rows, :].astype(BF16)
                         put(sums_out.at[k, there], sums_in.at[k, there], 6 + 2 * i + k)
 
@@ -652,13 +663,10 @@
             sent(h_two.at[pl.ds(0, ROWS)], pair_out.at[4 + i], pair_in.at[4 + i], at.sibling)
         for i in range(own_tiles):
             rows = pl.ds(i * ROWS, ROWS)
-            for k in range(2):
-                wait(sums_in.at[k, rows], 6 + 2 * i + k)
+            wait(sums_in.at[1, rows], 7 + 2 * i)
             full = resid[rows, :]
             scale = lax.rsqrt(jnp.mean(full * full, axis=1, keepdims=True) + EPSILON)
             normal = full * scale
-            mlp_out = mlp_sum[own_rows(i), :] + sums_in[0, rows, :].astype(F32)
-            output_ref[rows, :] = (row_mask(i) * (full + mlp_out)).astype(BF16)
             grad = grad_sum[own_rows(i), :] + sums_in[1, rows, :].astype(F32)
             total = low[own_rows(i), :].astype(F32) + norm_backward(grad, gain_two_ref[...], normal, scale)
             total_ref[rows, :] = total
@@ -666,6 +674,11 @@
             h_two[own_rows(i), :] = total.astype(BF16)
             put(h_two.at[own_rows(i)], h_two.at[own_rows(i)], 10 + i)
             pltpu.make_async_copy(h_two.at[own_rows(i)], attn_ref.at[own_rows(i)], local_sems.at[i]).start()
+        for i in range(own_tiles):
+            rows = pl.ds(i * ROWS, ROWS)
+            wait(sums_in.at[0, rows], 6 + 2 * i)
+            mlp_out = mlp_sum[own_rows(i), :] + sums_in[0, rows, :].astype(F32)
+            output_ref[rows, :] = (row_mask(i) * (resid[rows, :] + mlp_out)).astype(BF16)
         weight_rows(weights_zero, grad_zero_ref)
         gather.finish()
         for i in range(own_tiles):
@@ -715,9 +728,8 @@
         grid=(steps,),
         in_specs=[
             ANY, ANY, pl.BlockSpec(memory_space=pltpu.SMEM), whole((1, width)), whole((1, width)), whole((1, VALUE_HEAD)),
-            whole((1, keys)), whole(start.shape), whole(w_query.shape), whole(w_key.shape), whole(w_value.shape),
-            whole(w_gate.shape), whole(w_low_in.shape), whole(w_low_out.shape), whole(w_out.shape),
-            ANY,
+            whole((1, keys)), whole(start.shape), ANY, ANY, ANY, ANY, whole(w_low_in.shape), whole(w_low_out.shape),
+            ANY, ANY,
         ],
         out_specs=[rows_spec(columns) for columns, _ in row_shapes]
         + [
@@ -756,6 +768,8 @@
             pltpu.VMEM((2, own, width), BF16),
             pltpu.VMEM((2, own, width), BF16),
             pltpu.VMEM((heads, KEY_HEAD, VALUE_HEAD), F32),
+            *[pltpu.VMEM(w.shape, w.dtype) for w in (w_query, w_key, w_value, w_gate, w_out)],
+            pltpu.SemaphoreType.DMA((5,)),
             pltpu.SemaphoreType.DMA((tiles,)),
             pltpu.SemaphoreType.DMA((count,)),
             pltpu.SemaphoreType.DMA((count,)),
@@ -852,14 +866,14 @@
 def backward_kernel(
     half, mlp_chunks, attn_chunks,
     zero_ref, groups_ref, attn_ref, h_ref, query_ref, key_ref, value_ref, gate_ref, logits_ref, low_rank_ref,
-    attended_ref, mixed_ref, states_ref, w_query, w_key, w_value, w_gate, w_low_in, w_low_out, w_out,
-    tokens_ref, total_ref, gain_one_ref, gain_out_ref, gain_two_grad_ref,
+    attended_ref, mixed_ref, states_ref, w_query_ref, w_key_ref, w_value_ref, w_gate_ref, w_low_in, w_low_out,
+    w_out_ref, tokens_any, total_any, gain_one_ref, gain_out_ref, gain_two_grad_ref,
     mlp_out, attn_out, small_out, tokens_out,
     mlp, attn, mlp_via_x, mlp_via_y, mlp_from_x, mlp_from_y, mlp_from_z,
     attn_via_x, attn_via_y, attn_from_x, attn_from_y, attn_from_z, summed, swapped,
     small_own, small_in, small_z, h_turned, attn_turned, right, mixed_all, h_grad, h_grad_out, h_grad_in,
     memory_grad, gain_out_sum, low_in_sum, low_out_sum, bias_sum,
-    load_sems, mlp_sems_out, mlp_sems_in, attn_sems_out, attn_sems_in, pair_out, pair_in, small_sems_out, small_sems_in,
+    w_query, w_key, w_value, w_gate, w_out, tokens_ref, total_ref, weight_sems, load_sems, mlp_sems_out, mlp_sems_in, attn_sems_out, attn_sems_in, pair_out, pair_in, small_sems_out, small_sems_in,
 ):
     step = pl.program_id(0)
     at = Place()
@@ -966,10 +980,22 @@
     def own_rows(i):
         return pl.ds(pl.multiple_of(i * ROWS, ROWS), ROWS)
 
+    held = [
+        pltpu.make_async_copy(source, target, weight_sems.at[i])
+        for i, (source, target) in enumerate(
+            (
+                (w_out_ref, w_out), (w_query_ref, w_query), (w_key_ref, w_key), (w_value_ref, w_value),
+                (w_gate_ref, w_gate), (tokens_any, tokens_ref), (total_any, total_ref),
+            )
+        )
+    ]
+
     @pl.when(step == 0)
     def _():
         for chunk in loads:
             load(chunk).start()
+        for copy in held:
+            copy.start()
         memory_grad[...] = jnp.zeros_like(memory_grad)
         gain_out_sum[...] = jnp.zeros_like(gain_out_sum)
         low_in_sum[...] = jnp.zeros_like(low_in_sum)
@@ -982,6 +1008,11 @@
         @pl.when(step == where)
         def _():
             ticks_at(where, 0)
+
+    @pl.when(step == 0)
+    def _():
+        for copy in held[:5]:
+            copy.wait()
 
     @pl.when(step < tiles)
     def _():
@@ -1039,6 +1070,8 @@
 
     @pl.when(step == tiles)
     def _():
+        for copy in held[5:]:
+            copy.wait()
         gain_one = jnp.zeros((1, width), F32)
         for i in range(own_tiles):
             here = own_rows(i)
@@ -1153,7 +1186,7 @@
                 (ROWS // BLOCK, heads, KEY_HEAD, VALUE_HEAD), lambda i: (jnp.maximum(tiles - 1 - i, 0), 0, 0, 0)
             )
         ]
-        + [whole(a.shape) for a in constant],
+        + [whole(a.shape) if i in (4, 5) or i > 8 else ANY for i, a in enumerate(constant)],
         out_specs=[vmem, vmem, vmem, vmem],
         out_shape=[
             jax.ShapeDtypeStruct((rows // 2, 2 * mlp_width), F32),
@@ -1182,6 +1215,8 @@
             pltpu.VMEM((rank, width), F32),
             pltpu.VMEM((rank, keys), F32),
             pltpu.VMEM((1, keys), F32),
+            *[pltpu.VMEM(a.shape, a.dtype) for a in (w_query, w_key, w_value, w_gate, w_out, tokens, total)],
+            pltpu.SemaphoreType.DMA((7,)),
             pltpu.SemaphoreType.DMA((mlp_count,)),
             pltpu.SemaphoreType.DMA((mlp_count, 7)),
             pltpu.SemaphoreType.DMA((mlp_count, 7)),
@@ -1204,14 +1239,20 @@
     output_out, tokens_out, gain_one_out, query_out, key_out, value_out, gate_out, low_in_out, low_out_out, bias_out,
     gain_out_out, out_out, gain_two_out, mlp_out, tokens, output, mlp, attn, load_sems, sems,
 ):
-    staged = [(attn_ref, attn), (mlp_ref, mlp), (output_ref, output), (tokens_ref, tokens)]
+    staged = [(attn_ref, attn)]
+    moves = []
+    for i, target in enumerate((query_out, key_out, value_out, gate_out, out_out)):
+        moves.append((attn.at[:, edges[i] : edges[i + 1]], target))
+    for source, stage, target in (
+        (tokens_ref, tokens, tokens_out), (mlp_ref, mlp, mlp_out), (output_ref, output, output_out)
+    ):
+        size = source.shape[0] // 2
+        for rows in (pl.ds(0, size), pl.ds(size, size)):
+            staged.append((source.at[rows], stage.at[rows]))
+            moves.append((stage.at[rows], target.at[rows]))
     loads = [pltpu.make_async_copy(source, target, load_sems.at[i]) for i, (source, target) in enumerate(staged)]
     for load in loads:
         load.start()
-    moves = []
-    for i, target in enumerate((query_out, key_out, value_out, gate_out, out_out)):
-        moves.append((attn.at[:, edges[i] : edges[i + 1]], target))
-    moves += [(mlp, mlp_out), (output, output_out), (tokens, tokens_out)]
     copies = [pltpu.make_async_copy(source, target, sems.at[i]) for i, (source, target) in enumerate(moves)]
     for i, load in enumerate(loads):
         load.wait()
@@ -1262,8 +1303,8 @@
             pltpu.VMEM(output.shape, BF16),
             pltpu.VMEM(mlp.shape, F32),
             pltpu.VMEM(attn.shape, F32),
-            pltpu.SemaphoreType.DMA((4,)),
-            pltpu.SemaphoreType.DMA((8,)),
+            pltpu.SemaphoreType.DMA((7,)),
+            pltpu.SemaphoreType.DMA((11,)),
         ],
         compiler_params=pltpu.CompilerParams(vmem_limit_bytes=60 << 20),
         name="emit",

time: 239 us -> 237 us (level)
  no operation moved by 1% of the time
where the time goes in v7:
time: 237 us
  Pallas kernels  235 us (99%)
    pallas_call x1, Pallas kernels, backward(): pl.pallas_call(functools.partial(backward_kernel, mlp_width // 3, mlp_chu...  124 us
    pallas_call x1, Pallas kernels, layer(): pl.pallas_call(functools.partial(layer_kernel, count), grid=(steps,), in_...  106 us
    pallas_call x1, Pallas kernels, emit(): pl.pallas_call(functools.partial(emit_kernel, mlp.shape[1] // 6, edges),...  5.52 us

profile of v7, /device:TPU:0, one launch (start us, length us, event | category | flops | bytes accessed | tf_op | source)
XLA Modules:
  0.0 236.7 jit_solution(11378925248215628896)
XLA Ops:
  1.3 105.7 %layer.1 = (bf16[1024,1024]{1,0:T(8,128)(2,1)}, bf16[1024,256]{1,0:T(8,128)(2,1)}, bf16[1024,256]{1,0:T(8,128)(2,1)}, bf16[1024,512]{1,0:T(8,128)(2,1)}, f32[102...) custom-call(bf16[512,1024]{1,0:T(8,128)(2,1)} %bitcast.16, ...), custom_call_target="tpu_custom_call" | custom-call | tf_op jit(solution)/shard_map/layer/pallas_call | solution.py:726
  107.0 124.0 %backward.1 = (f32[32,8448]{1,0:T(8,128)}, f32[64,2048]{1,0:T(8,128)}, f32[240,128]{1,0:T(8,128)}, f32[512,1024]{1,0:T(8,128)}) custom-call(bf16[4,4,64,384]{3,2,1,0:T(8,128)(2,1)} %get-tuple-element.48.zero_ref, bf16[5,4,4,64,768]{4,3,2,1,0:T(8,128)(2,1)} %get-tuple-element.49.groups_ref, bf16[1024,1024]{1,0:T(8,128)(2,1)} %get-tuple-element.50.attn_ref, ...), custom_call_target="tpu_custom_call" | custom-call | tf_op jit(solution)/shard_map/backward/pallas_call | solution.py:1179
  231.0 5.5 %emit.1 = (bf16[512,1024]{1,0:T(8,128)(2,1)}, f32[512,1024]{1,0:T(8,128)}, f32[1,1024]{1,0:T(1,128)}, f32[64,256]{1,0:T(8,128)}, f32[64,256]{1,0:T(8,128)}, /*in...) custom-call(f32[32,8448]{1,0:T(8,128)} %get-tuple-element.63.mlp_ref, ...), custom_call_target="tpu_custom_call" | custom-call | tf_op jit(solution)/shard_map/emit/pallas_call | solution.py:1296

commit v8 on v7

--- a/solution.py
+++ b/solution.py
@@ -54,8 +54,8 @@
     end = total[BLOCK - 1 :, :]
     rise = jnp.exp(total - middle)
     fall = jnp.exp(middle - total)
-    early = rise * (jnp.exp(middle) * SCALE)
-    late = fall * jnp.exp(end - middle)
+    early = jnp.exp(total) * SCALE
+    late = jnp.exp(end - total)
     return rise * SCALE, fall, early, late, jnp.exp(end)
 
 

time: 237 us -> 237 us (level)
  no operation moved by 1% of the time
where the time goes in v8:
time: 237 us
  Pallas kernels  235 us (99%)
    pallas_call x1, Pallas kernels, backward(): pl.pallas_call(functools.partial(backward_kernel, mlp_width // 3, mlp_chu...  124 us
    pallas_call x1, Pallas kernels, layer(): pl.pallas_call(functools.partial(layer_kernel, count), grid=(steps,), in_...  106 us
    pallas_call x1, Pallas kernels, emit(): pl.pallas_call(functools.partial(emit_kernel, mlp.shape[1] // 6, edges),...  5.52 us

profile of v8, /device:TPU:0, one launch (start us, length us, event | category | flops | bytes accessed | tf_op | source)
XLA Modules:
  0.0 236.7 jit_solution(8297464338244461513)
XLA Ops:
  1.3 105.7 %layer.1 = (bf16[1024,1024]{1,0:T(8,128)(2,1)}, bf16[1024,256]{1,0:T(8,128)(2,1)}, bf16[1024,256]{1,0:T(8,128)(2,1)}, bf16[1024,512]{1,0:T(8,128)(2,1)}, f32[102...) custom-call(bf16[512,1024]{1,0:T(8,128)(2,1)} %bitcast.16, ...), custom_call_target="tpu_custom_call" | custom-call | tf_op jit(solution)/shard_map/layer/pallas_call | solution.py:726
  107.0 124.0 %backward.1 = (f32[32,8448]{1,0:T(8,128)}, f32[64,2048]{1,0:T(8,128)}, f32[240,128]{1,0:T(8,128)}, f32[512,1024]{1,0:T(8,128)}) custom-call(bf16[4,4,64,384]{3,2,1,0:T(8,128)(2,1)} %get-tuple-element.48.zero_ref, bf16[5,4,4,64,768]{4,3,2,1,0:T(8,128)(2,1)} %get-tuple-element.49.groups_ref, bf16[1024,1024]{1,0:T(8,128)(2,1)} %get-tuple-element.50.attn_ref, ...), custom_call_target="tpu_custom_call" | custom-call | tf_op jit(solution)/shard_map/backward/pallas_call | solution.py:1179
  231.0 5.5 %emit.1 = (bf16[512,1024]{1,0:T(8,128)(2,1)}, f32[512,1024]{1,0:T(8,128)}, f32[1,1024]{1,0:T(1,128)}, f32[64,256]{1,0:T(8,128)}, f32[64,256]{1,0:T(8,128)}, /*in...) custom-call(f32[32,8448]{1,0:T(8,128)} %get-tuple-element.63.mlp_ref, ...), custom_call_target="tpu_custom_call" | custom-call | tf_op jit(solution)/shard_map/emit/pallas_call | solution.py:1296
